TPU v7x, 32 devices: a whole 2x2x4 slice. The times are simulated.
32 devices in a mesh: rows: 8 (over y, x, core), cols: 4 (over z).
Axes of the slice: x: 2, y: 2, z: 4, core: 2. Of those that a mesh axis runs over, the one named last changes fastest.
Arguments:
- irradiance_layers: bfloat16 [2, 2048, 16384], P(None, ('rows', 'cols')), may hold values from 0 to 2
- initial_heat_anomaly: float32 [2, 2048, 16384], P(None, 'rows', 'cols'), may hold values from -12 to 12
- drift_rate_eastward: float32 [2, 2048, 16384], P(None, 'rows', 'cols'), may hold values from 0.35 to 0.45
- drift_rate_northward: float32 [2, 2048, 16384], P(None, 'rows', 'cols'), may hold values from 0.33 to 0.4
- extinction_factor: float32 [2, 2048, 16384], P(None, 'rows', 'cols'), may hold values from 0.1 to 1
- windward_polarity_eastward: int32 [2, 2048], P(None, 'rows'), may hold values from 0 to 1
- windward_polarity_northward: int32 [2, 16384], P(None, 'cols'), may hold values from 0 to 1
Outputs:
- phase_slabs: float32 [2, 2048, 16384], P(None, ('rows', 'cols'))
- temperature_end: float32 [2, 2048, 16384], P(None, 'rows', 'cols')
Inputs may be any that keep to these rules, and one draw needn't show every extreme that they name: `windward_polarity_eastward`: 1 means wind plus slew toward increasing x. `windward_polarity_northward`: 1 means wind plus slew toward increasing y.
All inputs are finite; a program needn't handle non-finite values.
Results may differ from a plain program's by a relative error of at most 0.0003.
Values may be sent and summed in bfloat16 or wider, within the bound.
No kernel may reach another device: no remote copies, remote signals or barrier semaphores. Data moves between devices by JAX's collectives and lax.ppermute only.
A program may use at most 192 MiB of HBM per device.

v0:
```python
import jax
import jax.numpy as jnp
from jax import lax
from jax.sharding import PartitionSpec as P

SUBSTEPS = 4


DIFFUSION = 0.03
HEAT_RATE = 0.25


def extended(block, sides, width):
    for axis, dim in sides:
        count = lax.axis_size(axis)
        forward = [(i, i + 1) for i in range(count - 1)]
        backward = [(target, source) for source, target in forward]
        low = lax.ppermute(
            lax.slice_in_dim(block, block.shape[dim] - width, None, axis=dim), axis, forward
        )
        high = lax.ppermute(lax.slice_in_dim(block, 0, width, axis=dim), axis, backward)
        block = jnp.concatenate([low, block, high], axis=dim)
    return block


def advance(padded, wind_x, wind_y, heating):
    middle = padded[1:-1, 1:-1]
    west_cell = padded[1:-1, :-2]
    east_cell = padded[1:-1, 2:]
    south_cell = padded[:-2, 1:-1]
    north_cell = padded[2:, 1:-1]
    upwind_x = jnp.where(wind_x > 0, west_cell, east_cell)
    upwind_y = jnp.where(wind_y > 0, south_cell, north_cell)
    neighbours = west_cell + east_cell + south_cell + north_cell - 4.0 * middle
    return (
        middle
        - jnp.abs(wind_x) * (middle - upwind_x)
        - jnp.abs(wind_y) * (middle - upwind_y)
        + DIFFUSION * neighbours
        + heating
    )


def body(
    irradiance_layers,
    initial_heat_anomaly,
    drift_rate_eastward,
    drift_rate_northward,
    extinction_factor,
    windward_polarity_eastward,
    windward_polarity_northward,
):
    optical_layers = initial_heat_anomaly.shape[0]
    arrived = lax.all_to_all(irradiance_layers, "cols", split_axis=2, concat_axis=1, tiled=True)
    phases = []
    finals = []
    for optical_layer in range(optical_layers):
        light_tile = arrived[optical_layer]
        wind_x = jnp.where(
            windward_polarity_eastward[optical_layer][:, None] == 1,
            drift_rate_eastward[optical_layer],
            -drift_rate_eastward[optical_layer],
        )
        wind_y = jnp.where(
            windward_polarity_northward[optical_layer][None, :] == 1,
            drift_rate_northward[optical_layer],
            -drift_rate_northward[optical_layer],
        )
        heating = HEAT_RATE * extinction_factor[optical_layer] * light_tile.astype(jnp.float32)
        heat_transport_advance = initial_heat_anomaly[optical_layer]
        phase_sum = jnp.zeros_like(heat_transport_advance)
        for section_index in range(SUBSTEPS):
            padded = extended(heat_transport_advance, (("rows", 0), ("cols", 1)), 1)
            heat_transport_advance = advance(padded, wind_x, wind_y, heating)
            phase_sum = phase_sum + heat_transport_advance / SUBSTEPS
        phases.append(phase_sum)
        finals.append(heat_transport_advance)
    phase_slabs = lax.all_to_all(jnp.stack(phases), "cols", split_axis=1, concat_axis=2, tiled=True)
    return (phase_slabs, jnp.stack(finals))


def solution(mesh):
    return jax.shard_map(
        body,
        mesh=mesh,
        in_specs=(
            P(None, ("rows", "cols"), None),
            P(None, "rows", "cols"),
            P(None, "rows", "cols"),
            P(None, "rows", "cols"),
            P(None, "rows", "cols"),
            P(None, "rows"),
            P(None, "cols"),
        ),
        out_specs=(P(None, ("rows", "cols"), None), P(None, "rows", "cols")),
        check_vma=False,
    )
```

profile of v0, /device:TPU:3, one launch (start us, length us, event | category | flops | bytes accessed | tf_op | source)
XLA Modules:
  0.0 627.9 jit_solution(5142534280835631980)
XLA Ops:
  0.6 17.8 %copy.19 = bf16[2,64,16384]{1,0,2:T(2,128)(2,1)} copy(bf16[2,64,16384]{2,1,0:T(8,128)(2,1)} %param.7) | data formatting | bytes 8388608 | tf_op args[0]
  18.4 9.6 %reshape.44 = bf16[4,2,262144]{2,1,0:T(2,128)(2,1)} reshape(bf16[16384,2,64]{2,1,0:T(2,128)(2,1)} %bitcast.140) | data formatting | bytes 8388608
  28.0 5.0 all-to-all-start
  34.1 3.7 collective-permute-start
  37.8 1.9 collective-permute-start.1
  39.7 4.5 collective-permute-start.16
  44.3 1.9 collective-permute-start.17
  46.3 4.0 slice_bitcast_fusion.1
  50.5 3.7 collective-permute-start.2
  55.7 4.0 collective-permute-start.18
  61.0 64.7 %all-to-all-done = bf16[4,2,262144]{2,1,0:T(2,128)(2,1)} async-done(((bf16[4,2,262144]{2,1,0:T(2,128)(2,1)}), bf16[4,2,262144]{2,1,0:T(2,128)(2,1)}, u32[]{:S(2)}, u32[]{:S(2)}) %all-to-all-start) | async-done | bytes 4194336 | tf_op jit(solution)/shard_map/all_to_all | solution.py:54
  125.6 9.3 %reshape.45 = bf16[16384,2,64]{2,1,0:T(2,128)(2,1)} reshape(bf16[4,2,262144]{2,1,0:T(2,128)(2,1)} %all-to-all-done) | data formatting | bytes 8388608
  134.9 18.6 %copy.21 = bf16[2,64,4,4096]{3,1,2,0:T(8,128)(2,1)} copy(bf16[2,64,4,4096]{1,0,3,2:T(2,128)(2,1)} %bitcast.139) | data formatting | bytes 8388608 | tf_op jit(solution)/shard_map/all_to_all | solution.py:54
  153.5 4.2 fusion.15
  158.4 20.0 %add_add_fusion.7 = (f32[256,4096]{1,0:T(8,128)S(1)}, pred[256,4096]{1,0:T(8,128)(4,1)}, pred[256,4096]{1,0:T(8,128)(4,1)}) fusion(f32[256,4096]{1,0:T(8,128)} %copy-done.8, f32[1,4096]{1,0:T(1,128)S(1)} %collective-permute-done, f32[1,4096]{1,0:T(1,128)S(1)} %collective-permute-done.1, f32[258,1]{1,0:T(8,128)} %copy-done.12, f32[258,1]{1,0:T(8,128)} %copy-done.13, ...), kind=kLoop, calls=%fused_computation.82 | loop fusion | flops 36700160 | bytes 25205008 | tf_op jit(solution)/shard_map/add | solution.py:36
  178.5 5.6 collective-permute-start.4
  184.1 1.9 collective-permute-start.5
  186.2 19.6 %add_add_fusion.3 = (f32[256,4096]{1,0:T(8,128)S(1)}, pred[256,4096]{1,0:T(8,128)(4,1)}, pred[256,4096]{1,0:T(8,128)(4,1)}) fusion(f32[256,4096]{1,0:T(8,128)} %copy-done.7, f32[1,4096]{1,0:T(1,128)S(1)} %collective-permute-done.16, f32[1,4096]{1,0:T(1,128)S(1)} %collective-permute-done.17, f32[258,1]{1,0:T(8,128)S(1)} %collective-permute-done.18, ...), kind=kLoop, calls=%fused_computation.76 | loop fusion | flops 36700160 | bytes 25205008 | tf_op jit(solution)/shard_map/add | solution.py:36
  205.8 4.5 collective-permute-start.20
  210.3 1.9 collective-permute-start.21
  216.4 3.2 collective-permute-start.22
  222.2 12.6 %add_add_fusion.6 = f32[256,4096]{1,0:T(8,128)} fusion(f32[256,4096]{1,0:T(8,128)S(1)} %get-tuple-element.8, pred[256,4096]{1,0:T(8,128)(4,1)} %get-tuple-element.10, f32[1,4096]{1,0:T(1,128)S(1)} %collective-permute-done.4, f32[1,4096]{1,0:T(1,128)S(1)} %collective-permute-done.5, pred[256,4096]{1,0:T(8,128)(4,1)} %get-tuple-element.9, ...), kind=kLoop, calls=%fused_computation.81 | loop fusion | flops 34603008 | bytes 25205008 | tf_op jit(solution)/shard_map/add | solution.py:36
  236.5 5.1 collective-permute-start.8
  241.5 1.9 collective-permute-start.9
  243.5 18.1 %add_add_fusion.2 = f32[256,4096]{1,0:T(8,128)} fusion(f32[256,4096]{1,0:T(8,128)} %copy-done, pred[256,4096]{1,0:T(8,128)(4,1)} %get-tuple-element.15, f32[1,4096]{1,0:T(1,128)S(1)} %collective-permute-done.20, f32[1,4096]{1,0:T(1,128)} %copy-done.22, pred[256,4096]{1,0:T(8,128)(4,1)} %get-tuple-element.14, f32[258,1]{1,0:T(8,128)S(1)} %collective-permute-done.22, ...), kind=kLoop, calls=%fused_computation.75 | loop fusion | flops 34603008 | bytes 25205008 | tf_op jit(solution)/shard_map/add | solution.py:36
  262.7 4.7 collective-permute-start.24
  267.4 1.9 collective-permute-start.25
  270.4 4.3 collective-permute-start.10
  276.6 4.0 collective-permute-start.26
  282.8 18.8 %add_add_fusion.5 = f32[256,4096]{1,0:T(8,128)} fusion(f32[256,4096]{1,0:T(8,128)} %add_add_fusion.6, pred[256,4096]{1,0:T(8,128)(4,1)} %get-tuple-element.10, f32[1,4096]{1,0:T(1,128)S(1)} %collective-permute-done.8, f32[1,4096]{1,0:T(1,128)S(1)} %collective-permute-done.9, pred[256,4096]{1,0:T(8,128)(4,1)} %get-tuple-element.9, f32[258,1]{1,0:T(8,128)} %copy-done.15, ...), kind=kLoop, calls=%fused_computation.80 | loop fusion | flops 34603008 | bytes 25205008 | tf_op jit(solution)/shard_map/add | solution.py:36
  303.2 5.4 collective-permute-start.12
  308.6 1.9 collective-permute-start.13
  310.5 18.1 %add_add_fusion.1 = f32[256,4096]{1,0:T(8,128)} fusion(f32[256,4096]{1,0:T(8,128)} %add_add_fusion.2, pred[256,4096]{1,0:T(8,128)(4,1)} %get-tuple-element.15, f32[1,4096]{1,0:T(1,128)S(1)} %collective-permute-done.24, f32[1,4096]{1,0:T(1,128)} %copy-done.23, pred[256,4096]{1,0:T(8,128)(4,1)} %get-tuple-element.14, f32[258,1]{1,0:T(8,128)S(1)} %collective-permute-done.26, ...), kind=kLoop, calls=%fused_computation.74 | loop fusion | flops 34603008 | bytes 25205008 | tf_op jit(solution)/shard_map/add | solution.py:36
  329.6 4.5 collective-permute-start.28
  334.2 2.3 collective-permute-start.29
  337.7 4.3 collective-permute-start.14
  343.3 1.8 pad_maximum_fusion.68
  345.1 4.8 collective-permute-start.30
  351.5 20.9 %multiply_bitcast_fusion = (f32[1,256,4096]{2,1,0:T(8,128)}, f32[256,4096]{1,0:T(8,128)}) fusion(f32[256,4096]{1,0:T(8,128)} %add_add_fusion.5, f32[256,4096]{1,0:T(8,128)S(1)} %get-tuple-element.8, f32[256,4096]{1,0:T(8,128)S(1)} %copy-done.2, bf16[1,4,64,4096]{3,2,1,0:T(8,128)(2,1)S(1)} %copy-done.6, f32[2,256,4096]{2,1,0:T(8,128)} %param.11, ...), kind=kLoop, calls=%fused_computation.78 | loop fusion | flops 38797312 | bytes 37787920 | tf_op jit(solution)/shard_map/stack | solution.py:78
  372.4 8.7 %copy.22 = f32[1,256,4096]{2,0,1:T(1,128)} copy(f32[1,256,4096]{2,1,0:T(8,128)} %get-tuple-element.6) | data formatting | bytes 8388608 | tf_op jit(solution)/shard_map/stack | solution.py:78
  381.1 19.5 %add_multiply_fusion = (f32[256,4096]{1,0:T(8,128)S(1)}, f32[256,4096]{1,0:T(8,128)}) fusion(f32[256,4096]{1,0:T(8,128)} %add_add_fusion.1, f32[256,4096]{1,0:T(8,128)S(1)} %copy-done.1, f32[256,4096]{1,0:T(8,128)} %add_add_fusion.2, bf16[1,4,64,4096]{3,2,1,0:T(8,128)(2,1)S(1)} %copy-done.4, f32[2,256,4096]{2,1,0:T(8,128)} %param.11, ...), kind=kLoop, calls=%fused_computation.72 | loop fusion | flops 38797312 | bytes 37787920 | tf_op jit(solution)/shard_map/add | solution.py:75
  400.6 4.6 stack.19
  405.3 9.2 %pad_maximum_fusion = f32[2,256,4096]{2,0,1:T(2,128)} fusion(f32[1,256,4096]{2,0,1:T(1,128)S(1)} %stack.19, f32[1,256,4096]{2,0,1:T(1,128)S(1)} %copy-done.11), kind=kLoop, calls=%fused_computation | loop fusion | flops 2097152 | bytes 16777216 | tf_op jit(solution)/shard_map/stack | solution.py:78
  414.4 6.9 %all-to-all-start.1 = ((f32[2,256,4096]{2,0,1:T(2,128)}), f32[2,256,4096]{2,0,1:T(2,128)}, u32[]{:S(2)}, u32[]{:S(2)}) async-start(f32[2,256,4096]{2,0,1:T(2,128)} %pad_maximum_fusion), calls=%async_computation.1 | async-start | bytes 16777216 | tf_op jit(solution)/shard_map/all_to_all | solution.py:78
  421.3 7.9 %pad_maximum_fusion.1 = f32[2,256,4096]{2,1,0:T(8,128)} fusion(f32[1,256,4096]{2,1,0:T(8,128)} %bitcast.143, f32[1,256,4096]{2,1,0:T(8,128)} %bitcast.142), kind=kLoop, calls=%fused_computation.1 | loop fusion | flops 2097152 | bytes 16777216 | tf_op jit(solution)/shard_map/stack | solution.py:79
  429.2 175.3 %all-to-all-done.1 = f32[2,256,4096]{2,0,1:T(2,128)} async-done(((f32[2,256,4096]{2,0,1:T(2,128)}), f32[2,256,4096]{2,0,1:T(2,128)}, u32[]{:S(2)}, u32[]{:S(2)}) %all-to-all-start.1) | async-done | bytes 8388640 | tf_op jit(solution)/shard_map/all_to_all | solution.py:78
  604.4 12.1 %copy.23 = f32[2,64,4,4096]{3,2,1,0:T(4,128)} copy(f32[2,64,4,4096]{3,0,1,2:T(2,128)} %bitcast.18) | data formatting | bytes 16777216 | tf_op jit(solution)/shard_map/all_to_all | solution.py:78
  616.6 10.9 %all_to_all.30 = f32[2,64,16384]{2,1,0:T(8,128)} reshape(f32[2,64,4,4096]{3,2,1,0:T(4,128)} %copy.23) | data formatting | bytes 16777216 | tf_op jit(solution)/shard_map/all_to_all | solution.py:78
  (128 shorter events, 26.0 us)
Async XLA Ops:
  28.0 18.2 %copy-start.24 = (s32[2,4096]{1,0:T(2,128)S(1)}, s32[2,4096]{1,0:T(2,128)}, u32[]{:S(2)}) copy-start(s32[2,4096]{1,0:T(2,128)} %param.13) | copy-start | bytes 98308
  28.0 97.7 %all-to-all-start = ((bf16[4,2,262144]{2,1,0:T(2,128)(2,1)}), bf16[4,2,262144]{2,1,0:T(2,128)(2,1)}, u32[]{:S(2)}, u32[]{:S(2)}) async-start(bf16[4,2,262144]{2,1,0:T(2,128)(2,1)} %reshape.44), calls=%async_computation | async-start | bytes 8388608 | tf_op jit(solution)/shard_map/all_to_all | solution.py:54
  34.1 16.3 %collective-permute-start = (f32[1,4096]{1,0:T(1,128)S(1)}, f32[1,4096]{1,0:T(1,128)S(1)}, u32[]{:S(2)}, u32[]{:S(2)}) collective-permute-start(f32[1,4096]{1,0:T(1,128)S(1)} %get-tuple-element.17), channel_id=1, source_target_pairs={{0,4},{4,8},{8,12},{12,16},{16,20},{20,24},{24,28},{1,5},{5,9},{9,... | collective-permute-start | bytes 49160 | tf_op jit(solution)/shard_map/ppermute | solution.py:18
  37.8 12.6 %collective-permute-start.1 = (f32[1,4096]{1,0:T(1,128)S(1)}, f32[1,4096]{1,0:T(1,128)S(1)}, u32[]{:S(2)}, u32[]{:S(2)}) collective-permute-start(f32[1,4096]{1,0:T(1,128)S(1)} %get-tuple-element.16), channel_id=1, source_target_pairs={{4,0},{8,4},{12,8},{16,12},{20,16},{24,20},{28,24},{5,1},{9,5},{13... | collective-permute-start | bytes 49160 | tf_op jit(solution)/shard_map/ppermute | solution.py:21
  39.7 15.8 %collective-permute-start.16 = (f32[1,4096]{1,0:T(1,128)S(1)}, f32[1,4096]{1,0:T(1,128)S(1)}, u32[]{:S(2)}, u32[]{:S(2)}) collective-permute-start(f32[1,4096]{1,0:T(1,128)S(1)} %get-tuple-element.19), channel_id=1, source_target_pairs={{0,4},{4,8},{8,12},{12,16},{16,20},{20,24},{24,28},{1,5},{5,9},{9,... | collective-permute-start | bytes 49160 | tf_op jit(solution)/shard_map/ppermute | solution.py:18
  44.3 11.3 %collective-permute-start.17 = (f32[1,4096]{1,0:T(1,128)S(1)}, f32[1,4096]{1,0:T(1,128)S(1)}, u32[]{:S(2)}, u32[]{:S(2)}) collective-permute-start(f32[1,4096]{1,0:T(1,128)S(1)} %get-tuple-element.18), channel_id=1, source_target_pairs={{4,0},{8,4},{12,8},{16,12},{20,16},{24,20},{28,24},{5,1},{9,5},{13... | collective-permute-start | bytes 49160 | tf_op jit(solution)/shard_map/ppermute | solution.py:21
  50.4 232.4 %copy-start.25 = (pred[256]{0:T(512)(128)(4,1)}, pred[256]{0:T(512)(128)(4,1)S(1)}, u32[]{:S(2)}) copy-start(pred[256]{0:T(512)(128)(4,1)S(1)} %get-tuple-element.4) | copy-start | bytes 772
  50.5 107.2 %collective-permute-start.2 = (f32[258,1]{1,0:T(8,128)S(1)}, f32[258,1]{1,0:T(8,128)S(1)}, u32[]{:S(2)}, u32[]{:S(2)}) collective-permute-start(f32[258,1]{1,0:T(8,128)S(1)} %get-tuple-element.29), channel_id=1, source_target_pairs={{0,1},{1,2},{2,3},{4,5},{5,6},{6,7},{8,9},{9,10},{10,11},{12,13},{... | collective-permute-start | bytes 3104 | tf_op jit(solution)/shard_map/ppermute | solution.py:18
  54.2 103.5 %collective-permute-start.3 = (f32[258,1]{1,0:T(8,128)S(1)}, f32[258,1]{1,0:T(8,128)S(1)}, u32[]{:S(2)}, u32[]{:S(2)}) collective-permute-start(f32[258,1]{1,0:T(8,128)S(1)} %get-tuple-element.28), channel_id=1, source_target_pairs={{1,0},{2,1},{3,2},{5,4},{6,5},{7,6},{9,8},{10,9},{11,10},{13,12},{... | collective-permute-start | bytes 3104 | tf_op jit(solution)/shard_map/ppermute | solution.py:21
  55.7 130.4 %collective-permute-start.18 = (f32[258,1]{1,0:T(8,128)S(1)}, f32[258,1]{1,0:T(8,128)S(1)}, u32[]{:S(2)}, u32[]{:S(2)}) collective-permute-start(f32[258,1]{1,0:T(8,128)S(1)} %get-tuple-element.37), channel_id=1, source_target_pairs={{0,1},{1,2},{2,3},{4,5},{5,6},{6,7},{8,9},{9,10},{10,11},{12,13},{... | collective-permute-start | bytes 3104 | tf_op jit(solution)/shard_map/ppermute | solution.py:18
  59.7 126.4 %collective-permute-start.19 = (f32[258,1]{1,0:T(8,128)S(1)}, f32[258,1]{1,0:T(8,128)}, u32[]{:S(2)}, u32[]{:S(2)}) collective-permute-start(f32[258,1]{1,0:T(8,128)S(1)} %get-tuple-element.36), channel_id=1, source_target_pairs={{1,0},{2,1},{3,2},{5,4},{6,5},{7,6},{9,8},{10,9},{11,10},{13,12},{... | collective-permute-start | bytes 3104 | tf_op jit(solution)/shard_map/ppermute | solution.py:21
  153.5 32.6 %slice-start = ((s8[8388608]{0:T(1024)(128)(4,1)}), s8[4194304]{0:T(1024)(128)(4,1)S(1)}, s32[]{:S(2)}) async-start(s8[8388608]{0:T(1024)(128)(4,1)} %bitcast.133), calls=%async_computation.2 | async-start | bytes 8388608
  153.5 32.6 %slice-start.2 = ((s8[8388608]{0:T(1024)(128)(4,1)}), s8[4194304]{0:T(1024)(128)(4,1)S(1)}, s32[]{:S(2)}) async-start(s8[8388608]{0:T(1024)(128)(4,1)} %bitcast.135), calls=%async_computation.4 | async-start | bytes 8388608
  153.5 32.6 %slice-start.4 = ((s8[8388608]{0:T(1024)(128)(4,1)}), s8[4194304]{0:T(1024)(128)(4,1)S(1)}, s32[]{:S(2)}) async-start(s8[8388608]{0:T(1024)(128)(4,1)} %bitcast.137), calls=%async_computation.6 | async-start | bytes 8388608
  157.7 20.8 %copy-start.5 = (bf16[1,4,64,4096]{3,2,1,0:T(8,128)(2,1)}, bf16[1,4,64,4096]{3,2,1,0:T(8,128)(2,1)S(1)}, u32[]{:S(2)}) copy-start(bf16[1,4,64,4096]{3,2,1,0:T(8,128)(2,1)S(1)} %get-tuple-element.44) | copy-start | bytes 6291460
  158.4 27.7 %slice-start.1 = ((s8[8388608]{0:T(1024)(128)(4,1)}), s8[4194304]{0:T(1024)(128)(4,1)S(1)}, s32[]{:S(2)}) async-start(s8[8388608]{0:T(1024)(128)(4,1)} %bitcast.133), calls=%async_computation.3 | async-start | bytes 8388608
  158.4 27.7 %slice-start.3 = ((s8[8388608]{0:T(1024)(128)(4,1)}), s8[4194304]{0:T(1024)(128)(4,1)S(1)}, s32[]{:S(2)}) async-start(s8[8388608]{0:T(1024)(128)(4,1)} %bitcast.135), calls=%async_computation.5 | async-start | bytes 8388608
  158.4 27.7 %slice-start.5 = ((s8[8388608]{0:T(1024)(128)(4,1)}), s8[4194304]{0:T(1024)(128)(4,1)S(1)}, s32[]{:S(2)}) async-start(s8[8388608]{0:T(1024)(128)(4,1)} %bitcast.137), calls=%async_computation.7 | async-start | bytes 8388608
  178.5 33.7 %collective-permute-start.4 = (f32[1,4096]{1,0:T(1,128)S(1)}, f32[1,4096]{1,0:T(1,128)S(1)}, u32[]{:S(2)}, u32[]{:S(2)}) collective-permute-start(f32[1,4096]{1,0:T(1,128)S(1)} %get-tuple-element.43), channel_id=1, source_target_pairs={{0,4},{4,8},{8,12},{12,16},{16,20},{20,24},{24,28},{1,5},{5,9},{9,... | collective-permute-start | bytes 49160 | tf_op jit(solution)/shard_map/ppermute | solution.py:18
  184.1 28.1 %collective-permute-start.5 = (f32[1,4096]{1,0:T(1,128)S(1)}, f32[1,4096]{1,0:T(1,128)S(1)}, u32[]{:S(2)}, u32[]{:S(2)}) collective-permute-start(f32[1,4096]{1,0:T(1,128)S(1)} %get-tuple-element.42), channel_id=1, source_target_pairs={{4,0},{8,4},{12,8},{16,12},{20,16},{24,20},{28,24},{5,1},{9,5},{13... | collective-permute-start | bytes 49160 | tf_op jit(solution)/shard_map/ppermute | solution.py:21
  205.8 9.2 %collective-permute-start.20 = (f32[1,4096]{1,0:T(1,128)S(1)}, f32[1,4096]{1,0:T(1,128)S(1)}, u32[]{:S(2)}, u32[]{:S(2)}) collective-permute-start(f32[1,4096]{1,0:T(1,128)S(1)} %get-tuple-element.51), channel_id=1, source_target_pairs={{0,4},{4,8},{8,12},{12,16},{16,20},{20,24},{24,28},{1,5},{5,9},{9,... | collective-permute-start | bytes 49160 | tf_op jit(solution)/shard_map/ppermute | solution.py:18
  210.3 6.0 collective-permute-start.21
  212.4 8.5 %collective-permute-start.6 = (f32[258,1]{1,0:T(8,128)S(1)}, f32[258,1]{1,0:T(8,128)S(1)}, u32[]{:S(2)}, u32[]{:S(2)}) collective-permute-start(f32[258,1]{1,0:T(8,128)S(1)} %get-tuple-element.27), channel_id=1, source_target_pairs={{0,1},{1,2},{2,3},{4,5},{5,6},{6,7},{8,9},{9,10},{10,11},{12,13},{... | collective-permute-start | bytes 3104 | tf_op jit(solution)/shard_map/ppermute | solution.py:18
  213.7 7.3 %collective-permute-start.7 = (f32[258,1]{1,0:T(8,128)S(1)}, f32[258,1]{1,0:T(8,128)S(1)}, u32[]{:S(2)}, u32[]{:S(2)}) collective-permute-start(f32[258,1]{1,0:T(8,128)S(1)} %get-tuple-element.26), channel_id=1, source_target_pairs={{1,0},{2,1},{3,2},{5,4},{6,5},{7,6},{9,8},{10,9},{11,10},{13,12},{... | collective-permute-start | bytes 3104 | tf_op jit(solution)/shard_map/ppermute | solution.py:21
  216.3 18.6 %copy-start.22 = (f32[1,4096]{1,0:T(1,128)}, f32[1,4096]{1,0:T(1,128)S(1)}, u32[]{:S(2)}) copy-start(f32[1,4096]{1,0:T(1,128)S(1)} %collective-permute-done.21) | copy-start | bytes 49156
  216.4 27.1 %collective-permute-start.22 = (f32[258,1]{1,0:T(8,128)S(1)}, f32[258,1]{1,0:T(8,128)S(1)}, u32[]{:S(2)}, u32[]{:S(2)}) collective-permute-start(f32[258,1]{1,0:T(8,128)S(1)} %get-tuple-element.35), channel_id=1, source_target_pairs={{0,1},{1,2},{2,3},{4,5},{5,6},{6,7},{8,9},{9,10},{10,11},{12,13},{... | collective-permute-start | bytes 3104 | tf_op jit(solution)/shard_map/ppermute | solution.py:18
  219.6 23.9 %collective-permute-start.23 = (f32[258,1]{1,0:T(8,128)S(1)}, f32[258,1]{1,0:T(8,128)}, u32[]{:S(2)}, u32[]{:S(2)}) collective-permute-start(f32[258,1]{1,0:T(8,128)S(1)} %get-tuple-element.34), channel_id=1, source_target_pairs={{1,0},{2,1},{3,2},{5,4},{6,5},{7,6},{9,8},{10,9},{11,10},{13,12},{... | collective-permute-start | bytes 3104 | tf_op jit(solution)/shard_map/ppermute | solution.py:21
  236.5 32.9 %collective-permute-start.8 = (f32[1,4096]{1,0:T(1,128)}, f32[1,4096]{1,0:T(1,128)S(1)}, u32[]{:S(2)}, u32[]{:S(2)}) collective-permute-start(f32[1,4096]{1,0:T(1,128)} %get-tuple-element.41), channel_id=1, source_target_pairs={{0,4},{4,8},{8,12},{12,16},{16,20},{20,24},{24,28},{1,5},{5,9},{9,... | collective-permute-start | bytes 49160 | tf_op jit(solution)/shard_map/ppermute | solution.py:18
  241.5 27.8 %collective-permute-start.9 = (f32[1,4096]{1,0:T(1,128)}, f32[1,4096]{1,0:T(1,128)S(1)}, u32[]{:S(2)}, u32[]{:S(2)}) collective-permute-start(f32[1,4096]{1,0:T(1,128)} %get-tuple-element.40), channel_id=1, source_target_pairs={{4,0},{8,4},{12,8},{16,12},{20,16},{24,20},{28,24},{5,1},{9,5},{13... | collective-permute-start | bytes 49160 | tf_op jit(solution)/shard_map/ppermute | solution.py:21
  262.7 13.3 %collective-permute-start.24 = (f32[1,4096]{1,0:T(1,128)S(1)}, f32[1,4096]{1,0:T(1,128)S(1)}, u32[]{:S(2)}, u32[]{:S(2)}) collective-permute-start(f32[1,4096]{1,0:T(1,128)S(1)} %get-tuple-element.49), channel_id=1, source_target_pairs={{0,4},{4,8},{8,12},{12,16},{16,20},{20,24},{24,28},{1,5},{5,9},{9,... | collective-permute-start | bytes 49160 | tf_op jit(solution)/shard_map/ppermute | solution.py:18
  267.4 8.6 %collective-permute-start.25 = (f32[1,4096]{1,0:T(1,128)S(1)}, f32[1,4096]{1,0:T(1,128)S(1)}, u32[]{:S(2)}, u32[]{:S(2)}) collective-permute-start(f32[1,4096]{1,0:T(1,128)S(1)} %get-tuple-element.48), channel_id=1, source_target_pairs={{4,0},{8,4},{12,8},{16,12},{20,16},{24,20},{28,24},{5,1},{9,5},{13... | collective-permute-start | bytes 49160 | tf_op jit(solution)/shard_map/ppermute | solution.py:21
  270.4 11.7 %collective-permute-start.10 = (f32[258,1]{1,0:T(8,128)S(1)}, f32[258,1]{1,0:T(8,128)S(1)}, u32[]{:S(2)}, u32[]{:S(2)}) collective-permute-start(f32[258,1]{1,0:T(8,128)S(1)} %get-tuple-element.25), channel_id=1, source_target_pairs={{0,1},{1,2},{2,3},{4,5},{5,6},{6,7},{8,9},{9,10},{10,11},{12,13},{... | collective-permute-start | bytes 3104 | tf_op jit(solution)/shard_map/ppermute | solution.py:18
  274.7 8.1 %collective-permute-start.11 = (f32[258,1]{1,0:T(8,128)S(1)}, f32[258,1]{1,0:T(8,128)}, u32[]{:S(2)}, u32[]{:S(2)}) collective-permute-start(f32[258,1]{1,0:T(8,128)S(1)} %get-tuple-element.24), channel_id=1, source_target_pairs={{1,0},{2,1},{3,2},{5,4},{6,5},{7,6},{9,8},{10,9},{11,10},{13,12},{... | collective-permute-start | bytes 3104 | tf_op jit(solution)/shard_map/ppermute | solution.py:21
  276.6 33.8 %collective-permute-start.26 = (f32[258,1]{1,0:T(8,128)S(1)}, f32[258,1]{1,0:T(8,128)S(1)}, u32[]{:S(2)}, u32[]{:S(2)}) collective-permute-start(f32[258,1]{1,0:T(8,128)S(1)} %get-tuple-element.33), channel_id=1, source_target_pairs={{0,1},{1,2},{2,3},{4,5},{5,6},{6,7},{8,9},{9,10},{10,11},{12,13},{... | collective-permute-start | bytes 3104 | tf_op jit(solution)/shard_map/ppermute | solution.py:18
  280.6 29.9 %collective-permute-start.27 = (f32[258,1]{1,0:T(8,128)S(1)}, f32[258,1]{1,0:T(8,128)}, u32[]{:S(2)}, u32[]{:S(2)}) collective-permute-start(f32[258,1]{1,0:T(8,128)S(1)} %get-tuple-element.32), channel_id=1, source_target_pairs={{1,0},{2,1},{3,2},{5,4},{6,5},{7,6},{9,8},{10,9},{11,10},{13,12},{... | collective-permute-start | bytes 3104 | tf_op jit(solution)/shard_map/ppermute | solution.py:21
  303.2 33.3 %collective-permute-start.12 = (f32[1,4096]{1,0:T(1,128)}, f32[1,4096]{1,0:T(1,128)S(1)}, u32[]{:S(2)}, u32[]{:S(2)}) collective-permute-start(f32[1,4096]{1,0:T(1,128)} %get-tuple-element.38), channel_id=1, source_target_pairs={{0,4},{4,8},{8,12},{12,16},{16,20},{20,24},{24,28},{1,5},{5,9},{9,... | collective-permute-start | bytes 49160 | tf_op jit(solution)/shard_map/ppermute | solution.py:18
  308.6 28.0 %collective-permute-start.13 = (f32[1,4096]{1,0:T(1,128)S(1)}, f32[1,4096]{1,0:T(1,128)S(1)}, u32[]{:S(2)}, u32[]{:S(2)}) collective-permute-start(f32[1,4096]{1,0:T(1,128)S(1)} %get-tuple-element.39), channel_id=1, source_target_pairs={{4,0},{8,4},{12,8},{16,12},{20,16},{24,20},{28,24},{5,1},{9,5},{13... | collective-permute-start | bytes 49160 | tf_op jit(solution)/shard_map/ppermute | solution.py:21
  329.6 13.7 %collective-permute-start.28 = (f32[1,4096]{1,0:T(1,128)S(1)}, f32[1,4096]{1,0:T(1,128)S(1)}, u32[]{:S(2)}, u32[]{:S(2)}) collective-permute-start(f32[1,4096]{1,0:T(1,128)S(1)} %get-tuple-element.46), channel_id=1, source_target_pairs={{0,4},{4,8},{8,12},{12,16},{16,20},{20,24},{24,28},{1,5},{5,9},{9,... | collective-permute-start | bytes 49160 | tf_op jit(solution)/shard_map/ppermute | solution.py:18
  334.1 17.3 %copy-start.2 = (f32[256,4096]{1,0:T(8,128)S(1)}, f32[256,4096]{1,0:T(8,128)}, u32[]{:S(2)}) copy-start(f32[256,4096]{1,0:T(8,128)} %add_add_fusion.6) | copy-start | bytes 12582916
  334.2 17.3 %copy-start.6 = (bf16[1,4,64,4096]{3,2,1,0:T(8,128)(2,1)S(1)}, bf16[1,4,64,4096]{3,2,1,0:T(8,128)(2,1)}, u32[]{:S(2)}) copy-start(bf16[1,4,64,4096]{3,2,1,0:T(8,128)(2,1)} %copy-done.5) | copy-start | bytes 6291460
  334.2 9.1 %collective-permute-start.29 = (f32[1,4096]{1,0:T(1,128)S(1)}, f32[1,4096]{1,0:T(1,128)S(1)}, u32[]{:S(2)}, u32[]{:S(2)}) collective-permute-start(f32[1,4096]{1,0:T(1,128)S(1)} %get-tuple-element.47), channel_id=1, source_target_pairs={{4,0},{8,4},{12,8},{16,12},{20,16},{24,20},{28,24},{5,1},{9,5},{13... | collective-permute-start | bytes 49160 | tf_op jit(solution)/shard_map/ppermute | solution.py:21
  337.7 13.7 %collective-permute-start.14 = (f32[258,1]{1,0:T(8,128)S(1)}, f32[258,1]{1,0:T(8,128)S(1)}, u32[]{:S(2)}, u32[]{:S(2)}) collective-permute-start(f32[258,1]{1,0:T(8,128)S(1)} %get-tuple-element.22), channel_id=1, source_target_pairs={{0,1},{1,2},{2,3},{4,5},{5,6},{6,7},{8,9},{9,10},{10,11},{12,13},{... | collective-permute-start | bytes 3104 | tf_op jit(solution)/shard_map/ppermute | solution.py:18
  342.0 9.4 %collective-permute-start.15 = (f32[258,1]{1,0:T(8,128)S(1)}, f32[258,1]{1,0:T(8,128)S(1)}, u32[]{:S(2)}, u32[]{:S(2)}) collective-permute-start(f32[258,1]{1,0:T(8,128)S(1)} %get-tuple-element.23), channel_id=1, source_target_pairs={{1,0},{2,1},{3,2},{5,4},{6,5},{7,6},{9,8},{10,9},{11,10},{13,12},{... | collective-permute-start | bytes 3104 | tf_op jit(solution)/shard_map/ppermute | solution.py:21
  343.3 29.1 %copy-start.17 = (f32[1,4096]{1,0:T(1,128)}, f32[1,4096]{1,0:T(1,128)S(1)}, u32[]{:S(2)}) copy-start(f32[1,4096]{1,0:T(1,128)S(1)} %collective-permute-done.28) | copy-start | bytes 49156
  343.3 29.0 %copy-start.21 = (f32[1,4096]{1,0:T(1,128)}, f32[1,4096]{1,0:T(1,128)S(1)}, u32[]{:S(2)}) copy-start(f32[1,4096]{1,0:T(1,128)S(1)} %collective-permute-done.29) | copy-start | bytes 49156
  345.1 36.0 %collective-permute-start.30 = (f32[258,1]{1,0:T(8,128)}, f32[258,1]{1,0:T(8,128)S(1)}, u32[]{:S(2)}, u32[]{:S(2)}) collective-permute-start(f32[258,1]{1,0:T(8,128)} %get-tuple-element.30), channel_id=1, source_target_pairs={{0,1},{1,2},{2,3},{4,5},{5,6},{6,7},{8,9},{9,10},{10,11},{12,13},{... | collective-permute-start | bytes 3104 | tf_op jit(solution)/shard_map/ppermute | solution.py:18
  349.9 31.2 %collective-permute-start.31 = (f32[258,1]{1,0:T(8,128)S(1)}, f32[258,1]{1,0:T(8,128)S(1)}, u32[]{:S(2)}, u32[]{:S(2)}) collective-permute-start(f32[258,1]{1,0:T(8,128)S(1)} %get-tuple-element.31), channel_id=1, source_target_pairs={{1,0},{2,1},{3,2},{5,4},{6,5},{7,6},{9,8},{10,9},{11,10},{13,12},{... | collective-permute-start | bytes 3104 | tf_op jit(solution)/shard_map/ppermute | solution.py:21
  414.4 190.0 %all-to-all-start.1 = ((f32[2,256,4096]{2,0,1:T(2,128)}), f32[2,256,4096]{2,0,1:T(2,128)}, u32[]{:S(2)}, u32[]{:S(2)}) async-start(f32[2,256,4096]{2,0,1:T(2,128)} %pad_maximum_fusion), calls=%async_computation.1 | async-start | bytes 16777216 | tf_op jit(solution)/shard_map/all_to_all | solution.py:78
  (20 other events, 140.9 us)
where the time goes:
time: 639 us; the launch traced here: 628 us
  waiting for transfers between devices  241 us (38%)
  other arithmetic  169 us (26%)
  local copies, waits for them, and re-layouts  109 us (17%)
  starting transfers between devices  106 us (17%)
    all_to_all x1, waiting for transfers between devices, body(): lax.all_to_all(jnp.stack(phases), 'cols', split_axis=1, concat_axis=2, ti...  175 us
    add x6, other arithmetic, advance(): middle - jnp.abs(wind_x) * (middle - upwind_x)  107 us
    ppermute x16, starting transfers between devices, extended(): lax.ppermute(lax.slice_in_dim(block, block.shape[dim] - width, None, axis...  67.5 us
    all_to_all x1, waiting for transfers between devices, body(): lax.all_to_all(irradiance_layers, 'cols', split_axis=2, concat_axis=1, ti...  64.7 us
    unnamed x71, local copies, waits for them, and re-layouts  39.8 us
    another operation x2, other arithmetic, body(): jnp.stack(phases)  30.1 us
    ppermute x16, starting transfers between devices, extended(): lax.ppermute(lax.slice_in_dim(block, 0, width, axis=dim), axis, backward)  26.5 us
    all_to_all x2, local copies, waits for them, and re-layouts, body(): lax.all_to_all(jnp.stack(phases), 'cols', split_axis=1, concat_axis=2, ti...  23 us
  transfers between devices with their start and end apart: 34, of which 4 were waited for; matrix products, arithmetic and copies ran while one was open for 31% of the time, Pallas kernels for 0%

commit v1 on v0

v1 whole, which is shorter than its diff:
```python
import functools

import jax
import jax.numpy as jnp
from jax import lax
from jax.experimental import pallas as pl
from jax.experimental.pallas import tpu as pltpu
from jax.sharding import PartitionSpec as P

SUBSTEPS = 4
DIFFUSION = 0.03
HEAT_RATE = 0.25
LANES = 128
HALO = 8
PITCH = 12
LEVELS = 32767.0
LIMIT = 60 * 1024 * 1024

ANY = pl.BlockSpec(memory_space=pl.ANY)
SMEM = pl.BlockSpec(memory_space=pltpu.SMEM)
VMEM = pl.BlockSpec(memory_space=pltpu.VMEM)


def cost(flops, moved):
    return pl.CostEstimate(flops=int(flops), transcendentals=0, bytes_accessed=int(moved))


def pack_light(where, irradiance, layer, parts, width):
    slabs, rows, columns = irradiance.shape
    tiles = width // LANES
    total = columns // LANES

    def kernel(where_ref, *refs):
        side = lax.broadcasted_iota(jnp.int32, (rows, LANES), 1) < LANES // 2
        for n in range(len(parts)):
            block, east, west, out = refs[n], refs[len(parts) + n], refs[2 * len(parts) + n], refs[3 * len(parts) + n]
            out[:, :width] = block[0]
            out[:, width:] = jnp.where(side, east[0].astype(jnp.float32), west[0].astype(jnp.float32)).astype(out.dtype)

    def main(k):
        return pl.BlockSpec((1, rows, width), lambda i, where_ref: (layer, 0, where_ref[0] ^ k))

    def east(k):
        return pl.BlockSpec(
            (1, rows, LANES),
            lambda i, where_ref: (layer, 0, jnp.minimum(((where_ref[0] ^ k) + 1) * tiles, total - 1)),
        )

    def west(k):
        return pl.BlockSpec(
            (1, rows, LANES), lambda i, where_ref: (layer, 0, jnp.maximum((where_ref[0] ^ k) * tiles - 1, 0))
        )

    return pl.pallas_call(
        kernel,
        out_shape=[jax.ShapeDtypeStruct((rows, width + LANES), irradiance.dtype)] * len(parts),
        grid_spec=pltpu.PrefetchScalarGridSpec(
            num_scalar_prefetch=1,
            grid=(1,),
            in_specs=[main(k) for k in parts] + [east(k) for k in parts] + [west(k) for k in parts],
            out_specs=[pl.BlockSpec((rows, width + LANES), lambda i, where_ref: (0, 0))] * len(parts),
        ),
        compiler_params=pltpu.CompilerParams(vmem_limit_bytes=LIMIT),
        cost_estimate=cost(0, 4 * len(parts) * rows * width),
    )(where, *([irradiance] * (3 * len(parts))))


def pack_rows(fields, polarity):
    layers, rows, width = fields[0].shape
    total = len(fields) * width + LANES

    def kernel(*refs):
        sources, (first, last, sem) = refs[: len(fields) + 1], refs[len(fields) + 1 :]
        copies = []
        for n, source in enumerate(sources):
            size = source.shape[2]
            for target, row in ((first, 0), (last, rows - HALO)):
                copies.append(
                    pltpu.make_async_copy(
                        source.at[:, pl.ds(row, HALO), :],
                        target.at[:, :, pl.ds(n * width, size)],
                        sem.at[len(copies)],
                    )
                )
        for copy in copies:
            copy.start()
        for copy in copies:
            copy.wait()

    edge = jax.ShapeDtypeStruct((layers, HALO, total), jnp.float32)
    return pl.pallas_call(
        kernel,
        out_shape=[edge, edge],
        in_specs=[ANY] * (len(fields) + 1),
        out_specs=[ANY, ANY],
        scratch_shapes=[pltpu.SemaphoreType.DMA((2 * len(fields) + 2,))],
        cost_estimate=cost(0, 16 * layers * HALO * total),
    )(*fields, polarity)


def pack_columns(fields, low, high, heading):
    layers, rows, width = fields[0].shape
    tiles = width // LANES
    count = len(fields)

    def kernel(*refs):
        first, last = refs[:count], refs[count : 2 * count]
        low_ref, high_ref, heading_first, heading_last, east, west = refs[2 * count :]
        lane = lax.broadcasted_iota(jnp.int32, (HALO, LANES), 1)

        def tile(n, layer, start, edge):
            if n == count:
                return (heading_first, heading_last)[edge][layer]
            column = n * width + edge * (width - LANES)
            if start is None:
                return low_ref[layer, :, column : column + LANES]
            if isinstance(start, str):
                return high_ref[layer, :, column : column + LANES]
            return (first, last)[edge][n][layer, pl.ds(start, HALO), :]

        def gather(start, row):
            for edge, out in ((1, east), (0, west)):
                packed = None
                for layer in range(layers):
                    for n in range(count + 1):
                        place = layer * (count + 1) + n
                        shift = (PITCH * place + 4 * edge) % LANES
                        moved = tile(n, layer, start, edge)
                        if shift:
                            moved = pltpu.roll(moved, shift, 1)
                        packed = moved if packed is None else jnp.where(lane >= PITCH * place, moved, packed)
                out[pl.ds(row, HALO), :] = packed

        gather(None, 0)
        gather("high", rows + HALO)

        def loop(i, carry):
            start = pl.multiple_of(i * HALO, HALO)
            gather(start, pl.multiple_of(start + HALO, HALO))
            return carry

        lax.fori_loop(0, rows // HALO, loop, 0)

    def block(column):
        return pl.BlockSpec((layers, rows, LANES), lambda i: (0, 0, column))

    def across(column):
        return pl.BlockSpec((layers, HALO, LANES), lambda i: (0, 0, column))

    whole = pl.BlockSpec(low.shape, lambda i: (0, 0, 0))
    packed = pl.BlockSpec((rows + 2 * HALO, LANES), lambda i: (0, 0))
    shape = jax.ShapeDtypeStruct((rows + 2 * HALO, LANES), jnp.float32)
    return pl.pallas_call(
        kernel,
        grid=(1,),
        out_shape=[shape, shape],
        in_specs=[block(0)] * count + [block(tiles - 1)] * count + [whole, whole, across(0), across(tiles - 1)],
        out_specs=[packed, packed],
        compiler_params=pltpu.CompilerParams(vmem_limit_bytes=LIMIT),
        cost_estimate=cost(0, 8 * count * layers * rows * LANES),
    )(*fields, *fields, low, high, heading, heading)


def edge_light(where, parts):
    rows, width = parts[0].shape
    count = len(parts)

    def kernel(where_ref, *refs):
        sources, (top, bottom, sem) = refs[:count], refs[count:]
        me = where_ref[0]
        for k, source in enumerate(sources):

            @pl.when(me == k)
            def _(source=source):
                copy = pltpu.make_async_copy(source.at[pl.ds(0, HALO), :], top, sem.at[0])
                copy.start()
                copy.wait()

            @pl.when((me ^ (count - 1)) == k)
            def _(source=source):
                copy = pltpu.make_async_copy(source.at[pl.ds(rows - HALO, HALO), :], bottom, sem.at[1])
                copy.start()
                copy.wait()

    edge = jax.ShapeDtypeStruct((HALO, width), parts[0].dtype)
    return pl.pallas_call(
        kernel,
        out_shape=[edge, edge],
        in_specs=[SMEM] + [ANY] * count,
        out_specs=[ANY, ANY],
        scratch_shapes=[pltpu.SemaphoreType.DMA((2,))],
        cost_estimate=cost(0, 8 * HALO * width),
    )(where, *parts)


def transport(where, scale, layer, fields, parts, low, high, light_low, light_high, west, east, polarity, heading, end):
    layers, rows, width = fields[0].shape
    count = len(parts)
    share = rows // count
    tiles = width // LANES
    blocks = rows // HALO + 2
    given = end is not None

    def kernel(where_ref, scale_ref, *refs):
        fields_ref, refs = refs[:4], refs[4:]
        parts_ref, refs = refs[:count], refs[count:]
        (low_ref, high_ref, light_low_ref, light_high_ref, west_ref, east_ref, polarity_ref, heading_ref), refs = (
            refs[:8],
            refs[8 + given :],
        )
        end_ref, codes_ref, refs = refs[0], refs[1 : 1 + count], refs[1 + count :]
        here, there, rate_x, rate_y, heat, phase, light, codes, row_sign, column_sign, load_sem, light_sem, store_sem = refs
        me = where_ref[0]
        lane = lax.broadcasted_iota(jnp.int32, (HALO, LANES), 1)
        leftmost, rightmost = lane == 0, lane == LANES - 1
        stores = (here, rate_x, rate_y, heat)

        def inner(n, j):
            return stores[n].at[j + 1, pl.ds(2 * HALO if n == 0 else HALO, rows), :]

        def load(n, j):
            return pltpu.make_async_copy(
                fields_ref[n].at[layer, :, pl.ds(pl.multiple_of(j * LANES, LANES), LANES)], inner(n, j), load_sem.at[n]
            )

        def start(j, carry):
            for n in range(4):
                load(n, j).start()
            return carry

        lax.fori_loop(0, tiles, start, 0)
        arrivals = [
            pltpu.make_async_copy(parts_ref[k], light.at[me ^ k], light_sem.at[k]) for k in range(count)
        ]
        for copy in arrivals:
            copy.start()

        zeros = jnp.zeros((HALO, LANES), jnp.float32)
        row_sign[:HALO] = low_ref[0, :, 4 * width :]
        row_sign[pl.ds(HALO, rows)] = polarity_ref[0]
        row_sign[rows + HALO :] = high_ref[0, :, 4 * width :]

        def clear(j, carry):
            for buffer in (here, there):
                buffer[j, :HALO] = zeros
                buffer[j, rows + 3 * HALO :] = zeros
            return carry

        lax.fori_loop(0, tiles + 2, clear, 0)
        for j in range(tiles):
            column_sign[j + 1] = heading_ref[0, :, j * LANES : (j + 1) * LANES]
            for n in range(4):
                base = HALO if n == 0 else 0
                column = n * width + j * LANES
                stores[n][j + 1, base : base + HALO] = low_ref[0, :, column : column + LANES]
                stores[n][j + 1, base + rows + HALO : base + rows + 2 * HALO] = high_ref[0, :, column : column + LANES]
        for n in range(5):
            place = PITCH * (layer * 5 + n)
            for source, j, shift in ((west_ref, 0, LANES - 4 - place), (east_ref, tiles + 1, -place % LANES)):
                for i in range(blocks if n < 4 else 1):
                    moved = source[i * HALO : (i + 1) * HALO, :]
                    if shift:
                        moved = pltpu.roll(moved, shift, 1)
                    if n == 4:
                        column_sign[j] = moved
                    else:
                        row = i * HALO + (HALO if n == 0 else 0)
                        stores[n][j, row : row + HALO] = moved
        for copy in arrivals:
            copy.wait()
        for n in range(4):
            span = stores[n].at[pl.ds(1, tiles), pl.ds(HALO, rows), :]
            pltpu.make_async_copy(span, span, load_sem.at[n]).wait()

        def warm(j, column):
            heat[j, :HALO] = HEAT_RATE * heat[j, :HALO] * light_low_ref[:, pl.ds(column, LANES)].astype(jnp.float32)
            for k in range(count):
                for row in range(0, share, 2 * HALO):
                    span = slice(HALO + k * share + row, HALO + k * share + row + 2 * HALO)
                    given_light = light[k, row : row + 2 * HALO, pl.ds(column, LANES)].astype(jnp.float32)
                    heat[j, span] = HEAT_RATE * heat[j, span] * given_light
            heat[j, rows + HALO :] = (
                HEAT_RATE * heat[j, rows + HALO :] * light_high_ref[:, pl.ds(column, LANES)].astype(jnp.float32)
            )

        def advance(source, j, i, along_y):
            row, behind, ahead = HALO * (i + 1), jnp.maximum(j - 1, 0), jnp.minimum(j + 1, tiles + 1)
            middle = source[j, row : row + HALO]
            south, north = source[j, row - 1 : row + HALO - 1], source[j, row + 1 : row + HALO + 1]
            beside_west = pltpu.roll(jnp.where(rightmost, source[behind, row : row + HALO], middle), 1, 1)
            beside_east = pltpu.roll(jnp.where(leftmost, source[ahead, row : row + HALO], middle), LANES - 1, 1)
            span = slice(HALO * i, HALO * (i + 1))
            speed_x, speed_y = rate_x[j, span], rate_y[j, span]
            upwind_x = jnp.where(row_sign[span] > 0.5, beside_west, beside_east)
            upwind_y = jnp.where(along_y, south, north)
            around = (beside_west + beside_east) + (south + north)
            keep = (1.0 - 4.0 * DIFFUSION) - (speed_x + speed_y)
            return middle, (keep * middle + speed_x * upwind_x) + (speed_y * upwind_y + DIFFUSION * around) + heat[j, span]

        def outside(buffer):
            for side, j in ((3, 0), (4, tiles + 1)):

                @pl.when(where_ref[side] == 1)
                def _(j=j):
                    for i in range(blocks):
                        buffer[j, HALO * (i + 1) : HALO * (i + 2)] = zeros

            for side, row in ((1, HALO), (2, rows + 2 * HALO)):

                @pl.when(where_ref[side] == 1)
                def _(row=row):
                    def loop(j, carry):
                        buffer[j, row : row + HALO] = zeros
                        return carry

                    lax.fori_loop(0, tiles + 2, loop, 0)

        def sweep(source, target, step):
            def tile(j, carry):
                along_y = column_sign[j] > 0.5
                for i in range(blocks):
                    middle, new = advance(source, j, i, along_y)
                    target[j, HALO * (i + 1) : HALO * (i + 2)] = new
                    if step and 0 < i < blocks - 1:
                        span = slice(HALO * (i - 1), HALO * i)
                        phase[j, span] = (middle if step == 1 else phase[j, span]) + new
                return carry

            lax.fori_loop(0, tiles + 2, tile, 0)
            outside(target)

        def heated(j, carry):
            warm(j + 1, pl.multiple_of(j * LANES, LANES))
            return carry

        warm(0, width)
        warm(tiles + 1, width)
        lax.fori_loop(0, tiles, heated, 0)
        sweep(here, there, 0)
        sweep(there, here, 1)
        sweep(here, there, 2)
        inverse = scale_ref[1]

        def store(j):
            return pltpu.make_async_copy(
                here.at[j, pl.ds(2 * HALO, rows), :],
                end_ref.at[layer, :, pl.ds(pl.multiple_of((j - 1) * LANES, LANES), LANES)],
                store_sem.at[0],
            )

        def final(j, carry):
            along_y = column_sign[j] > 0.5
            column = pl.multiple_of((j - 1) * LANES, LANES)
            for i in range(1, blocks - 1, 2):
                pair = []
                for b in (i, i + 1):
                    _, new = advance(there, j, b, along_y)
                    here[j, HALO * (b + 1) : HALO * (b + 2)] = new
                    mean = (phase[j, HALO * (b - 1) : HALO * b] + new) * (1.0 / SUBSTEPS)
                    level = jnp.sqrt(jnp.sqrt(jnp.abs(mean) * inverse)) * LEVELS
                    level = jnp.minimum(level, LEVELS) + 0.5
                    pair.append(jnp.where(mean < 0, -level, level).astype(jnp.int32))
                row = HALO * (i - 1)
                codes[row // share, row % share : row % share + 2 * HALO, pl.ds(column, LANES)] = jnp.concatenate(
                    pair, axis=0
                ).astype(jnp.int16)
            store(j).start()
            return carry

        lax.fori_loop(1, tiles + 1, final, 0)
        leaving = [
            pltpu.make_async_copy(codes.at[me ^ k], codes_ref[k], light_sem.at[k]) for k in range(count)
        ]
        for copy in leaving:
            copy.start()
        for copy in leaving:
            copy.wait()
        span = here.at[pl.ds(1, tiles), pl.ds(2 * HALO, rows), :]
        pltpu.make_async_copy(span, span, store_sem.at[0]).wait()

    total = tiles + 2
    edge = pl.BlockSpec((1,) + low.shape[1:], lambda i: (layer, 0, 0))
    operands = [where, scale, *fields, *parts, low, high, light_low, light_high, west, east, polarity, heading]
    in_specs = (
        [SMEM, SMEM]
        + [ANY] * (4 + count)
        + [edge, edge, VMEM, VMEM, VMEM, VMEM]
        + [
            pl.BlockSpec((1, rows, LANES), lambda i: (layer, 0, 0)),
            pl.BlockSpec((1, HALO, width), lambda i: (layer, 0, 0)),
        ]
    )
    if given:
        operands.append(end)
        in_specs.append(ANY)
    out = pl.pallas_call(
        kernel,
        grid=(1,),
        out_shape=[jax.ShapeDtypeStruct((layers, rows, width), jnp.float32)]
        + [jax.ShapeDtypeStruct((share, width), jnp.int16)] * count,
        in_specs=in_specs,
        out_specs=[ANY] * (1 + count),
        scratch_shapes=[
            pltpu.VMEM((total, rows + 4 * HALO, LANES), jnp.float32),
            pltpu.VMEM((total, rows + 4 * HALO, LANES), jnp.float32),
            pltpu.VMEM((total, rows + 2 * HALO, LANES), jnp.float32),
            pltpu.VMEM((total, rows + 2 * HALO, LANES), jnp.float32),
            pltpu.VMEM((total, rows + 2 * HALO, LANES), jnp.float32),
            pltpu.VMEM((total, rows, LANES), jnp.float32),
            pltpu.VMEM((count, share, width + LANES), jnp.bfloat16),
            pltpu.VMEM((count, share, width), jnp.int16),
            pltpu.VMEM((rows + 2 * HALO, LANES), jnp.float32),
            pltpu.VMEM((total, HALO, LANES), jnp.float32),
            pltpu.SemaphoreType.DMA((4,)),
            pltpu.SemaphoreType.DMA((count,)),
            pltpu.SemaphoreType.DMA((1,)),
        ],
        input_output_aliases={len(operands) - 1: 0} if given else {},
        compiler_params=pltpu.CompilerParams(vmem_limit_bytes=LIMIT),
        cost_estimate=cost(0, 120_000_000),
    )(*operands)
    return out[0], list(out[1:])


def unpack_phase(where, scale, layer, k, code, shape, slabs):
    rows, width = code.shape
    step = min(rows, 2 * HALO)
    given = slabs is not None

    def kernel(where_ref, scale_ref, code_ref, *refs):
        level = code_ref[...].astype(jnp.int32).astype(jnp.float32) * scale_ref[2]
        refs[-1][0] = (level * level) * (level * jnp.abs(level))

    operands = [where, scale, code]
    in_specs = [
        pl.BlockSpec(memory_space=pltpu.SMEM),
        pl.BlockSpec((step, width), lambda i, where_ref: (i, 0)),
    ]
    if given:
        operands.append(slabs)
        in_specs.append(ANY)
    return pl.pallas_call(
        kernel,
        out_shape=jax.ShapeDtypeStruct(shape, jnp.float32),
        grid_spec=pltpu.PrefetchScalarGridSpec(
            num_scalar_prefetch=1,
            grid=(rows // step,),
            in_specs=in_specs,
            out_specs=pl.BlockSpec((1, step, width), lambda i, where_ref: (layer, i, where_ref[0] ^ k)),
        ),
        input_output_aliases={len(operands) - 1: 0} if given else {},
        cost_estimate=cost(0, 6 * rows * width),
    )(*operands)


def body(
    irradiance_layers,
    initial_heat_anomaly,
    drift_rate_eastward,
    drift_rate_northward,
    extinction_factor,
    windward_polarity_eastward,
    windward_polarity_northward,
):
    fields = (initial_heat_anomaly, drift_rate_eastward, drift_rate_northward, extinction_factor)
    layers, rows, width = initial_heat_anomaly.shape
    count, lines = lax.axis_size("cols"), lax.axis_size("rows")
    me, line = lax.axis_index("cols"), lax.axis_index("rows")
    where = jnp.stack([me, line == 0, line == lines - 1, me == 0, me == count - 1]).astype(jnp.int32)
    order = sorted(range(1, count), key=lambda k: (k < count // 2, k))

    def trade(blocks):
        return {k: lax.ppermute(blocks[k], "cols", [(i, i ^ k) for i in range(count)]) for k in order}

    def pass_on(first, last, axis):
        size = lax.axis_size(axis)
        ahead = [(i, i + 1) for i in range(size - 1)]
        back = [(j, i) for i, j in ahead]
        return lax.ppermute(last, axis, ahead), lax.ppermute(first, axis, back)

    largest = lax.pmax(
        jnp.stack([jnp.max(jnp.abs(initial_heat_anomaly)), jnp.max(irradiance_layers).astype(jnp.float32)]),
        ("rows", "cols"),
    )
    bound = jnp.maximum(largest[0] + HEAT_RATE * SUBSTEPS * largest[1], 1e-30)
    scale = jnp.stack([bound, 1.0 / bound, jnp.sqrt(jnp.sqrt(bound)) / LEVELS])

    blocks = [None] * layers
    light = [None] * layers
    blocks[0] = dict(zip(order, pack_light(where, irradiance_layers, 0, order, width)))
    light[0] = trade(blocks[0])
    polarity = jnp.broadcast_to(
        windward_polarity_eastward.astype(jnp.float32)[:, :, None], (layers, rows, LANES)
    )
    heading = jnp.broadcast_to(
        windward_polarity_northward.astype(jnp.float32)[:, None, :], (layers, HALO, width)
    )
    first, last = pack_rows(fields, polarity)
    low, high = pass_on(first, last, "rows")
    to_east, to_west = pack_columns(fields, low, high, heading)
    west, east = pass_on(to_west, to_east, "cols")
    light[0][0] = pack_light(where, irradiance_layers, 0, [0], width)[0]
    for layer in range(1, layers):
        packed = pack_light(where, irradiance_layers, layer, order + [0], width)
        light[layer] = trade(dict(zip(order, packed)))
        light[layer][0] = packed[-1]

    end, slabs = None, None
    shape = (layers, rows // count, count * width)
    arriving = []
    for layer in range(layers):
        parts = [light[layer][k] for k in range(count)]
        top, bottom = edge_light(where, parts)
        light_low, light_high = pass_on(top, bottom, "rows")
        end, codes = transport(
            where, scale, layer, fields, parts, low, high, light_low, light_high, west, east, polarity, heading, end
        )
        received = trade(codes)
        received[0] = codes[0]
        arriving.append(received)
    for layer in range(layers):
        for k in [0] + order:
            slabs = unpack_phase(where, scale, layer, k, arriving[layer][k], shape, slabs)
    return slabs, end


def solution(mesh):
    return jax.shard_map(
        body,
        mesh=mesh,
        in_specs=(
            P(None, ("rows", "cols"), None),
            P(None, "rows", "cols"),
            P(None, "rows", "cols"),
            P(None, "rows", "cols"),
            P(None, "rows", "cols"),
            P(None, "rows"),
            P(None, "cols"),
        ),
        out_specs=(P(None, ("rows", "cols"), None), P(None, "rows", "cols")),
        check_vma=False,
    )
```

time: 639 us -> 358 us (0.56)
  the two profiles are of different devices: /device:TPU:3 before, /device:TPU:9 now
where the time goes in v1:
time: 358 us; the launch traced here: 354 us
  Pallas kernels  196 us (55%)
  blocking collectives  55.7 us (16%)
  waiting for transfers between devices  43.2 us (12%)
  starting transfers between devices  34.3 us (10%)
  other arithmetic  11.5 us (3%)
  local copies, waits for them, and re-layouts  10.5 us (3%)
    pallas_call x2, Pallas kernels, transport(): pl.pallas_call(kernel, grid=(1,), out_shape=[jax.ShapeDtypeStruct((layers...  69 us
    pallas_call x1, Pallas kernels, pack_rows(): pl.pallas_call(kernel, out_shape=[edge, edge], in_specs=[ANY] * (len(fiel...  65.2 us
    pmax x1, blocking collectives, body(): lax.pmax(jnp.stack([jnp.max(jnp.abs(initial_heat_anomaly)), jnp.max(irrad...  55.7 us
    pallas_call x8, Pallas kernels, unpack_phase(): pl.pallas_call(kernel, out_shape=jax.ShapeDtypeStruct(shape, jnp.float32)...  32.3 us
    ppermute x8, waiting for transfers between devices, pass_on(): return (lax.ppermute(last, axis, ahead), lax.ppermute(first, axis, back))  27.4 us
    ppermute x8, starting transfers between devices, pass_on(): return (lax.ppermute(last, axis, ahead), lax.ppermute(first, axis, back))  23.9 us
    ppermute x12, waiting for transfers between devices, trade(): lax.ppermute(blocks[k], 'cols', [(i, i ^ k) for i in range(count)])  15.8 us
    pallas_call x2, Pallas kernels, edge_light(): pl.pallas_call(kernel, out_shape=[edge, edge], in_specs=[SMEM] + [ANY] *...  14 us
  transfers between devices with their start and end apart: 20, of which 4 were waited for; matrix products, arithmetic and copies ran while one was open for 4% of the time, Pallas kernels for 36%

profile of v1, /device:TPU:9, one launch (start us, length us, event | category | flops | bytes accessed | tf_op | source)
XLA Modules:
  0.0 354.0 jit_solution(4652910338611520399)
XLA Ops:
  0.6 0.7 convert_element_type.4
  1.3 0.9 broadcast_in_dim.4.refs_4_.refs_14_
  2.2 65.2 %shard_map.87 = (f32[2,8,16512]{2,1,0:T(8,128)}, f32[2,8,16512]{2,1,0:T(8,128)}) custom-call(f32[2,256,4096]{2,1,0:T(8,128)} %refs_0_.13, f32[2,256,4096]{2,1,0:T(8,128)} %refs_1_.13, f32[2,256,4096]{2,1,0:T(8,128)} %refs_2_.13, f32[2,256,4096]{2,1,0:T(8,128)} %refs_3_.11, f32[2,256,128]{2,1,0:T(8,128)} %broadcast_in_dim.4.refs_4_.refs_14_), custom_call_target="tpu_custom_call" | custom-call | bytes 4227072 | tf_op jit(solution)/shard_map/pallas_call | solution.py:91
  67.4 3.7 %collective-permute-start.3 = (f32[2,8,16512]{2,1,0:T(8,128)}, f32[2,8,16512]{2,1,0:T(8,128)S(1)}, u32[]{:S(2)}, u32[]{:S(2)}) collective-permute-start(f32[2,8,16512]{2,1,0:T(8,128)} %get-tuple-element.31), channel_id=1, source_target_pairs={{0,4},{4,8},{8,12},{12,16},{16,20},{20,24},{24,28},{1,5},{5,9},{9,... | collective-permute-start | bytes 3170312 | tf_op jit(solution)/shard_map/ppermute | solution.py:479
  71.1 1.9 collective-permute-start.4
  73.6 3.3 shard_map.91
  77.0 2.3 collective-permute-start.10
  79.5 5.0 %reduce_max.19 = bf16[]{:T(256)} reduce(bf16[2,64,16384]{2,1,0:T(8,128)(2,1)} %refs_8_.3, bf16[]{:T(256)} %constant.24.clone.1), dimensions={0,1,2}, to_apply=%region_1.0 | reduce | flops 2097151 | bytes 4194308 | tf_op jit(solution)/shard_map/reduce_max | solution.py:482
  85.1 4.6 %abs_reduce_fusion = f32[]{:T(128)} fusion(f32[2,256,4096]{2,1,0:T(8,128)} %refs_0_.13), kind=kLoop, calls=%fused_computation | loop fusion | flops 4194303 | bytes 8388612 | tf_op jit(solution)/shard_map/reduce_max | solution.py:482
  89.6 0.6 pad_maximum_fusion
  90.3 55.7 %pmax.7 = f32[2]{0:T(128)S(1)} all-reduce(f32[2]{0:T(128)S(1)} %pad_maximum_fusion), channel_id=1, replica_groups=mesh['rows'=8,'cols'=4] {'rows','cols'}, use_global_device_ids=true, to_apply=%region_2.0 | all-reduce | flops 2 | bytes 16 | tf_op jit(solution)/shard_map/pmax | solution.py:481
  146.0 2.5 shard_map.90.refs_0_.refs_4_
  148.5 3.8 %shard_map.86 = (bf16[64,4224]{1,0:T(8,128)(2,1)}, bf16[64,4224]{1,0:T(8,128)(2,1)}, bf16[64,4224]{1,0:T(8,128)(2,1)}, bf16[64,4224]{1,0:T(8,128)(2,1)}) custom-call(s32[5]{0:T(128)} %stack.59.where_ref, bf16[2,64,16384]{2,1,0:T(8,128)(2,1)} %refs_8_.3, bf16[2,64,16384]{2,1,0:T(8,128)(2,1)} %refs_8_.3, bf16[2,64,16384]{2,1,0:T(8,128)(2,1)} %refs_8_.3, ...), custom_call_target="tpu_custom_call" | custom-call | bytes 4194304 | tf_op jit(solution)/shard_map/pallas_call | solution.py:54
  152.4 1.9 collective-permute-start
  154.3 0.8 copy-done.3
  155.1 7.0 %shard_map.92 = (bf16[8,4224]{1,0:T(8,128)(2,1)}, bf16[8,4224]{1,0:T(8,128)(2,1)}) custom-call(s32[5]{0:T(128)} %stack.59.where_ref, bf16[64,4224]{1,0:T(8,128)(2,1)} %shard_map.90.refs_0_.refs_4_, bf16[64,4224]{1,0:T(8,128)(2,1)} %copy-done.2, bf16[64,4224]{1,0:T(8,128)(2,1)} %copy-done.3, bf16[64,4224]{1,0:T(8,128)(2,1)} %collective-permute-done.11.refs_3_.refs_7_), custom_call_target="tpu_custom_call" | custom-call | bytes 270336 | tf_op jit(solution)/shard_map/pallas_call | solution.py:186
  162.1 5.6 %collective-permute-start.12 = (bf16[8,4224]{1,0:T(8,128)(2,1)}, bf16[8,4224]{1,0:T(8,128)(2,1)S(1)}, u32[]{:S(2)}, u32[]{:S(2)}) collective-permute-start(bf16[8,4224]{1,0:T(8,128)(2,1)} %get-tuple-element.40), channel_id=1, source_target_pairs={{0,4},{4,8},{8,12},{12,16},{16,20},{20,24},{24,28},{1,5},{5,9},{9,... | collective-permute-start | bytes 202760 | tf_op jit(solution)/shard_map/ppermute | solution.py:479
  167.6 1.9 collective-permute-start.13
  169.6 0.8 broadcast_in_dim.5.refs_10_.refs_11_.refs_15_
  171.0 6.0 %shard_map.89 = (f32[272,128]{1,0:T(8,128)}, f32[272,128]{1,0:T(8,128)}) custom-call(f32[2,256,4096]{2,1,0:T(8,128)} %refs_0_.13, f32[2,256,4096]{2,1,0:T(8,128)} %refs_1_.13, f32[2,256,4096]{2,1,0:T(8,128)} %refs_2_.13, f32[2,256,4096]{2,1,0:T(8,128)} %refs_3_.11, f32[2,256,4096]{2,1,0:T(8,128)} %refs_0_.13, f32[2,256,4096]{2,1,0:T(8,128)} %refs_1_.13, ...), custom_call_target="tpu_custom_call" | custom-call | bytes 2097152 | tf_op jit(solution)/shard_map/pallas_call | solution.py:153
  177.0 2.2 collective-permute-start.7
  179.2 3.1 collective-permute-start.8
  185.5 24.4 %collective-permute-done.8.refs_13_ = f32[272,128]{1,0:T(8,128)S(1)} collective-permute-done((f32[272,128]{1,0:T(8,128)}, f32[272,128]{1,0:T(8,128)S(1)}, u32[]{:S(2)}, u32[]{:S(2)}) %collective-permute-start.8) | collective-permute-done | bytes 139296 | tf_op jit(solution)/shard_map/ppermute | solution.py:479
  209.9 0.6 copy-done.7
  210.5 34.5 %shard_map.93 = (f32[2,256,4096]{2,1,0:T(8,128)}, s16[64,4096]{1,0:T(8,128)(2,1)}, s16[64,4096]{1,0:T(8,128)(2,1)}, s16[64,4096]{1,0:T(8,128)(2,1)}, s16[64,4096]{1,0:T(8,128)(2,1)}) custom-call(s32[5]{0:T(128)} %stack.59.where_ref, f32[3]{0:T(128)} %pad_maximum_fusion.1.scale_ref, f32[2,256,4096]{2,1,0:T(8,128)} %refs_0_.13, f32[2,256,4096]{2,1,0:T(8,128)} %refs_1_.13, ...), custom_call_target="tpu_custom_call" | custom-call | bytes 120000000 | tf_op jit(solution)/shard_map/pallas_call | solution.py:396
  245.2 0.8 copy-done.4
  246.1 7.0 %shard_map.88 = (bf16[8,4224]{1,0:T(8,128)(2,1)}, bf16[8,4224]{1,0:T(8,128)(2,1)}) custom-call(s32[5]{0:T(128)} %stack.59.where_ref, bf16[64,4224]{1,0:T(8,128)(2,1)} %get-tuple-element.27.refs_0_.refs_4_, bf16[64,4224]{1,0:T(8,128)(2,1)} %collective-permute-done.refs_1_.refs_5_, bf16[64,4224]{1,0:T(8,128)(2,1)} %copy-done.4, bf16[64,4224]{1,0:T(8,128)(2,1)} %copy-done.5), custom_call_target="tpu_custom_call" | custom-call | bytes 270336 | tf_op jit(solution)/shard_map/pallas_call | solution.py:186
  253.1 3.6 %collective-permute-start.5 = (bf16[8,4224]{1,0:T(8,128)(2,1)}, bf16[8,4224]{1,0:T(8,128)(2,1)S(1)}, u32[]{:S(2)}, u32[]{:S(2)}) collective-permute-start(bf16[8,4224]{1,0:T(8,128)(2,1)} %get-tuple-element.33), channel_id=1, source_target_pairs={{0,4},{4,8},{8,12},{12,16},{16,20},{20,24},{24,28},{1,5},{5,9},{9,... | collective-permute-start | bytes 202760 | tf_op jit(solution)/shard_map/ppermute | solution.py:479
  256.7 1.9 collective-permute-start.6
  258.7 1.4 collective-permute-start.18
  260.1 3.0 collective-permute-done.6.refs_11_
  263.8 34.5 %shard_map.94 = (f32[2,256,4096]{2,1,0:T(8,128)}, s16[64,4096]{1,0:T(8,128)(2,1)}, s16[64,4096]{1,0:T(8,128)(2,1)}, s16[64,4096]{1,0:T(8,128)(2,1)}, s16[64,4096]{1,0:T(8,128)(2,1)}) custom-call(s32[5]{0:T(128)} %stack.59.where_ref, f32[3]{0:T(128)} %pad_maximum_fusion.1.scale_ref, f32[2,256,4096]{2,1,0:T(8,128)} %refs_0_.13, ...), custom_call_target="tpu_custom_call", output_to_operand_aliasing={{0}: (18, {})} | custom-call | bytes 120000000 | tf_op jit(solution)/shard_map/pallas_call | solution.py:396
  298.7 3.2 collective-permute-start.14
  301.9 4.0 %shard_map.95.refs_0_ = f32[2,64,16384]{2,1,0:T(8,128)} custom-call(s32[5]{0:T(128)} %stack.59.where_ref, f32[3]{0:T(128)} %pad_maximum_fusion.1.scale_ref, s16[64,4096]{1,0:T(8,128)(2,1)} %get-tuple-element.50.code_ref), custom_call_target="tpu_custom_call" | custom-call | bytes 1572864 | tf_op jit(solution)/shard_map/pallas_call | solution.py:442
  305.9 4.0 %shard_map.96.refs_0_ = f32[2,64,16384]{2,1,0:T(8,128)} custom-call(s32[5]{0:T(128)} %stack.59.where_ref, f32[3]{0:T(128)} %pad_maximum_fusion.1.scale_ref, s16[64,4096]{1,0:T(8,128)(2,1)} %copy-done.8, f32[2,64,16384]{2,1,0:T(8,128)} %shard_map.95.refs_0_), custom_call_target="tpu_custom_call", output_to_operand_aliasing={{}: (3, {})} | custom-call | bytes 1572864 | tf_op jit(solution)/shard_map/pallas_call | solution.py:442
  310.0 0.8 copy-done.10
  310.8 4.0 %shard_map.97.refs_0_ = f32[2,64,16384]{2,1,0:T(8,128)} custom-call(s32[5]{0:T(128)} %stack.59.where_ref, f32[3]{0:T(128)} %pad_maximum_fusion.1.scale_ref, s16[64,4096]{1,0:T(8,128)(2,1)} %copy-done.10, f32[2,64,16384]{2,1,0:T(8,128)} %shard_map.96.refs_0_), custom_call_target="tpu_custom_call", output_to_operand_aliasing={{}: (3, {})} | custom-call | bytes 1572864 | tf_op jit(solution)/shard_map/pallas_call | solution.py:442
  314.8 0.8 copy-done.9
  315.7 4.0 %shard_map.98.refs_0_ = f32[2,64,16384]{2,1,0:T(8,128)} custom-call(s32[5]{0:T(128)} %stack.59.where_ref, f32[3]{0:T(128)} %pad_maximum_fusion.1.scale_ref, s16[64,4096]{1,0:T(8,128)(2,1)} %copy-done.9, f32[2,64,16384]{2,1,0:T(8,128)} %shard_map.97.refs_0_), custom_call_target="tpu_custom_call", output_to_operand_aliasing={{}: (3, {})} | custom-call | bytes 1572864 | tf_op jit(solution)/shard_map/pallas_call | solution.py:442
  319.7 4.0 %shard_map.99.refs_0_ = f32[2,64,16384]{2,1,0:T(8,128)} custom-call(s32[5]{0:T(128)} %stack.59.where_ref, f32[3]{0:T(128)} %pad_maximum_fusion.1.scale_ref, s16[64,4096]{1,0:T(8,128)(2,1)} %get-tuple-element.46.code_ref, f32[2,64,16384]{2,1,0:T(8,128)} %shard_map.98.refs_0_), custom_call_target="tpu_custom_call", output_to_operand_aliasing={{}: (3, {})} | custom-call | bytes 1572864 | tf_op jit(solution)/shard_map/pallas_call | solution.py:442
  323.8 8.5 %collective-permute-done.16.code_ref = s16[64,4096]{1,0:T(8,128)(2,1)S(1)} collective-permute-done((s16[64,4096]{1,0:T(8,128)(2,1)}, s16[64,4096]{1,0:T(8,128)(2,1)S(1)}, u32[]{:S(2)}, u32[]{:S(2)}) %collective-permute-start.16) | collective-permute-done | bytes 524320 | tf_op jit(solution)/shard_map/ppermute | solution.py:473
  332.2 0.8 copy-done.13
  333.0 4.0 %shard_map.100.refs_0_ = f32[2,64,16384]{2,1,0:T(8,128)} custom-call(s32[5]{0:T(128)} %stack.59.where_ref, f32[3]{0:T(128)} %pad_maximum_fusion.1.scale_ref, s16[64,4096]{1,0:T(8,128)(2,1)} %copy-done.13, f32[2,64,16384]{2,1,0:T(8,128)} %shard_map.99.refs_0_), custom_call_target="tpu_custom_call", output_to_operand_aliasing={{}: (3, {})} | custom-call | bytes 1572864 | tf_op jit(solution)/shard_map/pallas_call | solution.py:442
  337.0 7.3 %collective-permute-done.15.code_ref = s16[64,4096]{1,0:T(8,128)(2,1)S(1)} collective-permute-done((s16[64,4096]{1,0:T(8,128)(2,1)}, s16[64,4096]{1,0:T(8,128)(2,1)S(1)}, u32[]{:S(2)}, u32[]{:S(2)}) %collective-permute-start.15) | collective-permute-done | bytes 524320 | tf_op jit(solution)/shard_map/ppermute | solution.py:473
  344.4 0.8 copy-done.12
  345.2 4.0 %shard_map.101.refs_0_ = f32[2,64,16384]{2,1,0:T(8,128)} custom-call(s32[5]{0:T(128)} %stack.59.where_ref, f32[3]{0:T(128)} %pad_maximum_fusion.1.scale_ref, s16[64,4096]{1,0:T(8,128)(2,1)} %copy-done.12, f32[2,64,16384]{2,1,0:T(8,128)} %shard_map.100.refs_0_), custom_call_target="tpu_custom_call", output_to_operand_aliasing={{}: (3, {})} | custom-call | bytes 1572864 | tf_op jit(solution)/shard_map/pallas_call | solution.py:442
  349.2 0.8 copy-done.11
  350.0 4.0 %shard_map.102 = f32[2,64,16384]{2,1,0:T(8,128)} custom-call(s32[5]{0:T(128)} %stack.59.where_ref, f32[3]{0:T(128)} %pad_maximum_fusion.1.scale_ref, s16[64,4096]{1,0:T(8,128)(2,1)} %copy-done.11, f32[2,64,16384]{2,1,0:T(8,128)} %shard_map.101.refs_0_), custom_call_target="tpu_custom_call", output_to_operand_aliasing={{}: (3, {})} | custom-call | bytes 1572864 | tf_op jit(solution)/shard_map/pallas_call | solution.py:442
  (62 shorter events, 4.8 us)
Async XLA Ops:
  67.4 102.2 %collective-permute-start.3 = (f32[2,8,16512]{2,1,0:T(8,128)}, f32[2,8,16512]{2,1,0:T(8,128)S(1)}, u32[]{:S(2)}, u32[]{:S(2)}) collective-permute-start(f32[2,8,16512]{2,1,0:T(8,128)} %get-tuple-element.31), channel_id=1, source_target_pairs={{0,4},{4,8},{8,12},{12,16},{16,20},{20,24},{24,28},{1,5},{5,9},{9,... | collective-permute-start | bytes 3170312 | tf_op jit(solution)/shard_map/ppermute | solution.py:479
  71.1 98.5 %collective-permute-start.4 = (f32[2,8,16512]{2,1,0:T(8,128)}, f32[2,8,16512]{2,1,0:T(8,128)S(1)}, u32[]{:S(2)}, u32[]{:S(2)}) collective-permute-start(f32[2,8,16512]{2,1,0:T(8,128)} %get-tuple-element.32), channel_id=1, source_target_pairs={{4,0},{8,4},{12,8},{16,12},{20,16},{24,20},{28,24},{5,1},{9,5},{13... | collective-permute-start | bytes 3170312 | tf_op jit(solution)/shard_map/ppermute | solution.py:479
  76.9 75.5 %collective-permute-start.9 = (bf16[64,4224]{1,0:T(8,128)(2,1)}, bf16[64,4224]{1,0:T(8,128)(2,1)S(1)}, u32[]{:S(2)}, u32[]{:S(2)}) collective-permute-start(bf16[64,4224]{1,0:T(8,128)(2,1)} %get-tuple-element.37), channel_id=1, source_target_pairs={{0,1},{1,0},{2,3},{3,2},{4,5},{5,4},{6,7},{7,6},{8,9},{9,8},{10,11... | collective-permute-start | bytes 1622024 | tf_op jit(solution)/shard_map/ppermute | solution.py:473
  77.0 77.2 %collective-permute-start.10 = (bf16[64,4224]{1,0:T(8,128)(2,1)}, bf16[64,4224]{1,0:T(8,128)(2,1)S(1)}, u32[]{:S(2)}, u32[]{:S(2)}) collective-permute-start(bf16[64,4224]{1,0:T(8,128)(2,1)} %get-tuple-element.38), channel_id=1, source_target_pairs={{0,2},{1,3},{2,0},{3,1},{4,6},{5,7},{6,4},{7,5},{8,10},{9,11},{10,... | collective-permute-start | bytes 1622024 | tf_op jit(solution)/shard_map/ppermute | solution.py:473
  79.3 74.9 %collective-permute-start.11 = (bf16[64,4224]{1,0:T(8,128)(2,1)}, bf16[64,4224]{1,0:T(8,128)(2,1)}, u32[]{:S(2)}, u32[]{:S(2)}) collective-permute-start(bf16[64,4224]{1,0:T(8,128)(2,1)} %get-tuple-element.39), channel_id=1, source_target_pairs={{0,3},{1,2},{2,1},{3,0},{4,7},{5,6},{6,5},{7,4},{8,11},{9,10},{10,... | collective-permute-start | bytes 1622024 | tf_op jit(solution)/shard_map/ppermute | solution.py:473
  148.5 3.8 %copy-start.18 = (s32[2,4096]{1,0:T(2,128)S(1)}, s32[2,4096]{1,0:T(2,128)}, u32[]{:S(2)}) copy-start(s32[2,4096]{1,0:T(2,128)} %param.13) | copy-start | bytes 98308
  152.4 1.9 copy-start.2
  152.4 92.7 %collective-permute-start = (bf16[64,4224]{1,0:T(8,128)(2,1)}, bf16[64,4224]{1,0:T(8,128)(2,1)}, u32[]{:S(2)}, u32[]{:S(2)}) collective-permute-start(bf16[64,4224]{1,0:T(8,128)(2,1)} %get-tuple-element.28), channel_id=1, source_target_pairs={{0,1},{1,0},{2,3},{3,2},{4,5},{5,4},{6,7},{7,6},{8,9},{9,8},{10,11... | collective-permute-start | bytes 1622024 | tf_op jit(solution)/shard_map/ppermute | solution.py:473
  154.3 0.8 copy-start.3
  162.1 22.1 %collective-permute-start.12 = (bf16[8,4224]{1,0:T(8,128)(2,1)}, bf16[8,4224]{1,0:T(8,128)(2,1)S(1)}, u32[]{:S(2)}, u32[]{:S(2)}) collective-permute-start(bf16[8,4224]{1,0:T(8,128)(2,1)} %get-tuple-element.40), channel_id=1, source_target_pairs={{0,4},{4,8},{8,12},{12,16},{16,20},{20,24},{24,28},{1,5},{5,9},{9,... | collective-permute-start | bytes 202760 | tf_op jit(solution)/shard_map/ppermute | solution.py:479
  167.6 16.7 %collective-permute-start.13 = (bf16[8,4224]{1,0:T(8,128)(2,1)}, bf16[8,4224]{1,0:T(8,128)(2,1)S(1)}, u32[]{:S(2)}, u32[]{:S(2)}) collective-permute-start(bf16[8,4224]{1,0:T(8,128)(2,1)} %get-tuple-element.41), channel_id=1, source_target_pairs={{4,0},{8,4},{12,8},{16,12},{20,16},{24,20},{28,24},{5,1},{9,5},{13... | collective-permute-start | bytes 202760 | tf_op jit(solution)/shard_map/ppermute | solution.py:479
  169.6 1.1 copy-start
  169.6 1.4 copy-start.1
  171.0 13.2 %copy-start.20 = (bf16[64,4224]{1,0:T(8,128)(2,1)S(1)}, bf16[64,4224]{1,0:T(8,128)(2,1)}, u32[]{:S(2)}) copy-start(bf16[64,4224]{1,0:T(8,128)(2,1)} %get-tuple-element.29) | copy-start | bytes 1622020
  171.0 13.3 %copy-start.19 = (bf16[64,4224]{1,0:T(8,128)(2,1)S(1)}, bf16[64,4224]{1,0:T(8,128)(2,1)}, u32[]{:S(2)}) copy-start(bf16[64,4224]{1,0:T(8,128)(2,1)} %get-tuple-element.30) | copy-start | bytes 1622020
  177.0 8.5 %collective-permute-start.7 = (f32[272,128]{1,0:T(8,128)}, f32[272,128]{1,0:T(8,128)S(1)}, u32[]{:S(2)}, u32[]{:S(2)}) collective-permute-start(f32[272,128]{1,0:T(8,128)} %get-tuple-element.35), channel_id=1, source_target_pairs={{0,1},{1,2},{2,3},{4,5},{5,6},{6,7},{8,9},{9,10},{10,11},{12,13},{... | collective-permute-start | bytes 417800 | tf_op jit(solution)/shard_map/ppermute | solution.py:479
  179.2 30.7 %collective-permute-start.8 = (f32[272,128]{1,0:T(8,128)}, f32[272,128]{1,0:T(8,128)S(1)}, u32[]{:S(2)}, u32[]{:S(2)}) collective-permute-start(f32[272,128]{1,0:T(8,128)} %get-tuple-element.36), channel_id=1, source_target_pairs={{1,0},{2,1},{3,2},{5,4},{6,5},{7,6},{9,8},{10,9},{11,10},{13,12},{... | collective-permute-start | bytes 417800 | tf_op jit(solution)/shard_map/ppermute | solution.py:479
  184.2 25.7 %copy-start.14 = (bf16[8,4224]{1,0:T(8,128)(2,1)}, bf16[8,4224]{1,0:T(8,128)(2,1)S(1)}, u32[]{:S(2)}) copy-start(bf16[8,4224]{1,0:T(8,128)(2,1)S(1)} %collective-permute-done.12.refs_10_) | copy-start | bytes 202756
  184.2 60.9 %collective-permute-start.1 = (bf16[64,4224]{1,0:T(8,128)(2,1)S(1)}, bf16[64,4224]{1,0:T(8,128)(2,1)S(1)}, u32[]{:S(2)}, u32[]{:S(2)}) collective-permute-start(bf16[64,4224]{1,0:T(8,128)(2,1)S(1)} %copy-done.20), channel_id=1, source_target_pairs={{0,2},{1,3},{2,0},{3,1},{4,6},{5,7},{6,4},{7,5},{8,10},{9,11},{10,... | collective-permute-start | bytes 1622024 | tf_op jit(solution)/shard_map/ppermute | solution.py:473
  184.3 25.5 %copy-start.15 = (bf16[8,4224]{1,0:T(8,128)(2,1)}, bf16[8,4224]{1,0:T(8,128)(2,1)S(1)}, u32[]{:S(2)}) copy-start(bf16[8,4224]{1,0:T(8,128)(2,1)S(1)} %collective-permute-done.13.refs_11_) | copy-start | bytes 202756
  184.3 60.8 %collective-permute-start.2 = (bf16[64,4224]{1,0:T(8,128)(2,1)S(1)}, bf16[64,4224]{1,0:T(8,128)(2,1)S(1)}, u32[]{:S(2)}, u32[]{:S(2)}) collective-permute-start(bf16[64,4224]{1,0:T(8,128)(2,1)S(1)} %copy-done.19), channel_id=1, source_target_pairs={{0,3},{1,2},{2,1},{3,0},{4,7},{5,6},{6,5},{7,4},{8,11},{9,10},{10,... | collective-permute-start | bytes 1622024 | tf_op jit(solution)/shard_map/ppermute | solution.py:473
  185.5 24.4 %copy-start.6 = (f32[272,128]{1,0:T(8,128)}, f32[272,128]{1,0:T(8,128)S(1)}, u32[]{:S(2)}) copy-start(f32[272,128]{1,0:T(8,128)S(1)} %collective-permute-done.7.refs_12_) | copy-start | bytes 417796
  209.9 0.7 copy-start.7
  245.0 53.7 %collective-permute-start.19 = (s16[64,4096]{1,0:T(8,128)(2,1)}, s16[64,4096]{1,0:T(8,128)(2,1)S(1)}, u32[]{:S(2)}, u32[]{:S(2)}) collective-permute-start(s16[64,4096]{1,0:T(8,128)(2,1)} %get-tuple-element.49), channel_id=1, source_target_pairs={{0,2},{1,3},{2,0},{3,1},{4,6},{5,7},{6,4},{7,5},{8,10},{9,11},{10,... | collective-permute-start | bytes 1572872 | tf_op jit(solution)/shard_map/ppermute | solution.py:473
  245.1 0.8 copy-start.4
  245.1 1.0 copy-start.5
  253.1 7.0 %collective-permute-start.5 = (bf16[8,4224]{1,0:T(8,128)(2,1)}, bf16[8,4224]{1,0:T(8,128)(2,1)S(1)}, u32[]{:S(2)}, u32[]{:S(2)}) collective-permute-start(bf16[8,4224]{1,0:T(8,128)(2,1)} %get-tuple-element.33), channel_id=1, source_target_pairs={{0,4},{4,8},{8,12},{12,16},{16,20},{20,24},{24,28},{1,5},{5,9},{9,... | collective-permute-start | bytes 202760 | tf_op jit(solution)/shard_map/ppermute | solution.py:479
  256.7 6.4 %collective-permute-start.6 = (bf16[8,4224]{1,0:T(8,128)(2,1)}, bf16[8,4224]{1,0:T(8,128)(2,1)S(1)}, u32[]{:S(2)}, u32[]{:S(2)}) collective-permute-start(bf16[8,4224]{1,0:T(8,128)(2,1)} %get-tuple-element.34), channel_id=1, source_target_pairs={{4,0},{8,4},{12,8},{16,12},{20,16},{24,20},{28,24},{5,1},{9,5},{13... | collective-permute-start | bytes 202760 | tf_op jit(solution)/shard_map/ppermute | solution.py:479
  258.6 56.2 %collective-permute-start.17 = (s16[64,4096]{1,0:T(8,128)(2,1)}, s16[64,4096]{1,0:T(8,128)(2,1)S(1)}, u32[]{:S(2)}, u32[]{:S(2)}) collective-permute-start(s16[64,4096]{1,0:T(8,128)(2,1)} %get-tuple-element.47), channel_id=1, source_target_pairs={{0,1},{1,0},{2,3},{3,2},{4,5},{5,4},{6,7},{7,6},{8,9},{9,8},{10,11... | collective-permute-start | bytes 1572872 | tf_op jit(solution)/shard_map/ppermute | solution.py:473
  258.7 51.3 %collective-permute-start.18 = (s16[64,4096]{1,0:T(8,128)(2,1)}, s16[64,4096]{1,0:T(8,128)(2,1)S(1)}, u32[]{:S(2)}, u32[]{:S(2)}) collective-permute-start(s16[64,4096]{1,0:T(8,128)(2,1)} %get-tuple-element.48), channel_id=1, source_target_pairs={{0,3},{1,2},{2,1},{3,0},{4,7},{5,6},{6,5},{7,4},{8,11},{9,10},{10,... | collective-permute-start | bytes 1572872 | tf_op jit(solution)/shard_map/ppermute | solution.py:473
  260.1 3.0 copy-start.16
  263.1 0.6 copy-start.17
  298.3 34.0 %collective-permute-start.16 = (s16[64,4096]{1,0:T(8,128)(2,1)}, s16[64,4096]{1,0:T(8,128)(2,1)S(1)}, u32[]{:S(2)}, u32[]{:S(2)}) collective-permute-start(s16[64,4096]{1,0:T(8,128)(2,1)} %get-tuple-element.45), channel_id=1, source_target_pairs={{0,2},{1,3},{2,0},{3,1},{4,6},{5,7},{6,4},{7,5},{8,10},{9,11},{10,... | collective-permute-start | bytes 1572872 | tf_op jit(solution)/shard_map/ppermute | solution.py:473
  298.7 45.7 %collective-permute-start.15 = (s16[64,4096]{1,0:T(8,128)(2,1)}, s16[64,4096]{1,0:T(8,128)(2,1)S(1)}, u32[]{:S(2)}, u32[]{:S(2)}) collective-permute-start(s16[64,4096]{1,0:T(8,128)(2,1)} %get-tuple-element.44), channel_id=1, source_target_pairs={{0,3},{1,2},{2,1},{3,0},{4,7},{5,6},{6,5},{7,4},{8,11},{9,10},{10,... | collective-permute-start | bytes 1572872 | tf_op jit(solution)/shard_map/ppermute | solution.py:473
  298.7 7.2 %copy-start.8 = (s16[64,4096]{1,0:T(8,128)(2,1)}, s16[64,4096]{1,0:T(8,128)(2,1)S(1)}, u32[]{:S(2)}) copy-start(s16[64,4096]{1,0:T(8,128)(2,1)S(1)} %collective-permute-done.19.code_ref) | copy-start | bytes 1572868
  298.7 50.5 %collective-permute-start.14 = (s16[64,4096]{1,0:T(8,128)(2,1)}, s16[64,4096]{1,0:T(8,128)(2,1)S(1)}, u32[]{:S(2)}, u32[]{:S(2)}) collective-permute-start(s16[64,4096]{1,0:T(8,128)(2,1)} %get-tuple-element.43), channel_id=1, source_target_pairs={{0,1},{1,0},{2,3},{3,2},{4,5},{5,4},{6,7},{7,6},{8,9},{9,8},{10,11... | collective-permute-start | bytes 1572872 | tf_op jit(solution)/shard_map/ppermute | solution.py:473
  310.0 0.8 copy-start.10
  314.8 0.8 copy-start.9
  332.2 0.8 copy-start.13
  344.4 0.8 copy-start.12
  349.2 0.8 copy-start.11

commit v2 on v1

v2 whole, which is shorter than its diff:
```python
import functools

import jax
import jax.numpy as jnp
from jax import lax
from jax.experimental import pallas as pl
from jax.experimental.pallas import tpu as pltpu
from jax.sharding import PartitionSpec as P

SUBSTEPS = 4
DIFFUSION = 0.03
HEAT_RATE = 0.25
LANES = 128
HALO = 8
PITCH = 12
LEVELS = 32767.0
BOUND = 13.5
LIMIT = 44 * 1024 * 1024

HBM = pl.BlockSpec(memory_space=pltpu.HBM)
SMEM = pl.BlockSpec(memory_space=pltpu.SMEM)
VMEM = pl.BlockSpec(memory_space=pltpu.VMEM)


def cost(flops, moved):
    return pl.CostEstimate(flops=int(flops), transcendentals=0, bytes_accessed=int(moved))


def pack_light(where, irradiance, parts, width):
    slabs, rows, columns = irradiance.shape
    tiles = width // LANES
    total = columns // LANES

    def kernel(where_ref, *refs):
        side = lax.broadcasted_iota(jnp.int32, (rows, LANES), 1) < LANES // 2
        for n in range(len(parts)):
            block, east, west, out = refs[n], refs[len(parts) + n], refs[2 * len(parts) + n], refs[3 * len(parts) + n]
            out[:, :width] = block[0]
            out[:, width:] = jnp.where(side, east[0].astype(jnp.float32), west[0].astype(jnp.float32)).astype(out.dtype)

    def main(layer, k):
        return pl.BlockSpec((1, rows, width), lambda i, where_ref: (layer, 0, where_ref[0] ^ k))

    def east(layer, k):
        return pl.BlockSpec(
            (1, rows, LANES),
            lambda i, where_ref: (layer, 0, jnp.minimum(((where_ref[0] ^ k) + 1) * tiles, total - 1)),
        )

    def west(layer, k):
        return pl.BlockSpec(
            (1, rows, LANES), lambda i, where_ref: (layer, 0, jnp.maximum((where_ref[0] ^ k) * tiles - 1, 0))
        )

    return pl.pallas_call(
        kernel,
        name=f"pack_light_{len(parts)}",
        out_shape=[jax.ShapeDtypeStruct((rows, width + LANES), irradiance.dtype)] * len(parts),
        grid_spec=pltpu.PrefetchScalarGridSpec(
            num_scalar_prefetch=1,
            grid=(1,),
            in_specs=[main(*part) for part in parts] + [east(*part) for part in parts] + [west(*part) for part in parts],
            out_specs=[pl.BlockSpec((rows, width + LANES), lambda i, where_ref: (0, 0))] * len(parts),
        ),
        compiler_params=pltpu.CompilerParams(vmem_limit_bytes=LIMIT),
        cost_estimate=cost(0, 4 * len(parts) * rows * width),
    )(where, *([irradiance] * (3 * len(parts))))


def spans(count):
    sizes = [SUBSTEPS] + [SUBSTEPS - 1] * count
    return [(sum(sizes[:n]), size) for n, size in enumerate(sizes)]


def pack_rows(fields, polarity):
    layers, rows, width = fields[0].shape
    count = len(fields)
    places = spans(count)
    total = -(-sum(places[-1]) // HALO) * HALO

    def kernel(*refs):
        first, last = refs[-2:]
        for n, (start, size) in enumerate(places):
            below, above = refs[2 * n][...], refs[2 * n + 1][...]
            for tile in range(width // LANES):
                lanes = slice(tile * LANES, (tile + 1) * LANES)
                source = slice(0, LANES) if n == count else lanes
                first[:, start : start + size, lanes] = below[:, :size, source]
                last[:, start : start + size, lanes] = above[:, HALO - size :, source]

    def block(size, row):
        return pl.BlockSpec((layers, HALO, size), lambda i: (0, row, 0))

    edge = jax.ShapeDtypeStruct((layers, total, width), jnp.float32)
    out = pl.BlockSpec((layers, total, width), lambda i: (0, 0, 0))
    sizes = [width] * count + [LANES]
    return pl.pallas_call(
        kernel,
        name="pack_rows",
        grid=(1,),
        out_shape=[edge, edge],
        in_specs=[block(size, row) for size in sizes for row in (0, rows // HALO - 1)],
        out_specs=[out, out],
        compiler_params=pltpu.CompilerParams(vmem_limit_bytes=LIMIT),
        cost_estimate=cost(0, 16 * layers * HALO * width),
    )(*[field for field in (*fields, polarity) for _ in range(2)])


def pack_columns(fields, low, high, heading):
    layers, rows, width = fields[0].shape
    tiles = width // LANES
    count = len(fields)

    def kernel(*refs):
        first, last = refs[:count], refs[count : 2 * count]
        low_ref, high_ref, heading_first, heading_last, east, west, rim = refs[2 * count :]
        lane = lax.broadcasted_iota(jnp.int32, (HALO, LANES), 1)
        rim[...] = jnp.zeros_like(rim)
        for n, (start, size) in enumerate(spans(count)[:-1]):
            for edge, column in ((0, 0), (1, width - LANES)):
                for layer in range(layers):
                    lanes = slice(column, column + LANES)
                    rim[0, n, edge, layer, HALO - size :] = low_ref[layer, start : start + size, lanes]
                    rim[1, n, edge, layer, :size] = high_ref[layer, start : start + size, lanes]

        def tile(n, layer, start, edge):
            if n == count:
                return (heading_first, heading_last)[edge][layer]
            if isinstance(start, str):
                return rim[int(start == "high"), n, edge, layer]
            return (first, last)[edge][n][layer, pl.ds(start, HALO), :]

        def gather(start, row):
            for edge, out in ((1, east), (0, west)):
                packed = None
                for layer in range(layers):
                    for n in range(count + 1):
                        place = layer * (count + 1) + n
                        shift = (PITCH * place + 4 * edge) % LANES
                        moved = tile(n, layer, start, edge)
                        if shift:
                            moved = pltpu.roll(moved, shift, 1)
                        packed = moved if packed is None else jnp.where(lane >= PITCH * place, moved, packed)
                out[pl.ds(row, HALO), :] = packed

        gather("low", 0)
        gather("high", rows + HALO)

        def loop(i, carry):
            start = pl.multiple_of(i * HALO, HALO)
            gather(start, pl.multiple_of(start + HALO, HALO))
            return carry

        lax.fori_loop(0, rows // HALO, loop, 0)

    def block(column):
        return pl.BlockSpec((layers, rows, LANES), lambda i: (0, 0, column))

    def across(column):
        return pl.BlockSpec((layers, HALO, LANES), lambda i: (0, 0, column))

    whole = pl.BlockSpec(low.shape, lambda i: (0, 0, 0))
    packed = pl.BlockSpec((rows + 2 * HALO, LANES), lambda i: (0, 0))
    shape = jax.ShapeDtypeStruct((rows + 2 * HALO, LANES), jnp.float32)
    return pl.pallas_call(
        kernel,
        name="pack_columns",
        grid=(1,),
        out_shape=[shape, shape],
        in_specs=[block(0)] * count + [block(tiles - 1)] * count + [whole, whole, across(0), across(tiles - 1)],
        out_specs=[packed, packed],
        scratch_shapes=[pltpu.VMEM((2, count, 2, layers, HALO, LANES), jnp.float32)],
        compiler_params=pltpu.CompilerParams(vmem_limit_bytes=LIMIT),
        cost_estimate=cost(0, 8 * count * layers * rows * LANES),
    )(*fields, *fields, low, high, heading, heading)


def edge_light(where, layer, parts):
    rows, width = parts[0].shape
    count = len(parts)

    def kernel(where_ref, *refs):
        sources, (top, bottom) = refs[:count], refs[count:]
        me = where_ref[0]
        for k, source in enumerate(sources):

            @pl.when(me == k)
            def _(source=source):
                top[...] = source[:HALO, :]

            @pl.when((me ^ (count - 1)) == k)
            def _(source=source):
                bottom[...] = source[rows - HALO :, :]

    edge = jax.ShapeDtypeStruct((HALO, width), parts[0].dtype)
    return pl.pallas_call(
        kernel,
        name=f"edge_light_{layer}",
        out_shape=[edge, edge],
        in_specs=[SMEM] + [VMEM] * count,
        out_specs=[VMEM, VMEM],
        cost_estimate=cost(0, 8 * HALO * width),
    )(where, *parts)


def transport(where, layer, fields, parts, low, high, light_low, light_high, west, east, polarity, heading, end):
    layers, rows, width = fields[0].shape
    count = len(parts)
    share = rows // count
    tiles = width // LANES
    blocks = rows // HALO + 2
    places = spans(4)
    given = end is not None

    def kernel(where_ref, *refs):
        fields_ref, refs = refs[:4], refs[4:]
        parts_ref, refs = refs[:count], refs[count:]
        (low_ref, high_ref, light_low_ref, light_high_ref, west_ref, east_ref, polarity_ref, heading_ref), refs = (
            refs[:8],
            refs[8 + given :],
        )
        end_ref, codes_ref, refs = refs[0], refs[1 : 1 + count], refs[1 + count :]
        here, there, rate_x, rate_y, heat, phase, codes, row_sign, column_sign, load_sem, code_sem, store_sem = refs
        me = where_ref[0]
        lane = lax.broadcasted_iota(jnp.int32, (HALO, LANES), 1)
        leftmost, rightmost = lane == 0, lane == LANES - 1
        stores = (here, rate_x, rate_y, heat)

        def inner(n, j):
            return stores[n].at[j + 1, pl.ds(2 * HALO if n == 0 else HALO, rows), :]

        def load(j):
            for n in range(4):
                pltpu.make_async_copy(
                    fields_ref[n].at[layer, :, pl.ds(pl.multiple_of(j * LANES, LANES), LANES)], inner(n, j), load_sem.at[j]
                ).start()

        def loaded(j):
            span = rate_x.at[pl.ds(0, 4), pl.ds(HALO, rows), :]
            pltpu.make_async_copy(span, span, load_sem.at[j]).wait()

        def start(j, carry):
            load(j)
            return carry

        lax.fori_loop(0, tiles, start, 0)

        zeros = jnp.zeros((HALO, LANES), jnp.float32)
        row_sign[:HALO] = zeros
        row_sign[rows + HALO :] = zeros
        start_sign, size_sign = places[4]
        row_sign[HALO - size_sign : HALO] = low_ref[0, start_sign : start_sign + size_sign, :LANES]
        row_sign[pl.ds(HALO, rows)] = polarity_ref[0]
        row_sign[rows + HALO : rows + HALO + size_sign] = high_ref[0, start_sign : start_sign + size_sign, :LANES]

        def clear(j, carry):
            for buffer in (here, there):
                buffer[j, :HALO] = zeros
                buffer[j, HALO : 2 * HALO] = zeros
                buffer[j, rows + 2 * HALO : rows + 3 * HALO] = zeros
                buffer[j, rows + 3 * HALO :] = zeros
            for buffer in (rate_x, rate_y, heat):
                buffer[j, :HALO] = zeros
                buffer[j, rows + HALO :] = zeros
            return carry

        lax.fori_loop(0, tiles + 2, clear, 0)
        for j in range(tiles):
            column_sign[j + 1] = heading_ref[0, :, j * LANES : (j + 1) * LANES]
            for n in range(4):
                base = HALO if n == 0 else 0
                lanes = slice(j * LANES, (j + 1) * LANES)
                first, size = places[n]
                stores[n][j + 1, base + HALO - size : base + HALO] = low_ref[0, first : first + size, lanes]
                stores[n][j + 1, base + rows + HALO : base + rows + HALO + size] = high_ref[0, first : first + size, lanes]
        for n in range(5):
            place = PITCH * (layer * 5 + n)
            for source, j, shift in ((west_ref, 0, LANES - 4 - place), (east_ref, tiles + 1, -place % LANES)):
                for i in range(blocks if n < 4 else 1):
                    moved = source[i * HALO : (i + 1) * HALO, :]
                    if shift:
                        moved = pltpu.roll(moved, shift, 1)
                    if n == 4:
                        column_sign[j] = moved
                    else:
                        row = i * HALO + (HALO if n == 0 else 0)
                        stores[n][j, row : row + HALO] = moved
        def warm(j, column):
            heat[j, :HALO] = HEAT_RATE * heat[j, :HALO] * light_low_ref[:, pl.ds(column, LANES)].astype(jnp.float32)
            for k in range(count):
                base = HALO + (me ^ k) * share
                for row in range(0, share, 2 * HALO):
                    span = pl.ds(pl.multiple_of(base + row, HALO), 2 * HALO)
                    given_light = parts_ref[k][row : row + 2 * HALO, pl.ds(column, LANES)].astype(jnp.float32)
                    heat[j, span] = HEAT_RATE * heat[j, span] * given_light
            heat[j, rows + HALO :] = (
                HEAT_RATE * heat[j, rows + HALO :] * light_high_ref[:, pl.ds(column, LANES)].astype(jnp.float32)
            )

        def advance(source, j, i, along_y):
            row, behind, ahead = HALO * (i + 1), jnp.maximum(j - 1, 0), jnp.minimum(j + 1, tiles + 1)
            middle = source[j, row : row + HALO]
            south, north = source[j, row - 1 : row + HALO - 1], source[j, row + 1 : row + HALO + 1]
            beside_west = pltpu.roll(jnp.where(rightmost, source[behind, row : row + HALO], middle), 1, 1)
            beside_east = pltpu.roll(jnp.where(leftmost, source[ahead, row : row + HALO], middle), LANES - 1, 1)
            span = slice(HALO * i, HALO * (i + 1))
            speed_x, speed_y = rate_x[j, span], rate_y[j, span]
            upwind_x = jnp.where(row_sign[span] > 0.5, beside_west, beside_east)
            upwind_y = jnp.where(along_y, south, north)
            around = (beside_west + beside_east) + (south + north)
            keep = (1.0 - 4.0 * DIFFUSION) - (speed_x + speed_y)
            return middle, (keep * middle + speed_x * upwind_x) + (speed_y * upwind_y + DIFFUSION * around) + heat[j, span]

        def outside(buffer):
            for side, j in ((3, 0), (4, tiles + 1)):

                @pl.when(where_ref[side] == 1)
                def _(j=j):
                    for i in range(blocks):
                        buffer[j, HALO * (i + 1) : HALO * (i + 2)] = zeros

            for side, row in ((1, HALO), (2, rows + 2 * HALO)):

                @pl.when(where_ref[side] == 1)
                def _(row=row):
                    def loop(j, carry):
                        buffer[j, row : row + HALO] = zeros
                        return carry

                    lax.fori_loop(0, tiles + 2, loop, 0)

        def sweep(source, target, step):
            def tile(j, carry):
                if step == 0:

                    @pl.when(j < tiles)
                    def _():
                        loaded(j)

                    @pl.when((j > 0) & (j <= tiles))
                    def _():
                        warm(j, pl.multiple_of((j - 1) * LANES, LANES))

                along_y = column_sign[j] > 0.5
                for i in range(blocks):
                    middle, new = advance(source, j, i, along_y)
                    target[j, HALO * (i + 1) : HALO * (i + 2)] = new
                    if step and 0 < i < blocks - 1:
                        span = slice(HALO * (i - 1), HALO * i)
                        phase[j, span] = (middle if step == 1 else phase[j, span]) + new
                return carry

            lax.fori_loop(0, tiles + 2, tile, 0)
            outside(target)

        warm(0, width)
        warm(tiles + 1, width)
        sweep(here, there, 0)
        sweep(there, here, 1)
        sweep(here, there, 2)

        def store(j):
            return pltpu.make_async_copy(
                here.at[j, pl.ds(2 * HALO, rows), :],
                end_ref.at[layer, :, pl.ds(pl.multiple_of((j - 1) * LANES, LANES), LANES)],
                store_sem.at[0],
            )

        def final(j, carry):
            along_y = column_sign[j] > 0.5
            column = pl.multiple_of((j - 1) * LANES, LANES)
            for i in range(1, blocks - 1, 2):
                pair = []
                for b in (i, i + 1):
                    _, new = advance(there, j, b, along_y)
                    here[j, HALO * (b + 1) : HALO * (b + 2)] = new
                    mean = (phase[j, HALO * (b - 1) : HALO * b] + new) * (1.0 / SUBSTEPS)
                    level = jnp.maximum(jnp.abs(mean) * (1.0 / BOUND), 1e-35)
                    level = lax.rsqrt(lax.rsqrt(level * lax.rsqrt(level))) * LEVELS
                    level = jnp.minimum(level, LEVELS) + 0.5
                    pair.append(jnp.where(mean < 0, -level, level).astype(jnp.int32))
                row = HALO * (i - 1)
                codes[row // share, row % share : row % share + 2 * HALO, pl.ds(column, LANES)] = jnp.concatenate(
                    pair, axis=0
                ).astype(jnp.int16)
            store(j).start()
            return carry

        group = 8

        def leave(g, k):
            columns = pl.ds(pl.multiple_of(g * (group * LANES), LANES), group * LANES)
            return pltpu.make_async_copy(codes.at[me ^ k, :, columns], codes_ref[k].at[:, columns], code_sem.at[k])

        def finals(g, carry):
            lax.fori_loop(g * group + 1, (g + 1) * group + 1, final, 0)
            for k in range(count):
                leave(g, k).start()
            return carry

        lax.fori_loop(0, tiles // group, finals, 0)
        for k in range(count):
            pltpu.make_async_copy(codes.at[k], codes.at[k], code_sem.at[k]).wait()
        span = here.at[pl.ds(1, tiles), pl.ds(2 * HALO, rows), :]
        pltpu.make_async_copy(span, span, store_sem.at[0]).wait()

    total = tiles + 2
    edge = pl.BlockSpec((1,) + low.shape[1:], lambda i: (layer, 0, 0))
    operands = [where, *fields, *parts, low, high, light_low, light_high, west, east, polarity, heading]
    in_specs = (
        [SMEM]
        + [HBM] * 4
        + [VMEM] * count
        + [edge, edge, VMEM, VMEM, VMEM, VMEM]
        + [
            pl.BlockSpec((1, rows, LANES), lambda i: (layer, 0, 0)),
            pl.BlockSpec((1, HALO, width), lambda i: (layer, 0, 0)),
        ]
    )
    if given:
        operands.append(end)
        in_specs.append(HBM)
    out = pl.pallas_call(
        kernel,
        name=f"transport_{layer}",
        grid=(1,),
        out_shape=[jax.ShapeDtypeStruct((layers, rows, width), jnp.float32)]
        + [jax.ShapeDtypeStruct((share, width), jnp.int16)] * count,
        in_specs=in_specs,
        out_specs=[HBM] * (1 + count),
        scratch_shapes=[
            pltpu.VMEM((total, rows + 4 * HALO, LANES), jnp.float32),
            pltpu.VMEM((total, rows + 4 * HALO, LANES), jnp.float32),
            pltpu.VMEM((total, rows + 2 * HALO, LANES), jnp.float32),
            pltpu.VMEM((total, rows + 2 * HALO, LANES), jnp.float32),
            pltpu.VMEM((total, rows + 2 * HALO, LANES), jnp.float32),
            pltpu.VMEM((total, rows, LANES), jnp.float32),
            pltpu.VMEM((count, share, width), jnp.int16),
            pltpu.VMEM((rows + 2 * HALO, LANES), jnp.float32),
            pltpu.VMEM((total, HALO, LANES), jnp.float32),
            pltpu.SemaphoreType.DMA((tiles,)),
            pltpu.SemaphoreType.DMA((count,)),
            pltpu.SemaphoreType.DMA((1,)),
        ],
        input_output_aliases={len(operands) - 1: 0} if given else {},
        compiler_params=pltpu.CompilerParams(vmem_limit_bytes=LIMIT),
        cost_estimate=cost(0, 120_000_000),
    )(*operands)
    return out[0], list(out[1:])


def unpack_phase(where, layer, parts, arrived, shape, slabs):
    rows, width = arrived[0].shape
    count = len(parts)
    step = 2 * HALO
    given = slabs is not None
    factor = BOUND ** 0.125 / LEVELS

    def kernel(where_ref, *refs):
        sources, (out, values, store_sem) = refs[:count], refs[count + given :]
        me = where_ref[0]
        leaving = []
        for n, k in enumerate(parts):
            for start in range(0, rows, step):
                span = slice(start, start + step)
                level = sources[n][span, :].astype(jnp.int32).astype(jnp.float32) * factor
                square = level * level
                values[n, span, :] = (square * square) * (square * (level * jnp.abs(level)))
                place = pl.ds(pl.multiple_of((me ^ k) * width, width), width)
                leaving.append(
                    pltpu.make_async_copy(
                        values.at[n, pl.ds(start, step), :],
                        out.at[layer, pl.ds(start, step), place],
                        store_sem.at[n, start // step],
                    )
                )
                leaving[-1].start()
        for copy in leaving:
            copy.wait()

    operands = [where, *arrived]
    if given:
        operands.append(slabs)
    return pl.pallas_call(
        kernel,
        name=f"unpack_phase_{layer}",
        out_shape=jax.ShapeDtypeStruct(shape, jnp.float32),
        in_specs=[SMEM] + [VMEM] * count + [HBM] * given,
        out_specs=HBM,
        scratch_shapes=[
            pltpu.VMEM((count, rows, width), jnp.float32),
            pltpu.SemaphoreType.DMA((count, rows // step)),
        ],
        input_output_aliases={len(operands) - 1: 0} if given else {},
        compiler_params=pltpu.CompilerParams(vmem_limit_bytes=LIMIT),
        cost_estimate=cost(0, 6 * count * rows * width),
    )(*operands)


def body(
    irradiance_layers,
    initial_heat_anomaly,
    drift_rate_eastward,
    drift_rate_northward,
    extinction_factor,
    windward_polarity_eastward,
    windward_polarity_northward,
):
    fields = (initial_heat_anomaly, drift_rate_eastward, drift_rate_northward, extinction_factor)
    layers, rows, width = initial_heat_anomaly.shape
    count, lines = lax.axis_size("cols"), lax.axis_size("rows")
    me, line = lax.axis_index("cols"), lax.axis_index("rows")
    where = jnp.stack([me, line == 0, line == lines - 1, me == 0, me == count - 1]).astype(jnp.int32)
    order = sorted(range(1, count), key=lambda k: (k < count // 2, k))

    def trade(blocks):
        return {k: lax.ppermute(blocks[k], "cols", [(i, i ^ k) for i in range(count)]) for k in order}

    def pass_on(first, last, axis):
        size = lax.axis_size(axis)
        ahead = [(i, i + 1) for i in range(size - 1)]
        back = [(j, i) for i, j in ahead]
        return lax.ppermute(last, axis, ahead), lax.ppermute(first, axis, back)

    light = [None] * layers
    urgent = pack_light(where, irradiance_layers, [(0, k) for k in order], width)
    light[0] = trade(dict(zip(order, urgent)))
    irradiance_layers, urgent = lax.optimization_barrier((irradiance_layers, urgent))
    rest = [(0, 0)] + [(layer, k) for layer in range(1, layers) for k in order + [0]]
    packed = dict(zip(rest, pack_light(where, irradiance_layers, rest, width)))
    light[0][0] = packed[0, 0]
    fields, _ = lax.optimization_barrier((fields, packed[0, 0]))
    polarity = jnp.broadcast_to(
        windward_polarity_eastward.astype(jnp.float32)[:, :, None], (layers, rows, LANES)
    )
    heading = jnp.broadcast_to(
        windward_polarity_northward.astype(jnp.float32)[:, None, :], (layers, HALO, width)
    )
    first, last = pack_rows(fields, polarity)
    low, high = pass_on(first, last, "rows")
    to_east, to_west = pack_columns(fields, low, high, heading)
    west, east = pass_on(to_west, to_east, "cols")
    light[0], west, east, packed = lax.optimization_barrier((light[0], west, east, packed))
    for layer in range(1, layers):
        light[layer] = trade({k: packed[layer, k] for k in order})
        light[layer][0] = packed[layer, 0]

    end, slabs = None, None
    shape = (layers, rows // count, count * width)
    arriving = []
    for layer in range(layers):
        parts = [light[layer][k] for k in range(count)]
        top, bottom = edge_light(where, layer, parts)
        light_low, light_high = pass_on(top, bottom, "rows")
        end, codes = transport(
            where, layer, fields, parts, low, high, light_low, light_high, west, east, polarity, heading, end
        )
        if layer + 1 < layers:
            codes, light[layer + 1] = lax.optimization_barrier((codes, light[layer + 1]))
        received = trade(codes)
        received[0] = codes[0]
        arriving.append(received)
    for layer in range(layers):
        groups = [[0] + order] if layer < layers - 1 else [[0, order[-1]], order[:-1]]
        for parts in groups:
            slabs = unpack_phase(where, layer, parts, [arriving[layer][k] for k in parts], shape, slabs)
    return slabs, end


def solution(mesh):
    return jax.shard_map(
        body,
        mesh=mesh,
        in_specs=(
            P(None, ("rows", "cols"), None),
            P(None, "rows", "cols"),
            P(None, "rows", "cols"),
            P(None, "rows", "cols"),
            P(None, "rows", "cols"),
            P(None, "rows"),
            P(None, "cols"),
        ),
        out_specs=(P(None, ("rows", "cols"), None), P(None, "rows", "cols")),
        check_vma=False,
    )
```

time: 358 us -> 213 us (0.59)
  Pallas kernels: 196 us -> 75.9 us
  blocking collectives: 55.7 us -> 0 us
  waiting for transfers between devices: 43.2 us -> 85.5 us
  other arithmetic: 11.5 us -> 0.7 us
  starting transfers between devices: 34.3 us -> 41.9 us
  local copies, waits for them, and re-layouts: 10.5 us -> 6.04 us
    pallas_call x17 -> x11, Pallas kernels: 196 us -> 75.9 us  [the longest x2 56.2 us: transport(): pl.pallas_call(kernel, name=f'transport_{layer}', grid=(1,), out_shape=[j...]
    pmax x1 -> x0, blocking collectives: 55.7 us -> none  [body(): lax.pmax(jnp.stack([jnp.max(jnp.abs(initial_heat_anomaly)), jnp.max(irrad...]
    ppermute x12, waiting for transfers between devices: 15.8 us -> 70.7 us  [trade(): lax.ppermute(blocks[k], 'cols', [(i, i ^ k) for i in range(count)])]
    ppermute x8, waiting for transfers between devices: 27.4 us -> 14.8 us  [pass_on(): return (lax.ppermute(last, axis, ahead), lax.ppermute(first, axis, back))]
    reduce_max x2 -> x0, other arithmetic: 9.51 us -> none  [the longest x1 4.96 us: body(): jnp.max(irradiance_layers).astype(jnp.float32)]
    ppermute x12, starting transfers between devices: 10.4 us -> 15.7 us  [trade(): lax.ppermute(blocks[k], 'cols', [(i, i ^ k) for i in range(count)])]
    unnamed x42 -> x28, local copies, waits for them, and re-layouts: 7.62 us -> 5.81 us
  transfers between devices with their start and end apart: 20 -> 20, of which waited for: 4 -> 12; matrix products, arithmetic and copies ran while one was open for 4% -> 0% of each run, Pallas kernels for 36% -> 33%
where the time goes in v2:
time: 213 us; the launch traced here: 211 us
  waiting for transfers between devices  85.5 us (40%)
  Pallas kernels  75.9 us (36%)
  starting transfers between devices  41.9 us (20%)
  local copies, waits for them, and re-layouts  6.04 us (3%)
    ppermute x12, waiting for transfers between devices, trade(): lax.ppermute(blocks[k], 'cols', [(i, i ^ k) for i in range(count)])  70.7 us
    pallas_call x2, Pallas kernels, transport(): pl.pallas_call(kernel, name=f'transport_{layer}', grid=(1,), out_shape=[j...  56.2 us
    ppermute x8, starting transfers between devices, pass_on(): return (lax.ppermute(last, axis, ahead), lax.ppermute(first, axis, back))  26.2 us
    ppermute x12, starting transfers between devices, trade(): lax.ppermute(blocks[k], 'cols', [(i, i ^ k) for i in range(count)])  15.7 us
    ppermute x8, waiting for transfers between devices, pass_on(): return (lax.ppermute(last, axis, ahead), lax.ppermute(first, axis, back))  14.8 us
    pallas_call x3, Pallas kernels, unpack_phase(): pl.pallas_call(kernel, name=f'unpack_phase_{layer}', out_shape=jax.ShapeD...  6.74 us
    unnamed x28, local copies, waits for them, and re-layouts  5.81 us
    pallas_call x2, Pallas kernels, edge_light(): pl.pallas_call(kernel, name=f'edge_light_{layer}', out_shape=[edge, edge]...  4.48 us
  transfers between devices with their start and end apart: 20, of which 12 were waited for; matrix products, arithmetic and copies ran while one was open for 0% of the time, Pallas kernels for 33%

profile of v2, /device:TPU:9, one launch (start us, length us, event | category | flops | bytes accessed | tf_op | source)
XLA Modules:
  0.0 210.9 jit_solution(14045445404640850354)
XLA Ops:
  0.6 0.7 convert_element_type.4
  1.3 0.1 stack.39.where_ref
  1.4 2.2 %copy-done = bf16[2,64,16384]{2,1,0:T(8,128)(2,1)S(1)} copy-done((bf16[2,64,16384]{2,1,0:T(8,128)(2,1)S(1)}, bf16[2,64,16384]{2,1,0:T(8,128)(2,1)}, u32[]{:S(2)}) %copy-start) | copy-done | bytes 4194328
  3.6 0.7 pack_light_3.1
  4.3 0.0 slice-start.1
  4.3 1.8 pack_light_5.1
  6.1 0.1 broadcast_in_dim.4.refs_8_.refs_9_.refs_14_
  6.2 2.0 slice-done.1
  8.2 1.6 pack_rows.1
  9.8 3.7 %collective-permute-start.3 = (f32[2,16,4096]{2,1,0:T(8,128)S(1)}, f32[2,16,4096]{2,1,0:T(8,128)S(1)}, u32[]{:S(2)}, u32[]{:S(2)}) collective-permute-start(f32[2,16,4096]{2,1,0:T(8,128)S(1)} %get-tuple-element.60), channel_id=1, source_target_pairs={{0,4},{4,8},{8,12},{12,16},{16,20},{20,24},{24,28},{1,5},{5,9},{9,... | collective-permute-start | bytes 1572872 | tf_op jit(solution)/shard_map/ppermute | solution.py:523
  13.5 1.9 collective-permute-start.4
  15.4 2.4 %collective-permute-start.1 = (bf16[64,4224]{1,0:T(8,128)(2,1)S(1)}, bf16[64,4224]{1,0:T(8,128)(2,1)}, u32[]{:S(2)}, u32[]{:S(2)}) collective-permute-start(bf16[64,4224]{1,0:T(8,128)(2,1)S(1)} %get-tuple-element.51), channel_id=1, source_target_pairs={{0,2},{1,3},{2,0},{3,1},{4,6},{5,7},{6,4},{7,5},{8,10},{9,11},{10,... | collective-permute-start | bytes 1622024 | tf_op jit(solution)/shard_map/ppermute | solution.py:517
  17.8 0.0 collective-permute-start.2
  17.8 1.3 collective-permute-start
  19.1 0.5 collective-permute-done.3.refs_8_
  19.6 7.7 %collective-permute-done.4.refs_9_ = f32[2,16,4096]{2,1,0:T(8,128)S(1)} collective-permute-done((f32[2,16,4096]{2,1,0:T(8,128)S(1)}, f32[2,16,4096]{2,1,0:T(8,128)S(1)}, u32[]{:S(2)}, u32[]{:S(2)}) %collective-permute-start.4) | collective-permute-done | bytes 524320 | tf_op jit(solution)/shard_map/ppermute | solution.py:523
  27.3 0.0 copy-start.2
  27.3 4.4 %pack_columns.1 = (f32[272,128]{1,0:T(8,128)S(1)}, f32[272,128]{1,0:T(8,128)S(1)}) custom-call(f32[2,256,4096]{2,1,0:T(8,128)S(1)} %bitcast.6, f32[2,256,4096]{2,1,0:T(8,128)} %refs_1_.6, f32[2,256,4096]{2,1,0:T(8,128)} %refs_2_.6, f32[2,256,4096]{2,1,0:T(8,128)} %refs_3_.6, f32[2,256,4096]{2,1,0:T(8,128)S(1)} %bitcast.6, f32[2,256,4096]{2,1,0:T(8,128)} %refs_1_.6, ...), custom_call_target="tpu_custom_call" | custom-call | bytes 2097152 | tf_op jit(solution)/shard_map/pack_columns/pallas_call | solution.py:165
  31.7 3.2 %collective-permute-start.5 = (f32[272,128]{1,0:T(8,128)S(1)}, f32[272,128]{1,0:T(8,128)S(1)}, u32[]{:S(2)}, u32[]{:S(2)}) collective-permute-start(f32[272,128]{1,0:T(8,128)S(1)} %get-tuple-element.62), channel_id=1, source_target_pairs={{0,1},{1,2},{2,3},{4,5},{5,6},{6,7},{8,9},{9,10},{10,11},{12,13},{... | collective-permute-start | bytes 417800 | tf_op jit(solution)/shard_map/ppermute | solution.py:523
  35.0 2.1 collective-permute-start.6
  37.1 14.7 %collective-permute-done.1.refs_2_.refs_6_ = bf16[64,4224]{1,0:T(8,128)(2,1)} collective-permute-done((bf16[64,4224]{1,0:T(8,128)(2,1)S(1)}, bf16[64,4224]{1,0:T(8,128)(2,1)}, u32[]{:S(2)}, u32[]{:S(2)}) %collective-permute-start.1) | collective-permute-done | bytes 540704 | tf_op jit(solution)/shard_map/ppermute | solution.py:517
  51.7 12.5 %collective-permute-done.2.refs_3_.refs_7_ = bf16[64,4224]{1,0:T(8,128)(2,1)} collective-permute-done((bf16[64,4224]{1,0:T(8,128)(2,1)S(1)}, bf16[64,4224]{1,0:T(8,128)(2,1)}, u32[]{:S(2)}, u32[]{:S(2)}) %collective-permute-start.2) | collective-permute-done | bytes 540704 | tf_op jit(solution)/shard_map/ppermute | solution.py:517
  64.2 2.0 collective-permute-done.5.refs_12_
  66.3 3.2 %collective-permute-start.10 = (bf16[64,4224]{1,0:T(8,128)(2,1)}, bf16[64,4224]{1,0:T(8,128)(2,1)}, u32[]{:S(2)}, u32[]{:S(2)}) collective-permute-start(bf16[64,4224]{1,0:T(8,128)(2,1)} %get-tuple-element.82), channel_id=1, source_target_pairs={{0,2},{1,3},{2,0},{3,1},{4,6},{5,7},{6,4},{7,5},{8,10},{9,11},{10,... | collective-permute-start | bytes 1622024 | tf_op jit(solution)/shard_map/ppermute | solution.py:517
  69.5 2.2 %edge_light_0.1 = (bf16[8,4224]{1,0:T(8,128)(2,1)}, bf16[8,4224]{1,0:T(8,128)(2,1)}) custom-call(s32[5]{0:T(128)} %copy-done.7, bf16[64,4224]{1,0:T(8,128)(2,1)} %copy-done.1, bf16[64,4224]{1,0:T(8,128)(2,1)} %collective-permute-done.refs_1_.refs_5_, bf16[64,4224]{1,0:T(8,128)(2,1)} %collective-permute-done.1.refs_2_.refs_6_, ...), custom_call_target="tpu_custom_call" | custom-call | bytes 270336 | tf_op jit(solution)/shard_map/edge_light_0/pallas_call | solution.py:196
  71.7 5.4 %collective-permute-start.7 = (bf16[8,4224]{1,0:T(8,128)(2,1)}, bf16[8,4224]{1,0:T(8,128)(2,1)S(1)}, u32[]{:S(2)}, u32[]{:S(2)}) collective-permute-start(bf16[8,4224]{1,0:T(8,128)(2,1)} %get-tuple-element.72), channel_id=1, source_target_pairs={{0,4},{4,8},{8,12},{12,16},{16,20},{20,24},{24,28},{1,5},{5,9},{9,... | collective-permute-start | bytes 202760 | tf_op jit(solution)/shard_map/ppermute | solution.py:523
  77.2 2.1 collective-permute-start.8
  79.3 4.3 %collective-permute-done.8.refs_11_ = bf16[8,4224]{1,0:T(8,128)(2,1)S(1)} collective-permute-done((bf16[8,4224]{1,0:T(8,128)(2,1)}, bf16[8,4224]{1,0:T(8,128)(2,1)S(1)}, u32[]{:S(2)}, u32[]{:S(2)}) %collective-permute-start.8) | collective-permute-done | bytes 67616 | tf_op jit(solution)/shard_map/ppermute | solution.py:523
  83.5 28.1 %transport_0.1 = (f32[2,256,4096]{2,1,0:T(8,128)}, s16[64,4096]{1,0:T(8,128)(2,1)S(1)}, s16[64,4096]{1,0:T(8,128)(2,1)S(1)}, s16[64,4096]{1,0:T(8,128)(2,1)}, s16[64,4096]{1,0:T(8,128)(2,1)S(1)}) custom-call(s32[5]{0:T(128)S(1)} %copy-done.8, f32[2,256,4096]{2,1,0:T(8,128)} %refs_0_.6, f32[2,256,4096]{2,1,0:T(8,128)} %refs_1_.6, f32[2,256,4096]{2,1,0:T(8,128)} %refs_2_.6, ...), custom_call_target="tpu_custom_call" | custom-call | bytes 120000000 | tf_op jit(solution)/shard_map/transport_0/pallas_call | solution.py:423
  111.6 0.8 copy-done.5
  112.4 0.8 copy-done.10
  113.2 2.7 %collective-permute-done.11.refs_3_.refs_7_ = bf16[64,4224]{1,0:T(8,128)(2,1)} collective-permute-done((bf16[64,4224]{1,0:T(8,128)(2,1)}, bf16[64,4224]{1,0:T(8,128)(2,1)}, u32[]{:S(2)}, u32[]{:S(2)}) %collective-permute-start.11) | collective-permute-done | bytes 540704 | tf_op jit(solution)/shard_map/ppermute | solution.py:517
  115.9 2.2 %edge_light_1.1 = (bf16[8,4224]{1,0:T(8,128)(2,1)}, bf16[8,4224]{1,0:T(8,128)(2,1)}) custom-call(s32[5]{0:T(128)} %copy-done.7, bf16[64,4224]{1,0:T(8,128)(2,1)} %copy-done.3, bf16[64,4224]{1,0:T(8,128)(2,1)} %collective-permute-done.9.refs_1_.refs_5_, bf16[64,4224]{1,0:T(8,128)(2,1)} %collective-permute-done.10.refs_2_.refs_6_, ...), custom_call_target="tpu_custom_call" | custom-call | bytes 270336 | tf_op jit(solution)/shard_map/edge_light_1/pallas_call | solution.py:196
  118.2 5.9 %collective-permute-start.12 = (bf16[8,4224]{1,0:T(8,128)(2,1)}, bf16[8,4224]{1,0:T(8,128)(2,1)S(1)}, u32[]{:S(2)}, u32[]{:S(2)}) collective-permute-start(bf16[8,4224]{1,0:T(8,128)(2,1)} %get-tuple-element.88), channel_id=1, source_target_pairs={{0,4},{4,8},{8,12},{12,16},{16,20},{20,24},{24,28},{1,5},{5,9},{9,... | collective-permute-start | bytes 202760 | tf_op jit(solution)/shard_map/ppermute | solution.py:523
  124.0 1.9 collective-permute-start.13
  126.0 2.3 %collective-permute-start.18 = (s16[64,4096]{1,0:T(8,128)(2,1)}, s16[64,4096]{1,0:T(8,128)(2,1)S(1)}, u32[]{:S(2)}, u32[]{:S(2)}) collective-permute-start(s16[64,4096]{1,0:T(8,128)(2,1)} %copy-done.10), channel_id=1, source_target_pairs={{0,3},{1,2},{2,1},{3,0},{4,7},{5,6},{6,5},{7,4},{8,11},{9,10},{10,... | collective-permute-start | bytes 1572872 | tf_op jit(solution)/shard_map/ppermute | solution.py:517
  128.2 1.6 collective-permute-start.19
  129.9 0.3 collective-permute-done.13.refs_11_
  130.2 28.2 %transport_1.1 = (f32[2,256,4096]{2,1,0:T(8,128)}, s16[64,4096]{1,0:T(8,128)(2,1)S(1)}, s16[64,4096]{1,0:T(8,128)(2,1)S(1)}, s16[64,4096]{1,0:T(8,128)(2,1)S(1)}, s16[64,4096]{1,0:T(8,128)(2,1)S(1)}) custom-call(s32[5]{0:T(128)S(1)} %copy-done.9, f32[2,256,4096]{2,1,0:T(8,128)} %refs_0_.6, ...), custom_call_target="tpu_custom_call", output_to_operand_aliasing={{0}: (17, {})} | custom-call | bytes 120000000 | tf_op jit(solution)/shard_map/transport_1/pallas_call | solution.py:423
  158.3 3.7 %collective-permute-start.16 = (s16[64,4096]{1,0:T(8,128)(2,1)S(1)}, s16[64,4096]{1,0:T(8,128)(2,1)S(1)}, u32[]{:S(2)}, u32[]{:S(2)}) collective-permute-start(s16[64,4096]{1,0:T(8,128)(2,1)S(1)} %get-tuple-element.94), channel_id=1, source_target_pairs={{0,1},{1,0},{2,3},{3,2},{4,5},{5,4},{6,7},{7,6},{8,9},{9,8},{10,11... | collective-permute-start | bytes 1572872 | tf_op jit(solution)/shard_map/ppermute | solution.py:517
  162.1 1.3 collective-permute-start.15
  163.3 0.2 collective-permute-done.18.refs_2_
  163.5 2.8 %unpack_phase_0.1.refs_2_ = f32[2,64,16384]{2,1,0:T(8,128)} custom-call(s32[5]{0:T(128)S(1)} %copy-done.9, s16[64,4096]{1,0:T(8,128)(2,1)S(1)} %copy-done.6, s16[64,4096]{1,0:T(8,128)(2,1)S(1)} %collective-permute-done.17.refs_1_, s16[64,4096]{1,0:T(8,128)(2,1)S(1)} %collective-permute-done.18.refs_2_, s16[64,4096]{1,0:T(8,128)(2,1)S(1)} %collective-permute-done.19.refs_3_), custom_call_target="tpu_custom_call" | custom-call | bytes 6291456 | tf_op jit(solution)/shard_map/unpack_phase_0/pallas_call | solution.py:484
  166.3 14.1 %collective-permute-done.16.refs_1_ = s16[64,4096]{1,0:T(8,128)(2,1)S(1)} collective-permute-done((s16[64,4096]{1,0:T(8,128)(2,1)S(1)}, s16[64,4096]{1,0:T(8,128)(2,1)S(1)}, u32[]{:S(2)}, u32[]{:S(2)}) %collective-permute-start.16) | collective-permute-done | bytes 524320 | tf_op jit(solution)/shard_map/ppermute | solution.py:517
  180.4 2.0 unpack_phase_1.2.refs_2_
  182.4 14.0 %collective-permute-done.14.refs_0_ = s16[64,4096]{1,0:T(8,128)(2,1)S(1)} collective-permute-done((s16[64,4096]{1,0:T(8,128)(2,1)S(1)}, s16[64,4096]{1,0:T(8,128)(2,1)S(1)}, u32[]{:S(2)}, u32[]{:S(2)}) %collective-permute-start.14) | collective-permute-done | bytes 524320 | tf_op jit(solution)/shard_map/ppermute | solution.py:517
  196.4 12.5 %collective-permute-done.15.refs_1_ = s16[64,4096]{1,0:T(8,128)(2,1)S(1)} collective-permute-done((s16[64,4096]{1,0:T(8,128)(2,1)S(1)}, s16[64,4096]{1,0:T(8,128)(2,1)S(1)}, u32[]{:S(2)}, u32[]{:S(2)}) %collective-permute-start.15) | collective-permute-done | bytes 524320 | tf_op jit(solution)/shard_map/ppermute | solution.py:517
  208.9 2.0 unpack_phase_1.3
  (37 shorter events, 0.1 us)
Async XLA Ops:
  1.4 2.2 %copy-start = (bf16[2,64,16384]{2,1,0:T(8,128)(2,1)S(1)}, bf16[2,64,16384]{2,1,0:T(8,128)(2,1)}, u32[]{:S(2)}) copy-start(bf16[2,64,16384]{2,1,0:T(8,128)(2,1)} %refs_14_) | copy-start | bytes 12582916
  3.6 0.7 copy-start.7
  3.6 2.6 %slice-start = ((s8[8388608]{0:T(1024)(128)(4,1)}), s8[4194304]{0:T(1024)(128)(4,1)S(1)}, s32[]{:S(2)}) async-start(s8[8388608]{0:T(1024)(128)(4,1)} %bitcast.5), calls=%async_computation | async-start | bytes 8388608
  4.3 3.9 %slice-start.1 = ((s8[8388608]{0:T(1024)(128)(4,1)}), s8[4194304]{0:T(1024)(128)(4,1)S(1)}, s32[]{:S(2)}) async-start(s8[8388608]{0:T(1024)(128)(4,1)} %bitcast.5), calls=%async_computation.1 | async-start | bytes 8388608
  6.1 3.7 %copy-start.1 = (bf16[64,4224]{1,0:T(8,128)(2,1)}, bf16[64,4224]{1,0:T(8,128)(2,1)S(1)}, u32[]{:S(2)}) copy-start(bf16[64,4224]{1,0:T(8,128)(2,1)S(1)} %get-tuple-element.68.refs_0_.refs_4_) | copy-start | bytes 1622020
  6.1 3.7 %copy-start.3 = (bf16[64,4224]{1,0:T(8,128)(2,1)}, bf16[64,4224]{1,0:T(8,128)(2,1)S(1)}, u32[]{:S(2)}) copy-start(bf16[64,4224]{1,0:T(8,128)(2,1)S(1)} %get-tuple-element.84.refs_0_.refs_4_) | copy-start | bytes 1622020
  8.2 10.9 %copy-start.11 = (s32[2,4096]{1,0:T(2,128)S(1)}, s32[2,4096]{1,0:T(2,128)}, u32[]{:S(2)}) copy-start(s32[2,4096]{1,0:T(2,128)} %param.13) | copy-start | bytes 98308
  9.8 9.8 %collective-permute-start.3 = (f32[2,16,4096]{2,1,0:T(8,128)S(1)}, f32[2,16,4096]{2,1,0:T(8,128)S(1)}, u32[]{:S(2)}, u32[]{:S(2)}) collective-permute-start(f32[2,16,4096]{2,1,0:T(8,128)S(1)} %get-tuple-element.60), channel_id=1, source_target_pairs={{0,4},{4,8},{8,12},{12,16},{16,20},{20,24},{24,28},{1,5},{5,9},{9,... | collective-permute-start | bytes 1572872 | tf_op jit(solution)/shard_map/ppermute | solution.py:523
  13.5 13.8 %collective-permute-start.4 = (f32[2,16,4096]{2,1,0:T(8,128)S(1)}, f32[2,16,4096]{2,1,0:T(8,128)S(1)}, u32[]{:S(2)}, u32[]{:S(2)}) collective-permute-start(f32[2,16,4096]{2,1,0:T(8,128)S(1)} %get-tuple-element.61), channel_id=1, source_target_pairs={{4,0},{8,4},{12,8},{16,12},{20,16},{24,20},{28,24},{5,1},{9,5},{13... | collective-permute-start | bytes 1572872 | tf_op jit(solution)/shard_map/ppermute | solution.py:523
  15.4 36.3 %collective-permute-start.1 = (bf16[64,4224]{1,0:T(8,128)(2,1)S(1)}, bf16[64,4224]{1,0:T(8,128)(2,1)}, u32[]{:S(2)}, u32[]{:S(2)}) collective-permute-start(bf16[64,4224]{1,0:T(8,128)(2,1)S(1)} %get-tuple-element.51), channel_id=1, source_target_pairs={{0,2},{1,3},{2,0},{3,1},{4,6},{5,7},{6,4},{7,5},{8,10},{9,11},{10,... | collective-permute-start | bytes 1622024 | tf_op jit(solution)/shard_map/ppermute | solution.py:517
  17.8 46.4 %collective-permute-start.2 = (bf16[64,4224]{1,0:T(8,128)(2,1)S(1)}, bf16[64,4224]{1,0:T(8,128)(2,1)}, u32[]{:S(2)}, u32[]{:S(2)}) collective-permute-start(bf16[64,4224]{1,0:T(8,128)(2,1)S(1)} %get-tuple-element.52), channel_id=1, source_target_pairs={{0,3},{1,2},{2,1},{3,0},{4,7},{5,6},{6,5},{7,4},{8,11},{9,10},{10,... | collective-permute-start | bytes 1622024 | tf_op jit(solution)/shard_map/ppermute | solution.py:517
  17.8 46.4 %collective-permute-start = (bf16[64,4224]{1,0:T(8,128)(2,1)S(1)}, bf16[64,4224]{1,0:T(8,128)(2,1)}, u32[]{:S(2)}, u32[]{:S(2)}) collective-permute-start(bf16[64,4224]{1,0:T(8,128)(2,1)S(1)} %get-tuple-element.53), channel_id=1, source_target_pairs={{0,1},{1,0},{2,3},{3,2},{4,5},{5,4},{6,7},{7,6},{8,9},{9,8},{10,11... | collective-permute-start | bytes 1622024 | tf_op jit(solution)/shard_map/ppermute | solution.py:517
  27.3 56.2 %copy-start.2 = (bf16[64,4224]{1,0:T(8,128)(2,1)S(1)}, bf16[64,4224]{1,0:T(8,128)(2,1)}, u32[]{:S(2)}) copy-start(bf16[64,4224]{1,0:T(8,128)(2,1)} %copy-done.1) | copy-start | bytes 1622020
  27.3 56.2 %copy-start.8 = (s32[5]{0:T(128)S(1)}, s32[5]{0:T(128)}, u32[]{:S(2)}) copy-start(s32[5]{0:T(128)} %copy-done.7) | copy-start | bytes 64
  31.7 34.5 %collective-permute-start.5 = (f32[272,128]{1,0:T(8,128)S(1)}, f32[272,128]{1,0:T(8,128)S(1)}, u32[]{:S(2)}, u32[]{:S(2)}) collective-permute-start(f32[272,128]{1,0:T(8,128)S(1)} %get-tuple-element.62), channel_id=1, source_target_pairs={{0,1},{1,2},{2,3},{4,5},{5,6},{6,7},{8,9},{9,10},{10,11},{12,13},{... | collective-permute-start | bytes 417800 | tf_op jit(solution)/shard_map/ppermute | solution.py:523
  35.0 31.3 %collective-permute-start.6 = (f32[272,128]{1,0:T(8,128)S(1)}, f32[272,128]{1,0:T(8,128)S(1)}, u32[]{:S(2)}, u32[]{:S(2)}) collective-permute-start(f32[272,128]{1,0:T(8,128)S(1)} %get-tuple-element.63), channel_id=1, source_target_pairs={{1,0},{2,1},{3,2},{5,4},{6,5},{7,6},{9,8},{10,9},{11,10},{13,12},{... | collective-permute-start | bytes 417800 | tf_op jit(solution)/shard_map/ppermute | solution.py:523
  66.3 47.0 %collective-permute-start.9 = (bf16[64,4224]{1,0:T(8,128)(2,1)}, bf16[64,4224]{1,0:T(8,128)(2,1)}, u32[]{:S(2)}, u32[]{:S(2)}) collective-permute-start(bf16[64,4224]{1,0:T(8,128)(2,1)} %get-tuple-element.81), channel_id=1, source_target_pairs={{0,1},{1,0},{2,3},{3,2},{4,5},{5,4},{6,7},{7,6},{8,9},{9,8},{10,11... | collective-permute-start | bytes 1622024 | tf_op jit(solution)/shard_map/ppermute | solution.py:517
  66.3 47.0 %collective-permute-start.10 = (bf16[64,4224]{1,0:T(8,128)(2,1)}, bf16[64,4224]{1,0:T(8,128)(2,1)}, u32[]{:S(2)}, u32[]{:S(2)}) collective-permute-start(bf16[64,4224]{1,0:T(8,128)(2,1)} %get-tuple-element.82), channel_id=1, source_target_pairs={{0,2},{1,3},{2,0},{3,1},{4,6},{5,7},{6,4},{7,5},{8,10},{9,11},{10,... | collective-permute-start | bytes 1622024 | tf_op jit(solution)/shard_map/ppermute | solution.py:517
  69.5 46.5 %collective-permute-start.11 = (bf16[64,4224]{1,0:T(8,128)(2,1)}, bf16[64,4224]{1,0:T(8,128)(2,1)}, u32[]{:S(2)}, u32[]{:S(2)}) collective-permute-start(bf16[64,4224]{1,0:T(8,128)(2,1)} %get-tuple-element.83), channel_id=1, source_target_pairs={{0,3},{1,2},{2,1},{3,0},{4,7},{5,6},{6,5},{7,4},{8,11},{9,10},{10,... | collective-permute-start | bytes 1622024 | tf_op jit(solution)/shard_map/ppermute | solution.py:517
  71.7 7.5 %collective-permute-start.7 = (bf16[8,4224]{1,0:T(8,128)(2,1)}, bf16[8,4224]{1,0:T(8,128)(2,1)S(1)}, u32[]{:S(2)}, u32[]{:S(2)}) collective-permute-start(bf16[8,4224]{1,0:T(8,128)(2,1)} %get-tuple-element.72), channel_id=1, source_target_pairs={{0,4},{4,8},{8,12},{12,16},{16,20},{20,24},{24,28},{1,5},{5,9},{9,... | collective-permute-start | bytes 202760 | tf_op jit(solution)/shard_map/ppermute | solution.py:523
  77.2 53.0 %copy-start.4 = (bf16[64,4224]{1,0:T(8,128)(2,1)S(1)}, bf16[64,4224]{1,0:T(8,128)(2,1)}, u32[]{:S(2)}) copy-start(bf16[64,4224]{1,0:T(8,128)(2,1)} %copy-done.3) | copy-start | bytes 1622020
  77.2 53.0 %copy-start.9 = (s32[5]{0:T(128)S(1)}, s32[5]{0:T(128)}, u32[]{:S(2)}) copy-start(s32[5]{0:T(128)} %copy-done.7) | copy-start | bytes 64
  77.2 6.3 %collective-permute-start.8 = (bf16[8,4224]{1,0:T(8,128)(2,1)}, bf16[8,4224]{1,0:T(8,128)(2,1)S(1)}, u32[]{:S(2)}, u32[]{:S(2)}) collective-permute-start(bf16[8,4224]{1,0:T(8,128)(2,1)} %get-tuple-element.73), channel_id=1, source_target_pairs={{4,0},{8,4},{12,8},{16,12},{20,16},{24,20},{28,24},{5,1},{9,5},{13... | collective-permute-start | bytes 202760 | tf_op jit(solution)/shard_map/ppermute | solution.py:523
  111.6 0.8 copy-start.5
  112.4 0.8 copy-start.10
  115.9 46.1 %collective-permute-start.17 = (s16[64,4096]{1,0:T(8,128)(2,1)}, s16[64,4096]{1,0:T(8,128)(2,1)S(1)}, u32[]{:S(2)}, u32[]{:S(2)}) collective-permute-start(s16[64,4096]{1,0:T(8,128)(2,1)} %get-tuple-element.96), channel_id=1, source_target_pairs={{0,2},{1,3},{2,0},{3,1},{4,6},{5,7},{6,4},{7,5},{8,10},{9,11},{10,... | collective-permute-start | bytes 1572872 | tf_op jit(solution)/shard_map/ppermute | solution.py:517
  118.2 11.7 %collective-permute-start.12 = (bf16[8,4224]{1,0:T(8,128)(2,1)}, bf16[8,4224]{1,0:T(8,128)(2,1)S(1)}, u32[]{:S(2)}, u32[]{:S(2)}) collective-permute-start(bf16[8,4224]{1,0:T(8,128)(2,1)} %get-tuple-element.88), channel_id=1, source_target_pairs={{0,4},{4,8},{8,12},{12,16},{16,20},{20,24},{24,28},{1,5},{5,9},{9,... | collective-permute-start | bytes 202760 | tf_op jit(solution)/shard_map/ppermute | solution.py:523
  124.0 6.1 %collective-permute-start.13 = (bf16[8,4224]{1,0:T(8,128)(2,1)}, bf16[8,4224]{1,0:T(8,128)(2,1)S(1)}, u32[]{:S(2)}, u32[]{:S(2)}) collective-permute-start(bf16[8,4224]{1,0:T(8,128)(2,1)} %get-tuple-element.89), channel_id=1, source_target_pairs={{4,0},{8,4},{12,8},{16,12},{20,16},{24,20},{28,24},{5,1},{9,5},{13... | collective-permute-start | bytes 202760 | tf_op jit(solution)/shard_map/ppermute | solution.py:523
  126.0 37.6 %collective-permute-start.18 = (s16[64,4096]{1,0:T(8,128)(2,1)}, s16[64,4096]{1,0:T(8,128)(2,1)S(1)}, u32[]{:S(2)}, u32[]{:S(2)}) collective-permute-start(s16[64,4096]{1,0:T(8,128)(2,1)} %copy-done.10), channel_id=1, source_target_pairs={{0,3},{1,2},{2,1},{3,0},{4,7},{5,6},{6,5},{7,4},{8,11},{9,10},{10,... | collective-permute-start | bytes 1572872 | tf_op jit(solution)/shard_map/ppermute | solution.py:517
  128.2 35.3 %collective-permute-start.19 = (s16[64,4096]{1,0:T(8,128)(2,1)S(1)}, s16[64,4096]{1,0:T(8,128)(2,1)S(1)}, u32[]{:S(2)}, u32[]{:S(2)}) collective-permute-start(s16[64,4096]{1,0:T(8,128)(2,1)S(1)} %get-tuple-element.98), channel_id=1, source_target_pairs={{0,1},{1,0},{2,3},{3,2},{4,5},{5,4},{6,7},{7,6},{8,9},{9,8},{10,11... | collective-permute-start | bytes 1572872 | tf_op jit(solution)/shard_map/ppermute | solution.py:517
  130.2 33.4 %copy-start.6 = (s16[64,4096]{1,0:T(8,128)(2,1)S(1)}, s16[64,4096]{1,0:T(8,128)(2,1)}, u32[]{:S(2)}) copy-start(s16[64,4096]{1,0:T(8,128)(2,1)} %copy-done.5) | copy-start | bytes 1572868
  158.3 22.1 %collective-permute-start.16 = (s16[64,4096]{1,0:T(8,128)(2,1)S(1)}, s16[64,4096]{1,0:T(8,128)(2,1)S(1)}, u32[]{:S(2)}, u32[]{:S(2)}) collective-permute-start(s16[64,4096]{1,0:T(8,128)(2,1)S(1)} %get-tuple-element.94), channel_id=1, source_target_pairs={{0,1},{1,0},{2,3},{3,2},{4,5},{5,4},{6,7},{7,6},{8,9},{9,8},{10,11... | collective-permute-start | bytes 1572872 | tf_op jit(solution)/shard_map/ppermute | solution.py:517
  162.1 34.3 %collective-permute-start.14 = (s16[64,4096]{1,0:T(8,128)(2,1)S(1)}, s16[64,4096]{1,0:T(8,128)(2,1)S(1)}, u32[]{:S(2)}, u32[]{:S(2)}) collective-permute-start(s16[64,4096]{1,0:T(8,128)(2,1)S(1)} %get-tuple-element.91), channel_id=1, source_target_pairs={{0,2},{1,3},{2,0},{3,1},{4,6},{5,7},{6,4},{7,5},{8,10},{9,11},{10,... | collective-permute-start | bytes 1572872 | tf_op jit(solution)/shard_map/ppermute | solution.py:517
  162.1 46.8 %collective-permute-start.15 = (s16[64,4096]{1,0:T(8,128)(2,1)S(1)}, s16[64,4096]{1,0:T(8,128)(2,1)S(1)}, u32[]{:S(2)}, u32[]{:S(2)}) collective-permute-start(s16[64,4096]{1,0:T(8,128)(2,1)S(1)} %get-tuple-element.92), channel_id=1, source_target_pairs={{0,3},{1,2},{2,1},{3,0},{4,7},{5,6},{6,5},{7,4},{8,11},{9,10},{10,... | collective-permute-start | bytes 1572872 | tf_op jit(solution)/shard_map/ppermute | solution.py:517

commit v3 on v2

--- a/solution.py
+++ b/solution.py
@@ -72,38 +72,81 @@
     return [(sum(sizes[:n]), size) for n, size in enumerate(sizes)]
 
 
-def pack_rows(fields, polarity):
+def pack_first(where, irradiance, parts, fields, polarity):
     layers, rows, width = fields[0].shape
-    count = len(fields)
+    slabs, share, columns = irradiance.shape
+    count, pieces = len(fields), len(parts)
     places = spans(count)
     total = -(-sum(places[-1]) // HALO) * HALO
 
-    def kernel(*refs):
-        first, last = refs[-2:]
+    def kernel(where_ref, irradiance_ref, *refs):
+        fields_ref, (polarity_ref,), refs = refs[:count], refs[count : count + 1], refs[count + 1 :]
+        outs, (first, last, sides, edges, light_sem, side_sem, edge_sem) = refs[:pieces], refs[pieces:]
+        copies, beside, mains = [], [], []
+        for n, k in enumerate(parts):
+            target = where_ref[0] ^ k
+            start = pl.multiple_of(target * width, LANES)
+            after = pl.multiple_of(jnp.minimum(start + width, columns - LANES), LANES)
+            before = pl.multiple_of(jnp.maximum(start - LANES, 0), LANES)
+            for side, at in ((0, before), (1, after)):
+                beside.append(
+                    pltpu.make_async_copy(
+                        irradiance_ref.at[0, :, pl.ds(at, LANES)], sides.at[n, side], side_sem.at[n, side]
+                    )
+                )
+            mains.append(
+                pltpu.make_async_copy(
+                    irradiance_ref.at[0, :, pl.ds(start, width)], outs[n].at[:, pl.ds(0, width)], light_sem.at[n]
+                )
+            )
+        for n in range(count):
+            for edge, row in ((0, 0), (1, rows - HALO)):
+                copies.append(
+                    pltpu.make_async_copy(
+                        fields_ref[n].at[:, pl.ds(row, HALO), :], edges.at[n, edge], edge_sem.at[n, edge]
+                    )
+                )
+        for copy in (*copies, *beside, *mains):
+            copy.start()
+        for copy in copies:
+            copy.wait()
         for n, (start, size) in enumerate(places):
-            below, above = refs[2 * n][...], refs[2 * n + 1][...]
             for tile in range(width // LANES):
                 lanes = slice(tile * LANES, (tile + 1) * LANES)
-                source = slice(0, LANES) if n == count else lanes
-                first[:, start : start + size, lanes] = below[:, :size, source]
-                last[:, start : start + size, lanes] = above[:, HALO - size :, source]
-
-    def block(size, row):
-        return pl.BlockSpec((layers, HALO, size), lambda i: (0, row, 0))
+                for layer in range(layers):
+                    if n == count:
+                        below, above = polarity_ref[layer, :size], polarity_ref[layer, rows - size :]
+                    else:
+                        below, above = edges[n, 0, layer, :size, lanes], edges[n, 1, layer, HALO - size :, lanes]
+                    first[layer, start : start + size, lanes] = below
+                    last[layer, start : start + size, lanes] = above
+        for copy in beside:
+            copy.wait()
+        near = lax.broadcasted_iota(jnp.int32, (share, LANES), 1) < LANES // 2
+        for n in range(pieces):
+            west, east = sides[n, 0].astype(jnp.float32), sides[n, 1].astype(jnp.float32)
+            outs[n][:, width:] = jnp.where(near, east, west).astype(irradiance.dtype)
+        for copy in mains:
+            copy.wait()
 
     edge = jax.ShapeDtypeStruct((layers, total, width), jnp.float32)
-    out = pl.BlockSpec((layers, total, width), lambda i: (0, 0, 0))
-    sizes = [width] * count + [LANES]
-    return pl.pallas_call(
+    out = pl.pallas_call(
         kernel,
-        name="pack_rows",
-        grid=(1,),
-        out_shape=[edge, edge],
-        in_specs=[block(size, row) for size in sizes for row in (0, rows // HALO - 1)],
-        out_specs=[out, out],
+        name="pack_first",
+        out_shape=[jax.ShapeDtypeStruct((share, width + LANES), irradiance.dtype)] * pieces + [edge, edge],
+        in_specs=[SMEM] + [HBM] * (1 + count) + [VMEM],
+        out_specs=[VMEM] * (pieces + 2),
+        scratch_shapes=[
+            pltpu.VMEM((pieces, 2, share, LANES), irradiance.dtype),
+            pltpu.VMEM((count, 2, layers, HALO, width), jnp.float32),
+            pltpu.SemaphoreType.DMA((pieces,)),
+            pltpu.SemaphoreType.DMA((pieces, 2)),
+            pltpu.SemaphoreType.DMA((count, 2)),
+        ],
         compiler_params=pltpu.CompilerParams(vmem_limit_bytes=LIMIT),
         cost_estimate=cost(0, 16 * layers * HALO * width),
-    )(*[field for field in (*fields, polarity) for _ in range(2)])
+    )(where, irradiance, *fields, polarity)
+    return out[:pieces], out[pieces], out[pieces + 1]
 
 
 def pack_columns(fields, low, high, heading):
@@ -523,23 +566,21 @@
         return lax.ppermute(last, axis, ahead), lax.ppermute(first, axis, back)
 
     light = [None] * layers
-    urgent = pack_light(where, irradiance_layers, [(0, k) for k in order], width)
-    light[0] = trade(dict(zip(order, urgent)))
-    irradiance_layers, urgent = lax.optimization_barrier((irradiance_layers, urgent))
-    rest = [(0, 0)] + [(layer, k) for layer in range(1, layers) for k in order + [0]]
-    packed = dict(zip(rest, pack_light(where, irradiance_layers, rest, width)))
-    light[0][0] = packed[0, 0]
-    fields, _ = lax.optimization_barrier((fields, packed[0, 0]))
     polarity = jnp.broadcast_to(
         windward_polarity_eastward.astype(jnp.float32)[:, :, None], (layers, rows, LANES)
     )
     heading = jnp.broadcast_to(
         windward_polarity_northward.astype(jnp.float32)[:, None, :], (layers, HALO, width)
     )
-    first, last = pack_rows(fields, polarity)
+    urgent, first, last = pack_first(where, irradiance_layers, order, fields, polarity)
+    light[0] = trade(dict(zip(order, urgent)))
     low, high = pass_on(first, last, "rows")
     to_east, to_west = pack_columns(fields, low, high, heading)
     west, east = pass_on(to_west, to_east, "cols")
+    irradiance_layers, _ = lax.optimization_barrier((irradiance_layers, to_east))
+    rest = [(0, 0)] + [(layer, k) for layer in range(1, layers) for k in order + [0]]
+    packed = dict(zip(rest, pack_light(where, irradiance_layers, rest, width)))
+    light[0][0] = packed[0, 0]
     light[0], west, east, packed = lax.optimization_barrier((light[0], west, east, packed))
     for layer in range(1, layers):
         light[layer] = trade({k: packed[layer, k] for k in order})

time: 213 us -> 210 us (0.986)
  local copies, waits for them, and re-layouts: 6.04 us -> 13.8 us
  starting transfers between devices: 41.9 us -> 36.6 us
  waiting for transfers between devices: 85.5 us -> 82.3 us
    unnamed x28 -> x38, local copies, waits for them, and re-layouts: 5.81 us -> 13.6 us
    ppermute x12, waiting for transfers between devices: 70.7 us -> 66.6 us  [trade(): lax.ppermute(blocks[k], 'cols', [(i, i ^ k) for i in range(count)])]
    ppermute x8, starting transfers between devices: 26.2 us -> 22.9 us  [pass_on(): return (lax.ppermute(last, axis, ahead), lax.ppermute(first, axis, back))]
  transfers between devices with their start and end apart: 20 -> 20, of which waited for: 12 -> 11; matrix products, arithmetic and copies ran while one was open for 0% -> 0% of each run, Pallas kernels for 33% -> 34%
where the time goes in v3:
time: 210 us
  waiting for transfers between devices  82.3 us (39%)
  Pallas kernels  75.3 us (36%)
  starting transfers between devices  36.6 us (17%)
  local copies, waits for them, and re-layouts  13.8 us (7%)
    ppermute x12, waiting for transfers between devices, trade(): lax.ppermute(blocks[k], 'cols', [(i, i ^ k) for i in range(count)])  66.6 us
    pallas_call x2, Pallas kernels, transport(): pl.pallas_call(kernel, name=f'transport_{layer}', grid=(1,), out_shape=[j...  55.3 us
    ppermute x8, starting transfers between devices, pass_on(): return (lax.ppermute(last, axis, ahead), lax.ppermute(first, axis, back))  22.9 us
    ppermute x8, waiting for transfers between devices, pass_on(): return (lax.ppermute(last, axis, ahead), lax.ppermute(first, axis, back))  15.7 us
    ppermute x12, starting transfers between devices, trade(): lax.ppermute(blocks[k], 'cols', [(i, i ^ k) for i in range(count)])  13.8 us
    unnamed x38, local copies, waits for them, and re-layouts  13.6 us
    pallas_call x3, Pallas kernels, unpack_phase(): pl.pallas_call(kernel, name=f'unpack_phase_{layer}', out_shape=jax.ShapeD...  6.74 us
    pallas_call x1, Pallas kernels, pack_columns(): pl.pallas_call(kernel, name='pack_columns', grid=(1,), out_shape=[shape,...  4.5 us
  transfers between devices with their start and end apart: 20, of which 11 were waited for; matrix products, arithmetic and copies ran while one was open for 0% of the time, Pallas kernels for 34%

profile of v3, /device:TPU:9, one launch (start us, length us, event | category | flops | bytes accessed | tf_op | source)
XLA Modules:
  0.0 209.6 jit_solution(10527056775601857691)
XLA Ops:
  0.6 0.7 convert_element_type.4
  1.6 2.2 %copy-done = bf16[2,64,16384]{2,1,0:T(8,128)(2,1)S(1)} copy-done((bf16[2,64,16384]{2,1,0:T(8,128)(2,1)S(1)}, bf16[2,64,16384]{2,1,0:T(8,128)(2,1)}, u32[]{:S(2)}) %copy-start) | copy-done | bytes 4194328
  3.7 2.5 %pack_first.1 = (bf16[64,4224]{1,0:T(8,128)(2,1)S(1)}, bf16[64,4224]{1,0:T(8,128)(2,1)S(1)}, bf16[64,4224]{1,0:T(8,128)(2,1)S(1)}, f32[2,16,4096]{2,1,0:T(8,128)S(1)}, f32[2,16,4096]{2,1,0:T(8,128)S(1)}) custom-call(s32[5]{0:T(128)S(1)} %stack.39.where_ref, bf16[2,64,16384]{2,1,0:T(8,128)(2,1)S(1)} %copy-done, f32[2,256,4096]{2,1,0:T(8,128)} %refs_0_.8, ...), custom_call_target="tpu_custom_call" | custom-call | bytes 1048576 | tf_op jit(solution)/shard_map/pack_first/pallas_call | solution.py:133
  6.2 3.7 %collective-permute-start = (f32[2,16,4096]{2,1,0:T(8,128)S(1)}, f32[2,16,4096]{2,1,0:T(8,128)S(1)}, u32[]{:S(2)}, u32[]{:S(2)}) collective-permute-start(f32[2,16,4096]{2,1,0:T(8,128)S(1)} %get-tuple-element.47), channel_id=1, source_target_pairs={{0,4},{4,8},{8,12},{12,16},{16,20},{20,24},{24,28},{1,5},{5,9},{9,... | collective-permute-start | bytes 1572872 | tf_op jit(solution)/shard_map/ppermute | solution.py:566
  9.9 1.9 collective-permute-start.1
  12.1 2.3 %collective-permute-start.3 = (bf16[64,4224]{1,0:T(8,128)(2,1)S(1)}, bf16[64,4224]{1,0:T(8,128)(2,1)S(1)}, u32[]{:S(2)}, u32[]{:S(2)}) collective-permute-start(bf16[64,4224]{1,0:T(8,128)(2,1)S(1)} %get-tuple-element.53), channel_id=1, source_target_pairs={{0,2},{1,3},{2,0},{3,1},{4,6},{5,7},{6,4},{7,5},{8,10},{9,11},{10,... | collective-permute-start | bytes 1622024 | tf_op jit(solution)/shard_map/ppermute | solution.py:560
  14.6 1.4 collective-permute-done.refs_8_
  16.0 7.3 %collective-permute-done.1.refs_9_ = f32[2,16,4096]{2,1,0:T(8,128)S(1)} collective-permute-done((f32[2,16,4096]{2,1,0:T(8,128)S(1)}, f32[2,16,4096]{2,1,0:T(8,128)S(1)}, u32[]{:S(2)}, u32[]{:S(2)}) %collective-permute-start.1) | collective-permute-done | bytes 524320 | tf_op jit(solution)/shard_map/ppermute | solution.py:566
  23.4 3.4 %copy-done.2 = f32[2,256,4096]{2,1,0:T(8,128)S(1)} copy-done((f32[2,256,4096]{2,1,0:T(8,128)S(1)}, f32[2,256,4096]{2,1,0:T(8,128)}, u32[]{:S(2)}) %copy-start.2) | copy-done | bytes 8388632
  26.8 4.5 %pack_columns.1 = (f32[272,128]{1,0:T(8,128)S(1)}, f32[272,128]{1,0:T(8,128)S(1)}) custom-call(f32[2,256,4096]{2,1,0:T(8,128)S(1)} %copy-done.2, f32[2,256,4096]{2,1,0:T(8,128)} %refs_1_.8, f32[2,256,4096]{2,1,0:T(8,128)} %refs_2_.8, f32[2,256,4096]{2,1,0:T(8,128)} %refs_3_.8, f32[2,256,4096]{2,1,0:T(8,128)S(1)} %copy-done.2, f32[2,256,4096]{2,1,0:T(8,128)} %refs_1_.8, ...), custom_call_target="tpu_custom_call" | custom-call | bytes 2097152 | tf_op jit(solution)/shard_map/pack_columns/pallas_call | solution.py:208
  31.3 2.3 %collective-permute-start.6 = (f32[272,128]{1,0:T(8,128)S(1)}, f32[272,128]{1,0:T(8,128)S(1)}, u32[]{:S(2)}, u32[]{:S(2)}) collective-permute-start(f32[272,128]{1,0:T(8,128)S(1)} %get-tuple-element.55), channel_id=1, source_target_pairs={{1,0},{2,1},{3,2},{5,4},{6,5},{7,6},{9,8},{10,9},{11,10},{13,12},{... | collective-permute-start | bytes 417800 | tf_op jit(solution)/shard_map/ppermute | solution.py:566
  33.6 3.0 %collective-permute-start.5 = (f32[272,128]{1,0:T(8,128)S(1)}, f32[272,128]{1,0:T(8,128)S(1)}, u32[]{:S(2)}, u32[]{:S(2)}) collective-permute-start(f32[272,128]{1,0:T(8,128)S(1)} %get-tuple-element.49), channel_id=1, source_target_pairs={{0,1},{1,2},{2,3},{4,5},{5,6},{6,7},{8,9},{9,10},{10,11},{12,13},{... | collective-permute-start | bytes 417800 | tf_op jit(solution)/shard_map/ppermute | solution.py:566
  36.7 1.8 pack_light_5.1
  38.5 0.8 copy-done.9
  39.3 0.8 copy-done.11
  40.1 9.6 %collective-permute-done.3.refs_2_.refs_6_ = bf16[64,4224]{1,0:T(8,128)(2,1)S(1)} collective-permute-done((bf16[64,4224]{1,0:T(8,128)(2,1)S(1)}, bf16[64,4224]{1,0:T(8,128)(2,1)S(1)}, u32[]{:S(2)}, u32[]{:S(2)}) %collective-permute-start.3) | collective-permute-done | bytes 540704 | tf_op jit(solution)/shard_map/ppermute | solution.py:560
  49.7 12.4 %collective-permute-done.4.refs_3_.refs_7_ = bf16[64,4224]{1,0:T(8,128)(2,1)S(1)} collective-permute-done((bf16[64,4224]{1,0:T(8,128)(2,1)S(1)}, bf16[64,4224]{1,0:T(8,128)(2,1)S(1)}, u32[]{:S(2)}, u32[]{:S(2)}) %collective-permute-start.4) | collective-permute-done | bytes 540704 | tf_op jit(solution)/shard_map/ppermute | solution.py:560
  62.2 1.6 collective-permute-done.6.refs_13_
  63.8 2.5 %collective-permute-start.10 = (bf16[64,4224]{1,0:T(8,128)(2,1)}, bf16[64,4224]{1,0:T(8,128)(2,1)}, u32[]{:S(2)}, u32[]{:S(2)}) collective-permute-start(bf16[64,4224]{1,0:T(8,128)(2,1)} %get-tuple-element.74), channel_id=1, source_target_pairs={{0,2},{1,3},{2,0},{3,1},{4,6},{5,7},{6,4},{7,5},{8,10},{9,11},{10,... | collective-permute-start | bytes 1622024 | tf_op jit(solution)/shard_map/ppermute | solution.py:560
  66.4 2.2 %edge_light_0.1 = (bf16[8,4224]{1,0:T(8,128)(2,1)}, bf16[8,4224]{1,0:T(8,128)(2,1)}) custom-call(s32[5]{0:T(128)} %copy-done.13, bf16[64,4224]{1,0:T(8,128)(2,1)} %copy-done.9, bf16[64,4224]{1,0:T(8,128)(2,1)} %copy-done.3, bf16[64,4224]{1,0:T(8,128)(2,1)} %copy-done.5, bf16[64,4224]{1,0:T(8,128)(2,1)} %copy-done.7), custom_call_target="tpu_custom_call" | custom-call | bytes 270336 | tf_op jit(solution)/shard_map/edge_light_0/pallas_call | solution.py:239
  68.7 5.7 %collective-permute-start.7 = (bf16[8,4224]{1,0:T(8,128)(2,1)}, bf16[8,4224]{1,0:T(8,128)(2,1)S(1)}, u32[]{:S(2)}, u32[]{:S(2)}) collective-permute-start(bf16[8,4224]{1,0:T(8,128)(2,1)} %get-tuple-element.64), channel_id=1, source_target_pairs={{0,4},{4,8},{8,12},{12,16},{16,20},{20,24},{24,28},{1,5},{5,9},{9,... | collective-permute-start | bytes 202760 | tf_op jit(solution)/shard_map/ppermute | solution.py:566
  74.4 1.9 collective-permute-start.8
  76.3 4.3 %collective-permute-done.8.refs_11_ = bf16[8,4224]{1,0:T(8,128)(2,1)S(1)} collective-permute-done((bf16[8,4224]{1,0:T(8,128)(2,1)}, bf16[8,4224]{1,0:T(8,128)(2,1)S(1)}, u32[]{:S(2)}, u32[]{:S(2)}) %collective-permute-start.8) | collective-permute-done | bytes 67616 | tf_op jit(solution)/shard_map/ppermute | solution.py:566
  80.6 1.0 copy-done.4
  81.7 1.0 copy-done.6
  82.7 1.0 copy-done.8
  83.8 1.0 copy-done.10
  84.8 0.6 copy-done.14
  85.4 27.2 %transport_0.1 = (f32[2,256,4096]{2,1,0:T(8,128)}, s16[64,4096]{1,0:T(8,128)(2,1)S(1)}, s16[64,4096]{1,0:T(8,128)(2,1)S(1)}, s16[64,4096]{1,0:T(8,128)(2,1)}, s16[64,4096]{1,0:T(8,128)(2,1)S(1)}) custom-call(s32[5]{0:T(128)S(1)} %copy-done.14, f32[2,256,4096]{2,1,0:T(8,128)} %refs_0_.8, f32[2,256,4096]{2,1,0:T(8,128)} %refs_1_.8, f32[2,256,4096]{2,1,0:T(8,128)} %refs_2_.8, ...), custom_call_target="tpu_custom_call" | custom-call | bytes 120000000 | tf_op jit(solution)/shard_map/transport_0/pallas_call | solution.py:466
  112.6 0.8 copy-done.16
  113.4 0.8 copy-done.17
  114.2 1.7 collective-permute-start.17
  116.0 2.2 %edge_light_1.1 = (bf16[8,4224]{1,0:T(8,128)(2,1)}, bf16[8,4224]{1,0:T(8,128)(2,1)}) custom-call(s32[5]{0:T(128)} %copy-done.13, bf16[64,4224]{1,0:T(8,128)(2,1)} %copy-done.11, bf16[64,4224]{1,0:T(8,128)(2,1)} %collective-permute-done.9.refs_1_.refs_5_, bf16[64,4224]{1,0:T(8,128)(2,1)} %collective-permute-done.10.refs_2_.refs_6_, ...), custom_call_target="tpu_custom_call" | custom-call | bytes 270336 | tf_op jit(solution)/shard_map/edge_light_1/pallas_call | solution.py:239
  118.2 1.9 collective-permute-start.12
  120.1 2.4 %collective-permute-start.13 = (bf16[8,4224]{1,0:T(8,128)(2,1)}, bf16[8,4224]{1,0:T(8,128)(2,1)S(1)}, u32[]{:S(2)}, u32[]{:S(2)}) collective-permute-start(bf16[8,4224]{1,0:T(8,128)(2,1)} %get-tuple-element.81), channel_id=1, source_target_pairs={{4,0},{8,4},{12,8},{16,12},{20,16},{24,20},{28,24},{5,1},{9,5},{13... | collective-permute-start | bytes 202760 | tf_op jit(solution)/shard_map/ppermute | solution.py:566
  122.5 0.8 collective-permute-start.18
  123.4 2.5 %collective-permute-start.19 = (s16[64,4096]{1,0:T(8,128)(2,1)}, s16[64,4096]{1,0:T(8,128)(2,1)S(1)}, u32[]{:S(2)}, u32[]{:S(2)}) collective-permute-start(s16[64,4096]{1,0:T(8,128)(2,1)} %copy-done.16), channel_id=1, source_target_pairs={{0,1},{1,0},{2,3},{3,2},{4,5},{5,4},{6,7},{7,6},{8,9},{9,8},{10,11... | collective-permute-start | bytes 1572872 | tf_op jit(solution)/shard_map/ppermute | solution.py:560
  125.9 1.1 collective-permute-done.13.refs_11_
  127.0 28.1 %transport_1.1 = (f32[2,256,4096]{2,1,0:T(8,128)}, s16[64,4096]{1,0:T(8,128)(2,1)S(1)}, s16[64,4096]{1,0:T(8,128)(2,1)S(1)}, s16[64,4096]{1,0:T(8,128)(2,1)S(1)}, s16[64,4096]{1,0:T(8,128)(2,1)S(1)}) custom-call(s32[5]{0:T(128)S(1)} %copy-done.15, f32[2,256,4096]{2,1,0:T(8,128)} %refs_0_.8, ...), custom_call_target="tpu_custom_call", output_to_operand_aliasing={{0}: (17, {})} | custom-call | bytes 120000000 | tf_op jit(solution)/shard_map/transport_1/pallas_call | solution.py:466
  155.1 2.0 collective-permute-start.16
  157.1 1.3 collective-permute-start.15
  158.4 4.2 %collective-permute-done.18.refs_2_ = s16[64,4096]{1,0:T(8,128)(2,1)S(1)} collective-permute-done((s16[64,4096]{1,0:T(8,128)(2,1)}, s16[64,4096]{1,0:T(8,128)(2,1)S(1)}, u32[]{:S(2)}, u32[]{:S(2)}) %collective-permute-start.18) | collective-permute-done | bytes 524320 | tf_op jit(solution)/shard_map/ppermute | solution.py:560
  162.6 2.8 %unpack_phase_0.1.refs_2_ = f32[2,64,16384]{2,1,0:T(8,128)} custom-call(s32[5]{0:T(128)S(1)} %copy-done.15, s16[64,4096]{1,0:T(8,128)(2,1)S(1)} %get-tuple-element.87.refs_0_, s16[64,4096]{1,0:T(8,128)(2,1)S(1)} %collective-permute-done.17.refs_1_, s16[64,4096]{1,0:T(8,128)(2,1)S(1)} %collective-permute-done.18.refs_2_, ...), custom_call_target="tpu_custom_call" | custom-call | bytes 6291456 | tf_op jit(solution)/shard_map/unpack_phase_0/pallas_call | solution.py:527
  165.4 10.3 %collective-permute-done.16.refs_1_ = s16[64,4096]{1,0:T(8,128)(2,1)S(1)} collective-permute-done((s16[64,4096]{1,0:T(8,128)(2,1)S(1)}, s16[64,4096]{1,0:T(8,128)(2,1)S(1)}, u32[]{:S(2)}, u32[]{:S(2)}) %collective-permute-start.16) | collective-permute-done | bytes 524320 | tf_op jit(solution)/shard_map/ppermute | solution.py:560
  175.7 2.0 unpack_phase_1.2.refs_2_
  177.7 17.7 %collective-permute-done.14.refs_0_ = s16[64,4096]{1,0:T(8,128)(2,1)S(1)} collective-permute-done((s16[64,4096]{1,0:T(8,128)(2,1)S(1)}, s16[64,4096]{1,0:T(8,128)(2,1)S(1)}, u32[]{:S(2)}, u32[]{:S(2)}) %collective-permute-start.14) | collective-permute-done | bytes 524320 | tf_op jit(solution)/shard_map/ppermute | solution.py:560
  195.4 12.2 %collective-permute-done.15.refs_1_ = s16[64,4096]{1,0:T(8,128)(2,1)S(1)} collective-permute-done((s16[64,4096]{1,0:T(8,128)(2,1)S(1)}, s16[64,4096]{1,0:T(8,128)(2,1)S(1)}, u32[]{:S(2)}, u32[]{:S(2)}) %collective-permute-start.15) | collective-permute-done | bytes 524320 | tf_op jit(solution)/shard_map/ppermute | solution.py:560
  207.6 2.0 unpack_phase_1.3
  (45 shorter events, 0.9 us)
Async XLA Ops:
  1.4 35.2 %copy-start.13 = (s32[5]{0:T(128)}, s32[5]{0:T(128)S(1)}, u32[]{:S(2)}) copy-start(s32[5]{0:T(128)S(1)} %stack.39.where_ref) | copy-start | bytes 64
  1.5 2.2 %copy-start = (bf16[2,64,16384]{2,1,0:T(8,128)(2,1)S(1)}, bf16[2,64,16384]{2,1,0:T(8,128)(2,1)}, u32[]{:S(2)}) copy-start(bf16[2,64,16384]{2,1,0:T(8,128)(2,1)} %refs_14_) | copy-start | bytes 12582916
  3.7 10.8 %copy-start.18 = (s32[2,4096]{1,0:T(2,128)S(1)}, s32[2,4096]{1,0:T(2,128)}, u32[]{:S(2)}) copy-start(s32[2,4096]{1,0:T(2,128)} %param.13) | copy-start | bytes 98308
  6.2 9.8 %collective-permute-start = (f32[2,16,4096]{2,1,0:T(8,128)S(1)}, f32[2,16,4096]{2,1,0:T(8,128)S(1)}, u32[]{:S(2)}, u32[]{:S(2)}) collective-permute-start(f32[2,16,4096]{2,1,0:T(8,128)S(1)} %get-tuple-element.47), channel_id=1, source_target_pairs={{0,4},{4,8},{8,12},{12,16},{16,20},{20,24},{24,28},{1,5},{5,9},{9,... | collective-permute-start | bytes 1572872 | tf_op jit(solution)/shard_map/ppermute | solution.py:566
  9.9 13.4 %collective-permute-start.1 = (f32[2,16,4096]{2,1,0:T(8,128)S(1)}, f32[2,16,4096]{2,1,0:T(8,128)S(1)}, u32[]{:S(2)}, u32[]{:S(2)}) collective-permute-start(f32[2,16,4096]{2,1,0:T(8,128)S(1)} %get-tuple-element.48), channel_id=1, source_target_pairs={{4,0},{8,4},{12,8},{16,12},{20,16},{24,20},{28,24},{5,1},{9,5},{13... | collective-permute-start | bytes 1572872 | tf_op jit(solution)/shard_map/ppermute | solution.py:566
  11.9 28.2 %collective-permute-start.2 = (bf16[64,4224]{1,0:T(8,128)(2,1)S(1)}, bf16[64,4224]{1,0:T(8,128)(2,1)S(1)}, u32[]{:S(2)}, u32[]{:S(2)}) collective-permute-start(bf16[64,4224]{1,0:T(8,128)(2,1)S(1)} %get-tuple-element.52), channel_id=1, source_target_pairs={{0,1},{1,0},{2,3},{3,2},{4,5},{5,4},{6,7},{7,6},{8,9},{9,8},{10,11... | collective-permute-start | bytes 1622024 | tf_op jit(solution)/shard_map/ppermute | solution.py:560
  12.1 37.6 %collective-permute-start.3 = (bf16[64,4224]{1,0:T(8,128)(2,1)S(1)}, bf16[64,4224]{1,0:T(8,128)(2,1)S(1)}, u32[]{:S(2)}, u32[]{:S(2)}) collective-permute-start(bf16[64,4224]{1,0:T(8,128)(2,1)S(1)} %get-tuple-element.53), channel_id=1, source_target_pairs={{0,2},{1,3},{2,0},{3,1},{4,6},{5,7},{6,4},{7,5},{8,10},{9,11},{10,... | collective-permute-start | bytes 1622024 | tf_op jit(solution)/shard_map/ppermute | solution.py:560
  14.4 47.8 %collective-permute-start.4 = (bf16[64,4224]{1,0:T(8,128)(2,1)S(1)}, bf16[64,4224]{1,0:T(8,128)(2,1)S(1)}, u32[]{:S(2)}, u32[]{:S(2)}) collective-permute-start(bf16[64,4224]{1,0:T(8,128)(2,1)S(1)} %get-tuple-element.54), channel_id=1, source_target_pairs={{0,3},{1,2},{2,1},{3,0},{4,7},{5,6},{6,5},{7,4},{8,11},{9,10},{10,... | collective-permute-start | bytes 1622024 | tf_op jit(solution)/shard_map/ppermute | solution.py:560
  23.4 3.4 %copy-start.2 = (f32[2,256,4096]{2,1,0:T(8,128)S(1)}, f32[2,256,4096]{2,1,0:T(8,128)}, u32[]{:S(2)}) copy-start(f32[2,256,4096]{2,1,0:T(8,128)} %refs_0_.8) | copy-start | bytes 25165828
  26.8 9.9 %copy-start.1 = (bf16[2,64,16384]{2,1,0:T(8,128)(2,1)S(1)}, bf16[2,64,16384]{2,1,0:T(8,128)(2,1)}, u32[]{:S(2)}) copy-start(bf16[2,64,16384]{2,1,0:T(8,128)(2,1)} %refs_14_) | copy-start | bytes 12582916
  31.3 32.5 %collective-permute-start.6 = (f32[272,128]{1,0:T(8,128)S(1)}, f32[272,128]{1,0:T(8,128)S(1)}, u32[]{:S(2)}, u32[]{:S(2)}) collective-permute-start(f32[272,128]{1,0:T(8,128)S(1)} %get-tuple-element.55), channel_id=1, source_target_pairs={{1,0},{2,1},{3,2},{5,4},{6,5},{7,6},{9,8},{10,9},{11,10},{13,12},{... | collective-permute-start | bytes 417800 | tf_op jit(solution)/shard_map/ppermute | solution.py:566
  33.6 30.2 %collective-permute-start.5 = (f32[272,128]{1,0:T(8,128)S(1)}, f32[272,128]{1,0:T(8,128)S(1)}, u32[]{:S(2)}, u32[]{:S(2)}) collective-permute-start(f32[272,128]{1,0:T(8,128)S(1)} %get-tuple-element.49), channel_id=1, source_target_pairs={{0,1},{1,2},{2,3},{4,5},{5,6},{6,7},{8,9},{9,10},{10,11},{12,13},{... | collective-permute-start | bytes 417800 | tf_op jit(solution)/shard_map/ppermute | solution.py:566
  38.5 0.8 copy-start.9
  39.3 0.8 copy-start.11
  40.1 26.3 %copy-start.3 = (bf16[64,4224]{1,0:T(8,128)(2,1)}, bf16[64,4224]{1,0:T(8,128)(2,1)S(1)}, u32[]{:S(2)}) copy-start(bf16[64,4224]{1,0:T(8,128)(2,1)S(1)} %collective-permute-done.2.refs_1_.refs_5_) | copy-start | bytes 1622020
  49.7 16.7 %copy-start.5 = (bf16[64,4224]{1,0:T(8,128)(2,1)}, bf16[64,4224]{1,0:T(8,128)(2,1)S(1)}, u32[]{:S(2)}) copy-start(bf16[64,4224]{1,0:T(8,128)(2,1)S(1)} %collective-permute-done.3.refs_2_.refs_6_) | copy-start | bytes 1622020
  62.2 4.3 %copy-start.7 = (bf16[64,4224]{1,0:T(8,128)(2,1)}, bf16[64,4224]{1,0:T(8,128)(2,1)S(1)}, u32[]{:S(2)}) copy-start(bf16[64,4224]{1,0:T(8,128)(2,1)S(1)} %collective-permute-done.4.refs_3_.refs_7_) | copy-start | bytes 1622020
  63.8 50.5 %collective-permute-start.9 = (bf16[64,4224]{1,0:T(8,128)(2,1)}, bf16[64,4224]{1,0:T(8,128)(2,1)}, u32[]{:S(2)}, u32[]{:S(2)}) collective-permute-start(bf16[64,4224]{1,0:T(8,128)(2,1)} %get-tuple-element.73), channel_id=1, source_target_pairs={{0,1},{1,0},{2,3},{3,2},{4,5},{5,4},{6,7},{7,6},{8,9},{9,8},{10,11... | collective-permute-start | bytes 1622024 | tf_op jit(solution)/shard_map/ppermute | solution.py:560
  63.8 50.5 %collective-permute-start.10 = (bf16[64,4224]{1,0:T(8,128)(2,1)}, bf16[64,4224]{1,0:T(8,128)(2,1)}, u32[]{:S(2)}, u32[]{:S(2)}) collective-permute-start(bf16[64,4224]{1,0:T(8,128)(2,1)} %get-tuple-element.74), channel_id=1, source_target_pairs={{0,2},{1,3},{2,0},{3,1},{4,6},{5,7},{6,4},{7,5},{8,10},{9,11},{10,... | collective-permute-start | bytes 1622024 | tf_op jit(solution)/shard_map/ppermute | solution.py:560
  66.3 47.9 %collective-permute-start.11 = (bf16[64,4224]{1,0:T(8,128)(2,1)}, bf16[64,4224]{1,0:T(8,128)(2,1)}, u32[]{:S(2)}, u32[]{:S(2)}) collective-permute-start(bf16[64,4224]{1,0:T(8,128)(2,1)} %get-tuple-element.75), channel_id=1, source_target_pairs={{0,3},{1,2},{2,1},{3,0},{4,7},{5,6},{6,5},{7,4},{8,11},{9,10},{10,... | collective-permute-start | bytes 1622024 | tf_op jit(solution)/shard_map/ppermute | solution.py:560
  68.7 7.6 %collective-permute-start.7 = (bf16[8,4224]{1,0:T(8,128)(2,1)}, bf16[8,4224]{1,0:T(8,128)(2,1)S(1)}, u32[]{:S(2)}, u32[]{:S(2)}) collective-permute-start(bf16[8,4224]{1,0:T(8,128)(2,1)} %get-tuple-element.64), channel_id=1, source_target_pairs={{0,4},{4,8},{8,12},{12,16},{16,20},{20,24},{24,28},{1,5},{5,9},{9,... | collective-permute-start | bytes 202760 | tf_op jit(solution)/shard_map/ppermute | solution.py:566
  74.4 52.6 %copy-start.15 = (s32[5]{0:T(128)S(1)}, s32[5]{0:T(128)}, u32[]{:S(2)}) copy-start(s32[5]{0:T(128)} %copy-done.13) | copy-start | bytes 64
  74.4 6.2 %collective-permute-start.8 = (bf16[8,4224]{1,0:T(8,128)(2,1)}, bf16[8,4224]{1,0:T(8,128)(2,1)S(1)}, u32[]{:S(2)}, u32[]{:S(2)}) collective-permute-start(bf16[8,4224]{1,0:T(8,128)(2,1)} %get-tuple-element.65), channel_id=1, source_target_pairs={{4,0},{8,4},{12,8},{16,12},{20,16},{24,20},{28,24},{5,1},{9,5},{13... | collective-permute-start | bytes 202760 | tf_op jit(solution)/shard_map/ppermute | solution.py:566
  80.6 1.0 copy-start.4
  81.7 1.0 copy-start.6
  82.7 1.0 copy-start.8
  83.7 1.0 copy-start.10
  84.8 0.6 copy-start.14
  85.4 41.6 %copy-start.12 = (bf16[64,4224]{1,0:T(8,128)(2,1)S(1)}, bf16[64,4224]{1,0:T(8,128)(2,1)}, u32[]{:S(2)}) copy-start(bf16[64,4224]{1,0:T(8,128)(2,1)} %copy-done.11) | copy-start | bytes 1622020
  112.6 0.8 copy-start.16
  113.4 0.8 copy-start.17
  114.2 42.9 %collective-permute-start.17 = (s16[64,4096]{1,0:T(8,128)(2,1)}, s16[64,4096]{1,0:T(8,128)(2,1)S(1)}, u32[]{:S(2)}, u32[]{:S(2)}) collective-permute-start(s16[64,4096]{1,0:T(8,128)(2,1)} %get-tuple-element.88), channel_id=1, source_target_pairs={{0,2},{1,3},{2,0},{3,1},{4,6},{5,7},{6,4},{7,5},{8,10},{9,11},{10,... | collective-permute-start | bytes 1572872 | tf_op jit(solution)/shard_map/ppermute | solution.py:560
  118.2 7.7 %collective-permute-start.12 = (bf16[8,4224]{1,0:T(8,128)(2,1)}, bf16[8,4224]{1,0:T(8,128)(2,1)S(1)}, u32[]{:S(2)}, u32[]{:S(2)}) collective-permute-start(bf16[8,4224]{1,0:T(8,128)(2,1)} %get-tuple-element.80), channel_id=1, source_target_pairs={{0,4},{4,8},{8,12},{12,16},{16,20},{20,24},{24,28},{1,5},{5,9},{9,... | collective-permute-start | bytes 202760 | tf_op jit(solution)/shard_map/ppermute | solution.py:566
  120.1 6.9 %collective-permute-start.13 = (bf16[8,4224]{1,0:T(8,128)(2,1)}, bf16[8,4224]{1,0:T(8,128)(2,1)S(1)}, u32[]{:S(2)}, u32[]{:S(2)}) collective-permute-start(bf16[8,4224]{1,0:T(8,128)(2,1)} %get-tuple-element.81), channel_id=1, source_target_pairs={{4,0},{8,4},{12,8},{16,12},{20,16},{24,20},{28,24},{5,1},{9,5},{13... | collective-permute-start | bytes 202760 | tf_op jit(solution)/shard_map/ppermute | solution.py:566
  122.5 40.1 %collective-permute-start.18 = (s16[64,4096]{1,0:T(8,128)(2,1)}, s16[64,4096]{1,0:T(8,128)(2,1)S(1)}, u32[]{:S(2)}, u32[]{:S(2)}) collective-permute-start(s16[64,4096]{1,0:T(8,128)(2,1)} %copy-done.17), channel_id=1, source_target_pairs={{0,3},{1,2},{2,1},{3,0},{4,7},{5,6},{6,5},{7,4},{8,11},{9,10},{10,... | collective-permute-start | bytes 1572872 | tf_op jit(solution)/shard_map/ppermute | solution.py:560
  123.4 39.3 %collective-permute-start.19 = (s16[64,4096]{1,0:T(8,128)(2,1)}, s16[64,4096]{1,0:T(8,128)(2,1)S(1)}, u32[]{:S(2)}, u32[]{:S(2)}) collective-permute-start(s16[64,4096]{1,0:T(8,128)(2,1)} %copy-done.16), channel_id=1, source_target_pairs={{0,1},{1,0},{2,3},{3,2},{4,5},{5,4},{6,7},{7,6},{8,9},{9,8},{10,11... | collective-permute-start | bytes 1572872 | tf_op jit(solution)/shard_map/ppermute | solution.py:560
  155.1 20.6 %collective-permute-start.16 = (s16[64,4096]{1,0:T(8,128)(2,1)S(1)}, s16[64,4096]{1,0:T(8,128)(2,1)S(1)}, u32[]{:S(2)}, u32[]{:S(2)}) collective-permute-start(s16[64,4096]{1,0:T(8,128)(2,1)S(1)} %get-tuple-element.86), channel_id=1, source_target_pairs={{0,1},{1,0},{2,3},{3,2},{4,5},{5,4},{6,7},{7,6},{8,9},{9,8},{10,11... | collective-permute-start | bytes 1572872 | tf_op jit(solution)/shard_map/ppermute | solution.py:560
  157.1 38.3 %collective-permute-start.14 = (s16[64,4096]{1,0:T(8,128)(2,1)S(1)}, s16[64,4096]{1,0:T(8,128)(2,1)S(1)}, u32[]{:S(2)}, u32[]{:S(2)}) collective-permute-start(s16[64,4096]{1,0:T(8,128)(2,1)S(1)} %get-tuple-element.83), channel_id=1, source_target_pairs={{0,2},{1,3},{2,0},{3,1},{4,6},{5,7},{6,4},{7,5},{8,10},{9,11},{10,... | collective-permute-start | bytes 1572872 | tf_op jit(solution)/shard_map/ppermute | solution.py:560
  157.1 50.5 %collective-permute-start.15 = (s16[64,4096]{1,0:T(8,128)(2,1)S(1)}, s16[64,4096]{1,0:T(8,128)(2,1)S(1)}, u32[]{:S(2)}, u32[]{:S(2)}) collective-permute-start(s16[64,4096]{1,0:T(8,128)(2,1)S(1)} %get-tuple-element.84), channel_id=1, source_target_pairs={{0,3},{1,2},{2,1},{3,0},{4,7},{5,6},{6,5},{7,4},{8,11},{9,10},{10,... | collective-permute-start | bytes 1572872 | tf_op jit(solution)/shard_map/ppermute | solution.py:560

commit v4 on v3

--- a/solution.py
+++ b/solution.py
@@ -12,7 +12,7 @@
 HEAT_RATE = 0.25
 LANES = 128
 HALO = 8
-PITCH = 12
+PITCH = 4
 LEVELS = 32767.0
 BOUND = 13.5
 LIMIT = 44 * 1024 * 1024
@@ -149,10 +149,17 @@
     return out[:pieces], out[pieces], out[pieces + 1]
 
 
+def folds(layers, count, rows):
+    lanes = PITCH * layers * (count + 1)
+    groups = LANES // lanes
+    return lanes, -(-(rows // HALO + 2) // groups)
+
+
 def pack_columns(fields, low, high, heading):
     layers, rows, width = fields[0].shape
     tiles = width // LANES
     count = len(fields)
+    lanes_each, deep = folds(layers, count, rows)
 
     def kernel(*refs):
         first, last = refs[:count], refs[count : 2 * count]
@@ -173,28 +180,20 @@
                 return rim[int(start == "high"), n, edge, layer]
             return (first, last)[edge][n][layer, pl.ds(start, HALO), :]
 
-        def gather(start, row):
-            for edge, out in ((1, east), (0, west)):
+        for edge, out in ((1, east), (0, west)):
+            for row in range(deep):
                 packed = None
-                for layer in range(layers):
-                    for n in range(count + 1):
-                        place = layer * (count + 1) + n
-                        shift = (PITCH * place + 4 * edge) % LANES
-                        moved = tile(n, layer, start, edge)
-                        if shift:
-                            moved = pltpu.roll(moved, shift, 1)
-                        packed = moved if packed is None else jnp.where(lane >= PITCH * place, moved, packed)
-                out[pl.ds(row, HALO), :] = packed
-
-        gather("low", 0)
-        gather("high", rows + HALO)
-
-        def loop(i, carry):
-            start = pl.multiple_of(i * HALO, HALO)
-            gather(start, pl.multiple_of(start + HALO, HALO))
-            return carry
-
-        lax.fori_loop(0, rows // HALO, loop, 0)
+                for b in range(row, rows // HALO + 2, deep):
+                    start = "low" if b == 0 else "high" if b == rows // HALO + 1 else (b - 1) * HALO
+                    for layer in range(layers):
+                        for n in range(count + 1):
+                            place = (b // deep) * lanes_each + PITCH * (layer * (count + 1) + n)
+                            moved = tile(n, layer, start, edge)
+                            shift = (place + PITCH * edge) % LANES
+                            if shift:
+                                moved = pltpu.roll(moved, shift, 1)
+                            packed = moved if packed is None else jnp.where(lane >= place, moved, packed)
+                out[row * HALO : (row + 1) * HALO, :] = packed
 
     def block(column):
         return pl.BlockSpec((layers, rows, LANES), lambda i: (0, 0, column))
@@ -203,8 +202,8 @@
         return pl.BlockSpec((layers, HALO, LANES), lambda i: (0, 0, column))
 
     whole = pl.BlockSpec(low.shape, lambda i: (0, 0, 0))
-    packed = pl.BlockSpec((rows + 2 * HALO, LANES), lambda i: (0, 0))
-    shape = jax.ShapeDtypeStruct((rows + 2 * HALO, LANES), jnp.float32)
+    packed = pl.BlockSpec((deep * HALO, LANES), lambda i: (0, 0))
+    shape = jax.ShapeDtypeStruct((deep * HALO, LANES), jnp.float32)
     return pl.pallas_call(
         kernel,
         name="pack_columns",
@@ -253,6 +252,7 @@
     tiles = width // LANES
     blocks = rows // HALO + 2
     places = spans(4)
+    lanes_each, deep = folds(layers, 4, rows)
     given = end is not None
 
     def kernel(where_ref, *refs):
@@ -317,17 +317,19 @@
                 stores[n][j + 1, base + HALO - size : base + HALO] = low_ref[0, first : first + size, lanes]
                 stores[n][j + 1, base + rows + HALO : base + rows + HALO + size] = high_ref[0, first : first + size, lanes]
         for n in range(5):
-            place = PITCH * (layer * 5 + n)
-            for source, j, shift in ((west_ref, 0, LANES - 4 - place), (east_ref, tiles + 1, -place % LANES)):
+            for source, j, edge in ((west_ref, 0, LANES - PITCH), (east_ref, tiles + 1, 0)):
                 for i in range(blocks if n < 4 else 1):
-                    moved = source[i * HALO : (i + 1) * HALO, :]
-                    if shift:
-                        moved = pltpu.roll(moved, shift, 1)
+                    place = (i // deep) * lanes_each + PITCH * (layer * 5 + n)
+                    start = i % deep * HALO
+                    moved = source[start : start + HALO, :]
+                    if (edge - place) % LANES:
+                        moved = pltpu.roll(moved, (edge - place) % LANES, 1)
                     if n == 4:
                         column_sign[j] = moved
                     else:
                         row = i * HALO + (HALO if n == 0 else 0)
                         stores[n][j, row : row + HALO] = moved
+
         def warm(j, column):
             heat[j, :HALO] = HEAT_RATE * heat[j, :HALO] * light_low_ref[:, pl.ds(column, LANES)].astype(jnp.float32)
             for k in range(count):
@@ -602,7 +604,7 @@
         received[0] = codes[0]
         arriving.append(received)
     for layer in range(layers):
-        groups = [[0] + order] if layer < layers - 1 else [[0, order[-1]], order[:-1]]
+        groups = [[0] + order] if layer < layers - 1 else [[0, order[-1]]] + [[k] for k in order[:-1]]
         for parts in groups:
             slabs = unpack_phase(where, layer, parts, [arriving[layer][k] for k in parts], shape, slabs)
     return slabs, end

time: 210 us -> 208 us (level)
    pallas_call x1, Pallas kernels: 4.5 us -> 2.3 us  [pack_columns(): pl.pallas_call(kernel, name='pack_columns', grid=(1,), out_shape=[shape,...]
    pallas_call x3 -> x4, Pallas kernels: 6.74 us -> 8.48 us  [unpack_phase(): pl.pallas_call(kernel, name=f'unpack_phase_{layer}', out_shape=jax.ShapeD...]
    unnamed x38 -> x42, local copies, waits for them, and re-layouts: 13.6 us -> 15 us
where the time goes in v4:
time: 208 us; the launch traced here: 207 us
  waiting for transfers between devices  80.2 us (39%)
  Pallas kernels  74.8 us (36%)
  starting transfers between devices  35.7 us (17%)
  local copies, waits for them, and re-layouts  15.2 us (7%)
    ppermute x12, waiting for transfers between devices, trade(): lax.ppermute(blocks[k], 'cols', [(i, i ^ k) for i in range(count)])  64.9 us
    pallas_call x2, Pallas kernels, transport(): pl.pallas_call(kernel, name=f'transport_{layer}', grid=(1,), out_shape=[j...  55.3 us
    ppermute x8, starting transfers between devices, pass_on(): return (lax.ppermute(last, axis, ahead), lax.ppermute(first, axis, back))  23 us
    ppermute x8, waiting for transfers between devices, pass_on(): return (lax.ppermute(last, axis, ahead), lax.ppermute(first, axis, back))  15.3 us
    unnamed x42, local copies, waits for them, and re-layouts  15 us
    ppermute x12, starting transfers between devices, trade(): lax.ppermute(blocks[k], 'cols', [(i, i ^ k) for i in range(count)])  12.7 us
    pallas_call x4, Pallas kernels, unpack_phase(): pl.pallas_call(kernel, name=f'unpack_phase_{layer}', out_shape=jax.ShapeD...  8.48 us
    pallas_call x2, Pallas kernels, edge_light(): pl.pallas_call(kernel, name=f'edge_light_{layer}', out_shape=[edge, edge]...  4.47 us
  transfers between devices with their start and end apart: 20, of which 11 were waited for; matrix products, arithmetic and copies ran while one was open for 0% of the time, Pallas kernels for 34%

profile of v4, /device:TPU:9, one launch (start us, length us, event | category | flops | bytes accessed | tf_op | source)
XLA Modules:
  0.0 207.4 jit_solution(12080571831325731116)
XLA Ops:
  0.6 0.7 convert_element_type.4
  1.6 2.2 %copy-done = bf16[2,64,16384]{2,1,0:T(8,128)(2,1)S(1)} copy-done((bf16[2,64,16384]{2,1,0:T(8,128)(2,1)S(1)}, bf16[2,64,16384]{2,1,0:T(8,128)(2,1)}, u32[]{:S(2)}) %copy-start) | copy-done | bytes 4194328
  3.7 2.5 %pack_first.1 = (bf16[64,4224]{1,0:T(8,128)(2,1)S(1)}, bf16[64,4224]{1,0:T(8,128)(2,1)S(1)}, bf16[64,4224]{1,0:T(8,128)(2,1)S(1)}, f32[2,16,4096]{2,1,0:T(8,128)S(1)}, f32[2,16,4096]{2,1,0:T(8,128)S(1)}) custom-call(s32[5]{0:T(128)S(1)} %stack.39.where_ref, bf16[2,64,16384]{2,1,0:T(8,128)(2,1)S(1)} %copy-done, f32[2,256,4096]{2,1,0:T(8,128)} %refs_0_.8, ...), custom_call_target="tpu_custom_call" | custom-call | bytes 1048576 | tf_op jit(solution)/shard_map/pack_first/pallas_call | solution.py:133
  6.2 3.7 %collective-permute-start = (f32[2,16,4096]{2,1,0:T(8,128)S(1)}, f32[2,16,4096]{2,1,0:T(8,128)S(1)}, u32[]{:S(2)}, u32[]{:S(2)}) collective-permute-start(f32[2,16,4096]{2,1,0:T(8,128)S(1)} %get-tuple-element.47), channel_id=1, source_target_pairs={{0,4},{4,8},{8,12},{12,16},{16,20},{20,24},{24,28},{1,5},{5,9},{9,... | collective-permute-start | bytes 1572872 | tf_op jit(solution)/shard_map/ppermute | solution.py:568
  9.9 1.9 collective-permute-start.1
  12.1 2.3 %collective-permute-start.3 = (bf16[64,4224]{1,0:T(8,128)(2,1)S(1)}, bf16[64,4224]{1,0:T(8,128)(2,1)S(1)}, u32[]{:S(2)}, u32[]{:S(2)}) collective-permute-start(bf16[64,4224]{1,0:T(8,128)(2,1)S(1)} %get-tuple-element.53), channel_id=1, source_target_pairs={{0,2},{1,3},{2,0},{3,1},{4,6},{5,7},{6,4},{7,5},{8,10},{9,11},{10,... | collective-permute-start | bytes 1622024 | tf_op jit(solution)/shard_map/ppermute | solution.py:562
  14.6 1.4 collective-permute-done.refs_8_
  16.0 7.3 %collective-permute-done.1.refs_9_ = f32[2,16,4096]{2,1,0:T(8,128)S(1)} collective-permute-done((f32[2,16,4096]{2,1,0:T(8,128)S(1)}, f32[2,16,4096]{2,1,0:T(8,128)S(1)}, u32[]{:S(2)}, u32[]{:S(2)}) %collective-permute-start.1) | collective-permute-done | bytes 524320 | tf_op jit(solution)/shard_map/ppermute | solution.py:568
  23.4 3.4 %copy-done.2 = f32[2,256,4096]{2,1,0:T(8,128)S(1)} copy-done((f32[2,256,4096]{2,1,0:T(8,128)S(1)}, f32[2,256,4096]{2,1,0:T(8,128)}, u32[]{:S(2)}) %copy-start.2) | copy-done | bytes 8388632
  26.8 2.3 %pack_columns.1 = (f32[96,128]{1,0:T(8,128)S(1)}, f32[96,128]{1,0:T(8,128)S(1)}) custom-call(f32[2,256,4096]{2,1,0:T(8,128)S(1)} %copy-done.2, f32[2,256,4096]{2,1,0:T(8,128)} %refs_1_.8, f32[2,256,4096]{2,1,0:T(8,128)} %refs_2_.8, f32[2,256,4096]{2,1,0:T(8,128)} %refs_3_.8, f32[2,256,4096]{2,1,0:T(8,128)S(1)} %copy-done.2, f32[2,256,4096]{2,1,0:T(8,128)} %refs_1_.8, ...), custom_call_target="tpu_custom_call" | custom-call | bytes 2097152 | tf_op jit(solution)/shard_map/pack_columns/pallas_call | solution.py:207
  29.1 2.3 %collective-permute-start.6 = (f32[96,128]{1,0:T(8,128)S(1)}, f32[96,128]{1,0:T(8,128)S(1)}, u32[]{:S(2)}, u32[]{:S(2)}) collective-permute-start(f32[96,128]{1,0:T(8,128)S(1)} %get-tuple-element.55), channel_id=1, source_target_pairs={{1,0},{2,1},{3,2},{5,4},{6,5},{7,6},{9,8},{10,9},{11,10},{13,12},{... | collective-permute-start | bytes 147464 | tf_op jit(solution)/shard_map/ppermute | solution.py:568
  31.4 3.0 %collective-permute-start.5 = (f32[96,128]{1,0:T(8,128)S(1)}, f32[96,128]{1,0:T(8,128)S(1)}, u32[]{:S(2)}, u32[]{:S(2)}) collective-permute-start(f32[96,128]{1,0:T(8,128)S(1)} %get-tuple-element.49), channel_id=1, source_target_pairs={{0,1},{1,2},{2,3},{4,5},{5,6},{6,7},{8,9},{9,10},{10,11},{12,13},{... | collective-permute-start | bytes 147464 | tf_op jit(solution)/shard_map/ppermute | solution.py:568
  34.5 1.8 pack_light_5.1
  36.2 0.8 copy-done.3
  37.0 0.8 copy-done.13
  37.8 11.8 %collective-permute-done.3.refs_2_.refs_6_ = bf16[64,4224]{1,0:T(8,128)(2,1)S(1)} collective-permute-done((bf16[64,4224]{1,0:T(8,128)(2,1)S(1)}, bf16[64,4224]{1,0:T(8,128)(2,1)S(1)}, u32[]{:S(2)}, u32[]{:S(2)}) %collective-permute-start.3) | collective-permute-done | bytes 540704 | tf_op jit(solution)/shard_map/ppermute | solution.py:562
  49.7 11.6 %collective-permute-done.4.refs_3_.refs_7_ = bf16[64,4224]{1,0:T(8,128)(2,1)S(1)} collective-permute-done((bf16[64,4224]{1,0:T(8,128)(2,1)S(1)}, bf16[64,4224]{1,0:T(8,128)(2,1)S(1)}, u32[]{:S(2)}, u32[]{:S(2)}) %collective-permute-start.4) | collective-permute-done | bytes 540704 | tf_op jit(solution)/shard_map/ppermute | solution.py:562
  62.1 2.5 %collective-permute-start.10 = (bf16[64,4224]{1,0:T(8,128)(2,1)}, bf16[64,4224]{1,0:T(8,128)(2,1)}, u32[]{:S(2)}, u32[]{:S(2)}) collective-permute-start(bf16[64,4224]{1,0:T(8,128)(2,1)} %get-tuple-element.74), channel_id=1, source_target_pairs={{0,2},{1,3},{2,0},{3,1},{4,6},{5,7},{6,4},{7,5},{8,10},{9,11},{10,... | collective-permute-start | bytes 1622024 | tf_op jit(solution)/shard_map/ppermute | solution.py:562
  64.8 2.2 %edge_light_0.1 = (bf16[8,4224]{1,0:T(8,128)(2,1)}, bf16[8,4224]{1,0:T(8,128)(2,1)}) custom-call(s32[5]{0:T(128)} %copy-done.15, bf16[64,4224]{1,0:T(8,128)(2,1)} %copy-done.13, bf16[64,4224]{1,0:T(8,128)(2,1)} %copy-done.7, bf16[64,4224]{1,0:T(8,128)(2,1)} %copy-done.9, bf16[64,4224]{1,0:T(8,128)(2,1)} %copy-done.11), custom_call_target="tpu_custom_call" | custom-call | bytes 270336 | tf_op jit(solution)/shard_map/edge_light_0/pallas_call | solution.py:238
  67.0 5.6 %collective-permute-start.7 = (bf16[8,4224]{1,0:T(8,128)(2,1)}, bf16[8,4224]{1,0:T(8,128)(2,1)S(1)}, u32[]{:S(2)}, u32[]{:S(2)}) collective-permute-start(bf16[8,4224]{1,0:T(8,128)(2,1)} %get-tuple-element.64), channel_id=1, source_target_pairs={{0,4},{4,8},{8,12},{12,16},{16,20},{20,24},{24,28},{1,5},{5,9},{9,... | collective-permute-start | bytes 202760 | tf_op jit(solution)/shard_map/ppermute | solution.py:568
  72.7 2.1 collective-permute-start.8
  74.8 4.3 %collective-permute-done.8.refs_11_ = bf16[8,4224]{1,0:T(8,128)(2,1)S(1)} collective-permute-done((bf16[8,4224]{1,0:T(8,128)(2,1)}, bf16[8,4224]{1,0:T(8,128)(2,1)S(1)}, u32[]{:S(2)}, u32[]{:S(2)}) %collective-permute-start.8) | collective-permute-done | bytes 67616 | tf_op jit(solution)/shard_map/ppermute | solution.py:568
  79.0 1.0 copy-done.8
  80.1 1.0 copy-done.10
  81.1 1.0 copy-done.12
  82.2 1.0 copy-done.14
  83.2 0.7 copy-done.16
  83.9 27.3 %transport_0.1 = (f32[2,256,4096]{2,1,0:T(8,128)}, s16[64,4096]{1,0:T(8,128)(2,1)S(1)}, s16[64,4096]{1,0:T(8,128)(2,1)S(1)}, s16[64,4096]{1,0:T(8,128)(2,1)}, s16[64,4096]{1,0:T(8,128)(2,1)S(1)}) custom-call(s32[5]{0:T(128)S(1)} %copy-done.16, f32[2,256,4096]{2,1,0:T(8,128)} %refs_0_.8, f32[2,256,4096]{2,1,0:T(8,128)} %refs_1_.8, f32[2,256,4096]{2,1,0:T(8,128)} %refs_2_.8, ...), custom_call_target="tpu_custom_call" | custom-call | bytes 120000000 | tf_op jit(solution)/shard_map/transport_0/pallas_call | solution.py:468
  111.2 0.8 copy-done.18
  112.0 0.8 copy-done.19
  112.8 1.7 collective-permute-start.17
  114.5 2.2 %edge_light_1.1 = (bf16[8,4224]{1,0:T(8,128)(2,1)}, bf16[8,4224]{1,0:T(8,128)(2,1)}) custom-call(s32[5]{0:T(128)} %copy-done.15, bf16[64,4224]{1,0:T(8,128)(2,1)} %copy-done.3, bf16[64,4224]{1,0:T(8,128)(2,1)} %copy-done.5, bf16[64,4224]{1,0:T(8,128)(2,1)} %collective-permute-done.10.refs_2_.refs_6_, bf16[64,4224]{1,0:T(8,128)(2,1)} %collective-permute-done.11.refs_3_.refs_7_), custom_call_target="tpu_custom_call" | custom-call | bytes 270336 | tf_op jit(solution)/shard_map/edge_light_1/pallas_call | solution.py:238
  116.8 1.9 collective-permute-start.12
  118.7 2.4 %collective-permute-start.13 = (bf16[8,4224]{1,0:T(8,128)(2,1)}, bf16[8,4224]{1,0:T(8,128)(2,1)S(1)}, u32[]{:S(2)}, u32[]{:S(2)}) collective-permute-start(bf16[8,4224]{1,0:T(8,128)(2,1)} %get-tuple-element.81), channel_id=1, source_target_pairs={{4,0},{8,4},{12,8},{16,12},{20,16},{24,20},{28,24},{5,1},{9,5},{13... | collective-permute-start | bytes 202760 | tf_op jit(solution)/shard_map/ppermute | solution.py:568
  121.5 2.4 %collective-permute-start.19 = (s16[64,4096]{1,0:T(8,128)(2,1)}, s16[64,4096]{1,0:T(8,128)(2,1)S(1)}, u32[]{:S(2)}, u32[]{:S(2)}) collective-permute-start(s16[64,4096]{1,0:T(8,128)(2,1)} %copy-done.18), channel_id=1, source_target_pairs={{0,1},{1,0},{2,3},{3,2},{4,5},{5,4},{6,7},{7,6},{8,9},{9,8},{10,11... | collective-permute-start | bytes 1572872 | tf_op jit(solution)/shard_map/ppermute | solution.py:562
  123.9 1.7 collective-permute-done.13.refs_11_
  125.7 1.0 copy-done.6
  126.7 28.0 %transport_1.1 = (f32[2,256,4096]{2,1,0:T(8,128)}, s16[64,4096]{1,0:T(8,128)(2,1)S(1)}, s16[64,4096]{1,0:T(8,128)(2,1)S(1)}, s16[64,4096]{1,0:T(8,128)(2,1)S(1)}, s16[64,4096]{1,0:T(8,128)(2,1)S(1)}) custom-call(s32[5]{0:T(128)S(1)} %copy-done.17, f32[2,256,4096]{2,1,0:T(8,128)} %refs_0_.8, ...), custom_call_target="tpu_custom_call", output_to_operand_aliasing={{0}: (17, {})} | custom-call | bytes 120000000 | tf_op jit(solution)/shard_map/transport_1/pallas_call | solution.py:468
  154.7 1.5 collective-permute-start.16
  156.3 1.2 collective-permute-start.14
  157.5 3.8 %collective-permute-done.18.refs_2_ = s16[64,4096]{1,0:T(8,128)(2,1)S(1)} collective-permute-done((s16[64,4096]{1,0:T(8,128)(2,1)}, s16[64,4096]{1,0:T(8,128)(2,1)S(1)}, u32[]{:S(2)}, u32[]{:S(2)}) %collective-permute-start.18) | collective-permute-done | bytes 524320 | tf_op jit(solution)/shard_map/ppermute | solution.py:562
  161.2 3.3 %unpack_phase_0.1.refs_2_ = f32[2,64,16384]{2,1,0:T(8,128)} custom-call(s32[5]{0:T(128)S(1)} %copy-done.17, s16[64,4096]{1,0:T(8,128)(2,1)S(1)} %get-tuple-element.87.refs_0_, s16[64,4096]{1,0:T(8,128)(2,1)} %collective-permute-done.17.refs_1_, s16[64,4096]{1,0:T(8,128)(2,1)S(1)} %collective-permute-done.18.refs_2_, ...), custom_call_target="tpu_custom_call" | custom-call | bytes 6291456 | tf_op jit(solution)/shard_map/unpack_phase_0/pallas_call | solution.py:529
  164.5 10.7 %collective-permute-done.16.refs_1_ = s16[64,4096]{1,0:T(8,128)(2,1)S(1)} collective-permute-done((s16[64,4096]{1,0:T(8,128)(2,1)S(1)}, s16[64,4096]{1,0:T(8,128)(2,1)S(1)}, u32[]{:S(2)}, u32[]{:S(2)}) %collective-permute-start.16) | collective-permute-done | bytes 524320 | tf_op jit(solution)/shard_map/ppermute | solution.py:562
  175.2 2.0 unpack_phase_1.3.refs_1_
  177.2 16.8 %collective-permute-done.15.refs_0_ = s16[64,4096]{1,0:T(8,128)(2,1)S(1)} collective-permute-done((s16[64,4096]{1,0:T(8,128)(2,1)S(1)}, s16[64,4096]{1,0:T(8,128)(2,1)S(1)}, u32[]{:S(2)}, u32[]{:S(2)}) %collective-permute-start.15) | collective-permute-done | bytes 524320 | tf_op jit(solution)/shard_map/ppermute | solution.py:562
  194.0 1.6 unpack_phase_1.4.refs_1_
  195.6 10.2 %collective-permute-done.14.refs_0_ = s16[64,4096]{1,0:T(8,128)(2,1)S(1)} collective-permute-done((s16[64,4096]{1,0:T(8,128)(2,1)S(1)}, s16[64,4096]{1,0:T(8,128)(2,1)S(1)}, u32[]{:S(2)}, u32[]{:S(2)}) %collective-permute-start.14) | collective-permute-done | bytes 524320 | tf_op jit(solution)/shard_map/ppermute | solution.py:562
  205.8 1.6 unpack_phase_1.5
  (50 shorter events, 2.2 us)
Async XLA Ops:
  1.4 33.0 %copy-start.15 = (s32[5]{0:T(128)}, s32[5]{0:T(128)S(1)}, u32[]{:S(2)}) copy-start(s32[5]{0:T(128)S(1)} %stack.39.where_ref) | copy-start | bytes 64
  1.5 2.2 %copy-start = (bf16[2,64,16384]{2,1,0:T(8,128)(2,1)S(1)}, bf16[2,64,16384]{2,1,0:T(8,128)(2,1)}, u32[]{:S(2)}) copy-start(bf16[2,64,16384]{2,1,0:T(8,128)(2,1)} %refs_14_) | copy-start | bytes 12582916
  3.7 10.8 %copy-start.20 = (s32[2,4096]{1,0:T(2,128)S(1)}, s32[2,4096]{1,0:T(2,128)}, u32[]{:S(2)}) copy-start(s32[2,4096]{1,0:T(2,128)} %param.13) | copy-start | bytes 98308
  6.2 9.8 %collective-permute-start = (f32[2,16,4096]{2,1,0:T(8,128)S(1)}, f32[2,16,4096]{2,1,0:T(8,128)S(1)}, u32[]{:S(2)}, u32[]{:S(2)}) collective-permute-start(f32[2,16,4096]{2,1,0:T(8,128)S(1)} %get-tuple-element.47), channel_id=1, source_target_pairs={{0,4},{4,8},{8,12},{12,16},{16,20},{20,24},{24,28},{1,5},{5,9},{9,... | collective-permute-start | bytes 1572872 | tf_op jit(solution)/shard_map/ppermute | solution.py:568
  9.9 13.4 %collective-permute-start.1 = (f32[2,16,4096]{2,1,0:T(8,128)S(1)}, f32[2,16,4096]{2,1,0:T(8,128)S(1)}, u32[]{:S(2)}, u32[]{:S(2)}) collective-permute-start(f32[2,16,4096]{2,1,0:T(8,128)S(1)} %get-tuple-element.48), channel_id=1, source_target_pairs={{4,0},{8,4},{12,8},{16,12},{20,16},{24,20},{28,24},{5,1},{9,5},{13... | collective-permute-start | bytes 1572872 | tf_op jit(solution)/shard_map/ppermute | solution.py:568
  11.9 26.0 %collective-permute-start.2 = (bf16[64,4224]{1,0:T(8,128)(2,1)S(1)}, bf16[64,4224]{1,0:T(8,128)(2,1)S(1)}, u32[]{:S(2)}, u32[]{:S(2)}) collective-permute-start(bf16[64,4224]{1,0:T(8,128)(2,1)S(1)} %get-tuple-element.52), channel_id=1, source_target_pairs={{0,1},{1,0},{2,3},{3,2},{4,5},{5,4},{6,7},{7,6},{8,9},{9,8},{10,11... | collective-permute-start | bytes 1622024 | tf_op jit(solution)/shard_map/ppermute | solution.py:562
  12.1 37.6 %collective-permute-start.3 = (bf16[64,4224]{1,0:T(8,128)(2,1)S(1)}, bf16[64,4224]{1,0:T(8,128)(2,1)S(1)}, u32[]{:S(2)}, u32[]{:S(2)}) collective-permute-start(bf16[64,4224]{1,0:T(8,128)(2,1)S(1)} %get-tuple-element.53), channel_id=1, source_target_pairs={{0,2},{1,3},{2,0},{3,1},{4,6},{5,7},{6,4},{7,5},{8,10},{9,11},{10,... | collective-permute-start | bytes 1622024 | tf_op jit(solution)/shard_map/ppermute | solution.py:562
  14.4 46.9 %collective-permute-start.4 = (bf16[64,4224]{1,0:T(8,128)(2,1)S(1)}, bf16[64,4224]{1,0:T(8,128)(2,1)S(1)}, u32[]{:S(2)}, u32[]{:S(2)}) collective-permute-start(bf16[64,4224]{1,0:T(8,128)(2,1)S(1)} %get-tuple-element.54), channel_id=1, source_target_pairs={{0,3},{1,2},{2,1},{3,0},{4,7},{5,6},{6,5},{7,4},{8,11},{9,10},{10,... | collective-permute-start | bytes 1622024 | tf_op jit(solution)/shard_map/ppermute | solution.py:562
  23.4 3.4 %copy-start.2 = (f32[2,256,4096]{2,1,0:T(8,128)S(1)}, f32[2,256,4096]{2,1,0:T(8,128)}, u32[]{:S(2)}) copy-start(f32[2,256,4096]{2,1,0:T(8,128)} %refs_0_.8) | copy-start | bytes 25165828
  26.8 7.7 %copy-start.1 = (bf16[2,64,16384]{2,1,0:T(8,128)(2,1)S(1)}, bf16[2,64,16384]{2,1,0:T(8,128)(2,1)}, u32[]{:S(2)}) copy-start(bf16[2,64,16384]{2,1,0:T(8,128)(2,1)} %refs_14_) | copy-start | bytes 12582916
  29.1 32.8 %collective-permute-start.6 = (f32[96,128]{1,0:T(8,128)S(1)}, f32[96,128]{1,0:T(8,128)S(1)}, u32[]{:S(2)}, u32[]{:S(2)}) collective-permute-start(f32[96,128]{1,0:T(8,128)S(1)} %get-tuple-element.55), channel_id=1, source_target_pairs={{1,0},{2,1},{3,2},{5,4},{6,5},{7,6},{9,8},{10,9},{11,10},{13,12},{... | collective-permute-start | bytes 147464 | tf_op jit(solution)/shard_map/ppermute | solution.py:568
  31.4 30.5 %collective-permute-start.5 = (f32[96,128]{1,0:T(8,128)S(1)}, f32[96,128]{1,0:T(8,128)S(1)}, u32[]{:S(2)}, u32[]{:S(2)}) collective-permute-start(f32[96,128]{1,0:T(8,128)S(1)} %get-tuple-element.49), channel_id=1, source_target_pairs={{0,1},{1,2},{2,3},{4,5},{5,6},{6,7},{8,9},{9,10},{10,11},{12,13},{... | collective-permute-start | bytes 147464 | tf_op jit(solution)/shard_map/ppermute | solution.py:568
  36.2 0.8 copy-start.3
  37.0 0.8 copy-start.13
  37.8 26.9 %copy-start.7 = (bf16[64,4224]{1,0:T(8,128)(2,1)}, bf16[64,4224]{1,0:T(8,128)(2,1)S(1)}, u32[]{:S(2)}) copy-start(bf16[64,4224]{1,0:T(8,128)(2,1)S(1)} %collective-permute-done.2.refs_1_.refs_5_) | copy-start | bytes 1622020
  49.7 15.1 %copy-start.9 = (bf16[64,4224]{1,0:T(8,128)(2,1)}, bf16[64,4224]{1,0:T(8,128)(2,1)S(1)}, u32[]{:S(2)}) copy-start(bf16[64,4224]{1,0:T(8,128)(2,1)S(1)} %collective-permute-done.3.refs_2_.refs_6_) | copy-start | bytes 1622020
  61.3 0.8 copy-start.11
  62.1 50.7 %collective-permute-start.9 = (bf16[64,4224]{1,0:T(8,128)(2,1)}, bf16[64,4224]{1,0:T(8,128)(2,1)S(1)}, u32[]{:S(2)}, u32[]{:S(2)}) collective-permute-start(bf16[64,4224]{1,0:T(8,128)(2,1)} %get-tuple-element.73), channel_id=1, source_target_pairs={{0,1},{1,0},{2,3},{3,2},{4,5},{5,4},{6,7},{7,6},{8,9},{9,8},{10,11... | collective-permute-start | bytes 1622024 | tf_op jit(solution)/shard_map/ppermute | solution.py:562
  62.1 50.7 %collective-permute-start.10 = (bf16[64,4224]{1,0:T(8,128)(2,1)}, bf16[64,4224]{1,0:T(8,128)(2,1)}, u32[]{:S(2)}, u32[]{:S(2)}) collective-permute-start(bf16[64,4224]{1,0:T(8,128)(2,1)} %get-tuple-element.74), channel_id=1, source_target_pairs={{0,2},{1,3},{2,0},{3,1},{4,6},{5,7},{6,4},{7,5},{8,10},{9,11},{10,... | collective-permute-start | bytes 1622024 | tf_op jit(solution)/shard_map/ppermute | solution.py:562
  64.6 48.2 %collective-permute-start.11 = (bf16[64,4224]{1,0:T(8,128)(2,1)}, bf16[64,4224]{1,0:T(8,128)(2,1)}, u32[]{:S(2)}, u32[]{:S(2)}) collective-permute-start(bf16[64,4224]{1,0:T(8,128)(2,1)} %get-tuple-element.75), channel_id=1, source_target_pairs={{0,3},{1,2},{2,1},{3,0},{4,7},{5,6},{6,5},{7,4},{8,11},{9,10},{10,... | collective-permute-start | bytes 1622024 | tf_op jit(solution)/shard_map/ppermute | solution.py:562
  67.0 7.7 %collective-permute-start.7 = (bf16[8,4224]{1,0:T(8,128)(2,1)}, bf16[8,4224]{1,0:T(8,128)(2,1)S(1)}, u32[]{:S(2)}, u32[]{:S(2)}) collective-permute-start(bf16[8,4224]{1,0:T(8,128)(2,1)} %get-tuple-element.64), channel_id=1, source_target_pairs={{0,4},{4,8},{8,12},{12,16},{16,20},{20,24},{24,28},{1,5},{5,9},{9,... | collective-permute-start | bytes 202760 | tf_op jit(solution)/shard_map/ppermute | solution.py:568
  72.7 53.0 %copy-start.17 = (s32[5]{0:T(128)S(1)}, s32[5]{0:T(128)}, u32[]{:S(2)}) copy-start(s32[5]{0:T(128)} %copy-done.15) | copy-start | bytes 64
  72.7 53.0 %copy-start.4 = (bf16[64,4224]{1,0:T(8,128)(2,1)S(1)}, bf16[64,4224]{1,0:T(8,128)(2,1)}, u32[]{:S(2)}) copy-start(bf16[64,4224]{1,0:T(8,128)(2,1)} %copy-done.3) | copy-start | bytes 1622020
  72.7 6.3 %collective-permute-start.8 = (bf16[8,4224]{1,0:T(8,128)(2,1)}, bf16[8,4224]{1,0:T(8,128)(2,1)S(1)}, u32[]{:S(2)}, u32[]{:S(2)}) collective-permute-start(bf16[8,4224]{1,0:T(8,128)(2,1)} %get-tuple-element.65), channel_id=1, source_target_pairs={{4,0},{8,4},{12,8},{16,12},{20,16},{24,20},{28,24},{5,1},{9,5},{13... | collective-permute-start | bytes 202760 | tf_op jit(solution)/shard_map/ppermute | solution.py:568
  79.0 1.0 copy-start.8
  80.1 1.0 copy-start.10
  81.1 1.0 copy-start.12
  82.2 1.0 copy-start.14
  83.2 0.7 copy-start.16
  111.2 0.8 copy-start.18
  112.0 0.8 copy-start.19
  112.8 1.7 copy-start.5
  112.8 43.5 %collective-permute-start.17 = (s16[64,4096]{1,0:T(8,128)(2,1)}, s16[64,4096]{1,0:T(8,128)(2,1)}, u32[]{:S(2)}, u32[]{:S(2)}) collective-permute-start(s16[64,4096]{1,0:T(8,128)(2,1)} %get-tuple-element.88), channel_id=1, source_target_pairs={{0,2},{1,3},{2,0},{3,1},{4,6},{5,7},{6,4},{7,5},{8,10},{9,11},{10,... | collective-permute-start | bytes 1572872 | tf_op jit(solution)/shard_map/ppermute | solution.py:562
  116.8 7.2 %collective-permute-start.12 = (bf16[8,4224]{1,0:T(8,128)(2,1)}, bf16[8,4224]{1,0:T(8,128)(2,1)S(1)}, u32[]{:S(2)}, u32[]{:S(2)}) collective-permute-start(bf16[8,4224]{1,0:T(8,128)(2,1)} %get-tuple-element.80), channel_id=1, source_target_pairs={{0,4},{4,8},{8,12},{12,16},{16,20},{20,24},{24,28},{1,5},{5,9},{9,... | collective-permute-start | bytes 202760 | tf_op jit(solution)/shard_map/ppermute | solution.py:568
  118.7 7.0 %collective-permute-start.13 = (bf16[8,4224]{1,0:T(8,128)(2,1)}, bf16[8,4224]{1,0:T(8,128)(2,1)S(1)}, u32[]{:S(2)}, u32[]{:S(2)}) collective-permute-start(bf16[8,4224]{1,0:T(8,128)(2,1)} %get-tuple-element.81), channel_id=1, source_target_pairs={{4,0},{8,4},{12,8},{16,12},{20,16},{24,20},{28,24},{5,1},{9,5},{13... | collective-permute-start | bytes 202760 | tf_op jit(solution)/shard_map/ppermute | solution.py:568
  121.1 40.2 %collective-permute-start.18 = (s16[64,4096]{1,0:T(8,128)(2,1)}, s16[64,4096]{1,0:T(8,128)(2,1)S(1)}, u32[]{:S(2)}, u32[]{:S(2)}) collective-permute-start(s16[64,4096]{1,0:T(8,128)(2,1)} %copy-done.19), channel_id=1, source_target_pairs={{0,3},{1,2},{2,1},{3,0},{4,7},{5,6},{6,5},{7,4},{8,11},{9,10},{10,... | collective-permute-start | bytes 1572872 | tf_op jit(solution)/shard_map/ppermute | solution.py:562
  121.5 39.7 %collective-permute-start.19 = (s16[64,4096]{1,0:T(8,128)(2,1)}, s16[64,4096]{1,0:T(8,128)(2,1)S(1)}, u32[]{:S(2)}, u32[]{:S(2)}) collective-permute-start(s16[64,4096]{1,0:T(8,128)(2,1)} %copy-done.18), channel_id=1, source_target_pairs={{0,1},{1,0},{2,3},{3,2},{4,5},{5,4},{6,7},{7,6},{8,9},{9,8},{10,11... | collective-permute-start | bytes 1572872 | tf_op jit(solution)/shard_map/ppermute | solution.py:562
  125.6 1.0 copy-start.6
  154.7 20.5 %collective-permute-start.16 = (s16[64,4096]{1,0:T(8,128)(2,1)S(1)}, s16[64,4096]{1,0:T(8,128)(2,1)S(1)}, u32[]{:S(2)}, u32[]{:S(2)}) collective-permute-start(s16[64,4096]{1,0:T(8,128)(2,1)S(1)} %get-tuple-element.86), channel_id=1, source_target_pairs={{0,1},{1,0},{2,3},{3,2},{4,5},{5,4},{6,7},{7,6},{8,9},{9,8},{10,11... | collective-permute-start | bytes 1572872 | tf_op jit(solution)/shard_map/ppermute | solution.py:562
  156.2 37.8 %collective-permute-start.15 = (s16[64,4096]{1,0:T(8,128)(2,1)S(1)}, s16[64,4096]{1,0:T(8,128)(2,1)S(1)}, u32[]{:S(2)}, u32[]{:S(2)}) collective-permute-start(s16[64,4096]{1,0:T(8,128)(2,1)S(1)} %get-tuple-element.84), channel_id=1, source_target_pairs={{0,2},{1,3},{2,0},{3,1},{4,6},{5,7},{6,4},{7,5},{8,10},{9,11},{10,... | collective-permute-start | bytes 1572872 | tf_op jit(solution)/shard_map/ppermute | solution.py:562
  156.3 49.5 %collective-permute-start.14 = (s16[64,4096]{1,0:T(8,128)(2,1)S(1)}, s16[64,4096]{1,0:T(8,128)(2,1)S(1)}, u32[]{:S(2)}, u32[]{:S(2)}) collective-permute-start(s16[64,4096]{1,0:T(8,128)(2,1)S(1)} %get-tuple-element.83), channel_id=1, source_target_pairs={{0,3},{1,2},{2,1},{3,0},{4,7},{5,6},{6,5},{7,4},{8,11},{9,10},{10,... | collective-permute-start | bytes 1572872 | tf_op jit(solution)/shard_map/ppermute | solution.py:562
